TPU v7x, 32 devices: a whole 2x2x4 slice. The times are simulated.
32 devices in a mesh: section: 8 (over z, core), tensor: 4 (over y, x).
Axes of the slice: x: 2, y: 2, z: 4, core: 2. Of those that a mesh axis runs over, the one named last changes fastest.
Arguments:
- fwd_in: bfloat16 [8, 128, 2304], P('section', None, 'tensor'), may hold values from -6 to 6
- back_in: bfloat16 [8, 128, 2304], P('section', None, 'tensor'), may hold values from -0.59765625 to 0.59765625
- stash: bfloat16 [2, 8, 128, 2304], P(None, 'section', None, 'tensor'), may hold values from -6 to 6
- w_qkv: bfloat16 [8, 2304, 3, 4, 128], P('section', None, None, 'tensor'), may hold values from -0.125 to 0.125
- w_out: bfloat16 [8, 4, 128, 2304], P('section', 'tensor'), may hold values from -0.25 to 0.25
- norm_gain: bfloat16 [8, 2304], P('section'), may hold values from 0.25 to 1.75
- final_gain: bfloat16 [2304], replicated, may hold values from 0.25 to 1.75
- table: bfloat16 [8192, 2304], P(('section', 'tensor')), may hold values from -0.5625 to 0.5625
- ids: int32 [2, 128], replicated, may hold values from 0 to 8191
- back_ids: int32 [2, 128], replicated, may hold values from 0 to 8191
- targets: int32 [2, 128], replicated, may hold values from 0 to 8191
Outputs:
- fwd_out: bfloat16 [8, 128, 2304], P('section', None, 'tensor')
- back_out: bfloat16 [8, 128, 2304], P('section', None, 'tensor')
- table_grad: bfloat16 [8192, 2304], P(('section', 'tensor'))
- losses: float32 [2], replicated
All inputs are finite; a program needn't handle non-finite values.
Results may differ from a plain program's by a relative error of at most 0.035.
Values may be sent and summed in bfloat16 or wider, within the bound.
No kernel may reach another device: no remote copies, remote signals or barrier semaphores. Data moves between devices by JAX's collectives and lax.ppermute only.
A program may use at most 64 MiB of HBM per device.

v0:
```python
import math

import jax
import jax.numpy as jnp
from jax import lax
from jax.sharding import PartitionSpec as P

EPS = 1e-06
ATTN_CAP = 50.0
LOGIT_CAP = 30.0


def for_sending(x):

    def short(part):
        return part.astype(jnp.bfloat16) if part.dtype == jnp.float32 else part

    return jax.tree.map(short, x)


def passed_along(block, axis, distance):
    devices = range(lax.axis_size(axis))
    route = [(i - distance, i) for i in devices if i - distance in devices]
    return lax.ppermute(block, axis, route)


def broadcast(block, axis, holder):
    block = jnp.where(lax.axis_index(axis) == holder, block, jnp.zeros_like(block))
    return lax.psum(block, axis)


def widen(values):
    return jax.tree.map(
        lambda part, own: part.astype(own.dtype),
        lax.all_gather(for_sending(values), "tensor", axis=1, tiled=True),
        values,
    )


def sum_width(term):
    return lax.psum_scatter(
        term.astype(jnp.bfloat16), "tensor", scatter_dimension=1, tiled=True
    ).astype(jnp.float32)


def stat_width(values):
    return lax.psum(values, "tensor")


def sum_section(values):
    return jax.tree.map(
        lambda part: part.astype(jnp.float32), lax.psum(for_sending(values), "section")
    )


def pass_section(values, offset):
    return passed_along(values, "section", offset)


def feed(values, root):
    return broadcast(widen(values), "section", root)


def reduce_lookup(parts, width_pos, piece):
    summed = lax.psum(parts, ("section", "tensor"))
    return lax.dynamic_slice_in_dim(summed, width_pos * piece, piece, 1)


def row_scale(values):
    return lax.rsqrt(jnp.mean(values * values, axis=-1, keepdims=True) + EPS)


def attend(normed, weights):
    qkv = jnp.einsum("rd,dchk->chrk", normed, weights, preferred_element_type=jnp.float32).astype(
        jnp.bfloat16
    )
    query, keys, values = (qkv[0], qkv[1], qkv[2])
    length = normed.shape[0]
    scores = jnp.einsum(
        "hqk,hsk->hqs", query, keys, preferred_element_type=jnp.float32
    ) * query.shape[-1] ** (-0.5)
    capped = jnp.tanh(scores / ATTN_CAP)
    places = lax.iota(jnp.int32, length)
    causal = places[None, :] <= places[:, None]
    raised = jnp.where(causal[None], jnp.exp(ATTN_CAP * capped), 0.0)
    probs = (raised / jnp.sum(raised, axis=-1, keepdims=True)).astype(jnp.bfloat16)
    mixed = jnp.einsum("hqs,hsk->hqk", probs, values, preferred_element_type=jnp.float32).astype(
        jnp.bfloat16
    )
    return (query, keys, values, capped, probs, mixed)


def norm_back(xfull, xpiece, gpiece, dnorm, full_width):
    scale = row_scale(xfull)
    stat = stat_width(jnp.sum(xpiece * gpiece * dnorm, axis=1))
    return scale * gpiece * dnorm - xpiece * scale**3 * stat[:, None] / full_width


def body(
    fwd_in, back_in, stash, w_qkv, w_out, norm_gain, final_gain, table, ids, back_ids, targets
):
    section_pos = lax.axis_index("section")
    section_count = lax.axis_size("section")
    width_pos = lax.axis_index("tensor")
    width_count = lax.axis_size("tensor")
    acts = fwd_in[0]
    cots = back_in[0]
    rows, piece = acts.shape
    full_width = piece * width_count
    vocab_rows = table.shape[0]
    first_col = (section_pos * width_count + width_pos) * vocab_rows
    columns = first_col + lax.iota(jnp.int32, vocab_rows)
    emb_scale = math.sqrt(full_width)
    gain = norm_gain[0].astype(jnp.float32)
    gain_piece = lax.dynamic_slice_in_dim(gain, width_pos * piece, piece, 0)
    fgain = final_gain.astype(jnp.float32)
    fgain_piece = lax.dynamic_slice_in_dim(fgain, width_pos * piece, piece, 0)
    weights = w_qkv[0]
    outw = w_out[0]
    ticks = ids.shape[0]
    is_first = section_pos == 0
    is_last = section_pos == section_count - 1
    grad = jnp.zeros((vocab_rows, full_width), jnp.float32)
    losses = []
    previous = acts
    for tick in range(ticks):
        xfull = widen(acts).astype(jnp.float32)
        normed = (xfull * row_scale(xfull) * gain).astype(jnp.bfloat16)
        mixed = attend(normed, weights)[5]
        part = jnp.einsum("hrk,hkd->rd", mixed, outw, preferred_element_type=jnp.float32)
        outs_fwd = (acts.astype(jnp.float32) + sum_width(part)).astype(jnp.bfloat16)
        hidden = feed(outs_fwd, section_count - 1).astype(jnp.float32)
        hscale = row_scale(hidden)
        hnormed = (hidden * hscale * fgain).astype(jnp.bfloat16)
        raw = lax.dot_general(
            hnormed, table, (((1,), (1,)), ((), ())), preferred_element_type=jnp.float32
        )
        capped = jnp.tanh(raw / LOGIT_CAP)
        logits = LOGIT_CAP * capped
        raised = jnp.exp(logits)
        hit = targets[tick][:, None] == columns[None, :]
        tile_sums = stat_width(
            (jnp.sum(raised, axis=1), jnp.sum(jnp.where(hit, logits, 0.0), axis=1))
        )
        total, picked = sum_section(tile_sums)
        losses.append(jnp.mean(jnp.log(total) - picked))
        dlog = (
            (raised / total[:, None] - hit.astype(jnp.float32)) * (1.0 - capped * capped)
        ).astype(jnp.bfloat16)
        dpart = jnp.dot(dlog, table, preferred_element_type=jnp.float32)
        dhid = sum_section(sum_width(dpart))
        grad = grad + lax.dot_general(
            dlog, hnormed, (((0,), (0,)), ((), ())), preferred_element_type=jnp.float32
        )
        hpiece = lax.dynamic_slice_in_dim(hidden, width_pos * piece, piece, 1)
        cot_last = norm_back(hidden, hpiece, fgain_piece, dhid, full_width).astype(jnp.bfloat16)
        inputs_back = stash[tick, 0]
        if tick > 0:
            inputs_back = jnp.where(is_last, previous, inputs_back)
        bfull, upper = widen((inputs_back, cots))
        bfloat = bfull.astype(jnp.float32)
        bnormed = (bfloat * row_scale(bfloat) * gain).astype(jnp.bfloat16)
        query, keys, values, acapped, probs, amixed = attend(bnormed, weights)
        dmix = jnp.einsum("rd,hkd->hrk", upper, outw, preferred_element_type=jnp.float32).astype(
            jnp.bfloat16
        )
        dprob = jnp.einsum("hrk,hsk->hrs", dmix, values, preferred_element_type=jnp.float32)
        pfull = probs.astype(jnp.float32)
        dscore = pfull * (dprob - jnp.sum(dprob * pfull, axis=-1, keepdims=True))
        dlogit = (dscore * (1.0 - acapped * acapped) * query.shape[-1] ** (-0.5)).astype(
            jnp.bfloat16
        )
        dquery = jnp.einsum(
            "hqs,hsk->hqk", dlogit, keys, preferred_element_type=jnp.float32
        ).astype(jnp.bfloat16)
        dkeys = jnp.einsum(
            "hqs,hqk->hsk", dlogit, query, preferred_element_type=jnp.float32
        ).astype(jnp.bfloat16)
        dvalues = jnp.einsum(
            "hqs,hqk->hsk", probs, dmix, preferred_element_type=jnp.float32
        ).astype(jnp.bfloat16)
        stacked = jnp.stack([dquery, dkeys, dvalues])
        dterm = jnp.einsum("chrk,dchk->rd", stacked, weights, preferred_element_type=jnp.float32)
        dnorm = sum_width(dterm)
        bpiece = lax.dynamic_slice_in_dim(bfloat, width_pos * piece, piece, 1)
        dxf = norm_back(bfloat, bpiece, gain_piece, dnorm, full_width)
        outs_back = (cots.astype(jnp.float32) + dxf).astype(jnp.bfloat16)
        leaving = feed(outs_back, 0)
        back_hits = (back_ids[tick][:, None] == columns[None, :]).astype(jnp.bfloat16)
        look_grad = lax.dot_general(
            back_hits, leaving, (((0,), (0,)), ((), ())), preferred_element_type=jnp.float32
        )
        grad = grad + look_grad * emb_scale
        hits = (ids[tick][:, None] == columns[None, :]).astype(jnp.bfloat16)
        embedded = reduce_lookup(
            jnp.dot(hits, table, preferred_element_type=jnp.float32), width_pos, piece
        )
        entering = (embedded * emb_scale).astype(jnp.bfloat16)
        previous = acts
        acts = jnp.where(is_first, entering, pass_section(outs_fwd, 1))
        cots = jnp.where(is_last, cot_last, pass_section(outs_back, -1))
    return (acts[None], cots[None], grad.astype(jnp.bfloat16), jnp.stack(losses))


def solution(mesh):
    return jax.shard_map(
        body,
        mesh=mesh,
        in_specs=(
            P("section", None, "tensor"),
            P("section", None, "tensor"),
            P(None, "section", None, "tensor"),
            P("section", None, None, "tensor", None),
            P("section", "tensor", None, None),
            P("section", None),
            P(),
            P(("section", "tensor"), None),
            P(),
            P(),
            P(),
        ),
        out_specs=(
            P("section", None, "tensor"),
            P("section", None, "tensor"),
            P(("section", "tensor"), None),
            P(),
        ),
        check_vma=False,
    )
```

profile of v0, /device:TPU:29, one launch (start us, length us, event | category | flops | bytes accessed | tf_op | source)
XLA Modules:
  0.0 574.3 jit_solution(3762362679505095675)
XLA Ops:
  8.1 8.4 %all-gather = bf16[1,128,2304]{1,2,0:T(8,128)(2,1)S(1)} all-gather(bf16[1,128,576]{1,2,0:T(8,128)(2,1)} %param.11), channel_id=2, replica_groups=mesh['section'=8,'tensor'=4] {'tensor'}, dimensions={2}, use_global_device_ids=true | all-gather | bytes 737280 | tf_op jit(solution)/shard_map/all_gather | solution.py:35
  17.5 1.1 fusion.48
  20.1 2.2 convolution_convert_fusion.3
  23.1 1.7 fusion.124
  24.8 1.7 fusion.126
  26.5 23.4 %reduce-scatter.7.cloned.1.call-done = bf16[128,576]{0,1:T(8,128)(2,1)} async-done(((bf16[128,2304]{0,1:T(8,128)(2,1)}), bf16[128,576]{0,1:T(8,128)(2,1)}) %reduce-scatter.7.cloned.1.call-update) | async-done | bytes 147472 | tf_op jit(solution)/shard_map/reduce_scatter | solution.py:41
  49.9 1.7 add_convert_fusion.1
  51.6 1.3 collective-permute-start
  52.9 111.9 %all-reduce.14.cloned.1.call-done = (f32[128,2304]{0,1:T(8,128)}, f32[128,2304]{0,1:T(8,128)}) async-done(((f32[128,2304]{0,1:T(8,128)}, f32[128,2304]{0,1:T(8,128)}), (f32[128,2304]{0,1:T(8,128)}, f32[128,2304]{0,1:T(8,128)})) %all-reduce.14.cloned.1.call-update) | async-done | bytes 2359312 | tf_op jit(solution)/shard_map/psum | solution.py:65
  166.5 9.0 %all_gather.31 = bf16[128,2304]{0,1:T(8,128)(2,1)S(1)} all-gather(bf16[128,576]{0,1:T(8,128)(2,1)S(1)} %fusion.112), channel_id=1, replica_groups=mesh['section'=8,'tensor'=4] {'tensor'}, dimensions={1}, use_global_device_ids=true | all-gather | bytes 737280 | tf_op jit(solution)/shard_map/all_gather | solution.py:35
  175.8 1.1 fusion.45
  177.6 1.3 fusion.167
  178.9 2.2 convolution_convert_fusion.2
  181.2 7.9 %all_gather.33 = bf16[128,2304]{0,1:T(8,128)(2,1)S(1)} all-gather(bf16[128,576]{0,1:T(8,128)(2,1)} %add_convert_fusion.1), channel_id=1, replica_groups=mesh['section'=8,'tensor'=4] {'tensor'}, dimensions={1}, use_global_device_ids=true | all-gather | bytes 737280 | tf_op jit(solution)/shard_map/all_gather | solution.py:35
  190.0 20.6 %reduce-scatter.9.cloned.1.call-done = bf16[128,576]{0,1:T(8,128)(2,1)} async-done(((bf16[128,2304]{0,1:T(8,128)(2,1)}), bf16[128,576]{0,1:T(8,128)(2,1)}) %reduce-scatter.9.cloned.1.call-update) | async-done | bytes 147472 | tf_op jit(solution)/shard_map/reduce_scatter | solution.py:41
  212.3 7.4 %all_gather.32 = bf16[128,2304]{0,1:T(8,128)(2,1)S(1)} all-gather(bf16[128,576]{0,1:T(8,128)(2,1)S(1)} %add_convert_fusion), channel_id=1, replica_groups=mesh['section'=8,'tensor'=4] {'tensor'}, dimensions={1}, use_global_device_ids=true | all-gather | bytes 737280 | tf_op jit(solution)/shard_map/all_gather | solution.py:35
  220.6 1.6 slice.70
  222.2 1.3 convert_element_type.317
  223.5 10.1 %all-gather.2 = bf16[1,128,2304]{1,2,0:T(8,128)(2,1)} all-gather(bf16[1,128,576]{1,2,0:T(8,128)(2,1)} %param.12), channel_id=4, replica_groups=mesh['section'=8,'tensor'=4] {'tensor'}, dimensions={2}, use_global_device_ids=true | all-gather | bytes 737280 | tf_op jit(solution)/shard_map/all_gather | solution.py:35
  233.6 1.3 slice_bitcast_fusion.33
  234.8 45.5 %all-reduce.20.cloned.1.call-done = (bf16[128,2304]{0,1:T(8,128)(2,1)}, bf16[128,2304]{0,1:T(8,128)(2,1)}) async-done(((bf16[128,2304]{0,1:T(8,128)(2,1)}, bf16[128,2304]{0,1:T(8,128)(2,1)}), (bf16[128,2304]{0,1:T(8,128)(2,1)}, bf16[128,2304]{0,1:T(8,128)(2,1)})) %all-reduce.20.cloned.1.call-update) | async-done | bytes 1179664 | tf_op jit(solution)/shard_map/psum | solution.py:29
  280.3 1.6 multiply_reduce_fusion.1
  284.2 2.3 fusion.123
  286.5 7.8 %all-reduce.3 = (bf16[128]{0:T(256)(128)(2,1)}, bf16[128]{0:T(256)(128)(2,1)}) all-reduce(f32[128]{0:T(128)} %get-tuple-element.5, f32[128]{0:T(128)} %get-tuple-element.10), channel_id=1, replica_groups=mesh['section'=8,'tensor'=4] {'tensor'}, use_global_device_ids=true, to_apply=%region_20.21 | all-reduce | flops 256 | bytes 1536 | tf_op jit(solution)/shard_map/psum | solution.py:47
  294.3 15.9 %all-reduce.5 = (bf16[128]{0:T(256)(128)(2,1)}, bf16[128]{0:T(256)(128)(2,1)}) all-reduce(bf16[128]{0:T(256)(128)(2,1)} %get-tuple-element.21, bf16[128]{0:T(256)(128)(2,1)} %get-tuple-element.20), channel_id=1, replica_groups=mesh['section'=8,'tensor'=4] {'section'}, use_global_device_ids=true, to_apply=%region_12.13 | all-reduce | flops 256 | bytes 1024 | tf_op jit(solution)/shard_map/psum | solution.py:52
  311.4 2.4 convolution_convert_fusion.1
  313.9 11.9 %all-gather.1 = bf16[1,1,128,2304]{2,3,1,0:T(8,128)(2,1)S(1)} all-gather(bf16[1,1,128,576]{2,3,1,0:T(8,128)(2,1)} %slice.70), channel_id=3, replica_groups=mesh['section'=8,'tensor'=4] {'tensor'}, dimensions={3}, use_global_device_ids=true | all-gather | bytes 737280 | tf_op jit(solution)/shard_map/all_gather | solution.py:35
  327.1 1.7 fusion.42
  330.3 1.5 convolution_convert_fusion
  334.3 1.4 fusion.4
  335.9 8.4 %all_gather.36 = bf16[128,2304]{0,1:T(8,128)(2,1)S(1)} all-gather(bf16[128,576]{0,1:T(8,128)(2,1)S(1)} %bitcast_select_fusion), channel_id=1, replica_groups=mesh['section'=8,'tensor'=4] {'tensor'}, dimensions={1}, use_global_device_ids=true | all-gather | bytes 737280 | tf_op jit(solution)/shard_map/all_gather | solution.py:35
  345.8 1.7 fusion.39
  347.5 20.7 %reduce-scatter.13.cloned.1.call-done = bf16[128,576]{0,1:T(8,128)(2,1)} async-done(((bf16[128,2304]{0,1:T(8,128)(2,1)}), bf16[128,576]{0,1:T(8,128)(2,1)}) %reduce-scatter.13.cloned.1.call-update) | async-done | bytes 147472 | tf_op jit(solution)/shard_map/reduce_scatter | solution.py:41
  368.3 2.0 fusion.153
  372.3 1.1 convert_element_type.356
  373.5 22.8 %reduce-scatter.15.cloned.1.call-done = bf16[128,576]{0,1:T(8,128)(2,1)} async-done(((bf16[128,2304]{0,1:T(8,128)(2,1)}), bf16[128,576]{0,1:T(8,128)(2,1)}) %reduce-scatter.15.cloned.1.call-update) | async-done | bytes 147472 | tf_op jit(solution)/shard_map/reduce_scatter | solution.py:41
  396.3 1.7 fusion.101
  398.0 1.1 convert_element_type.316
  399.1 1.1 convert_element_type.326
  400.2 20.8 %all-reduce.18.cloned.1.call-done = (bf16[128,576]{0,1:T(8,128)(2,1)}, bf16[128,576]{0,1:T(8,128)(2,1)}) async-done(((bf16[128,576]{0,1:T(8,128)(2,1)}, bf16[128,576]{0,1:T(8,128)(2,1)}), (bf16[128,576]{0,1:T(8,128)(2,1)}, bf16[128,576]{0,1:T(8,128)(2,1)})) %all-reduce.18.cloned.1.call-update) | async-done | bytes 294928 | tf_op jit(solution)/shard_map/psum | solution.py:52
  421.1 1.9 fusion.94
  423.0 7.6 %all-reduce.2 = (f32[128]{0:T(128)}, f32[128]{0:T(128)}) all-reduce(f32[128]{0:T(128)} %fusion.101, f32[128]{0:T(128)} %get-tuple-element.9), channel_id=1, replica_groups=mesh['section'=8,'tensor'=4] {'tensor'}, use_global_device_ids=true, to_apply=%region_31.32 | all-reduce | flops 256 | bytes 2048 | tf_op jit(solution)/shard_map/psum | solution.py:47
  430.6 1.2 fusion.100
  431.8 5.4 collective-permute-start.2
  437.3 1.3 slice_bitcast_fusion.30
  438.6 1.3 collective-permute-start.1
  439.9 1.2 fusion.113
  441.2 8.4 %all_gather.37 = bf16[128,2304]{0,1:T(8,128)(2,1)S(1)} all-gather(bf16[128,576]{0,1:T(8,128)(2,1)S(1)} %fusion.113), channel_id=1, replica_groups=mesh['section'=8,'tensor'=4] {'tensor'}, dimensions={1}, use_global_device_ids=true | all-gather | bytes 737280 | tf_op jit(solution)/shard_map/all_gather | solution.py:35
  450.7 1.4 fusion.5
  452.3 1.8 fusion.111
  454.1 2.3 fusion.108
  456.4 10.5 %all_gather.38 = bf16[128,2304]{0,1:T(8,128)(2,1)S(1)} all-gather(bf16[128,576]{0,1:T(8,128)(2,1)S(1)} %copy-done.18), channel_id=1, replica_groups=mesh['section'=8,'tensor'=4] {'tensor'}, dimensions={1}, use_global_device_ids=true | all-gather | bytes 737280 | tf_op jit(solution)/shard_map/all_gather | solution.py:35
  467.8 13.6 %reduce-scatter.17.cloned.1.call-done = bf16[128,576]{0,1:T(8,128)(2,1)} async-done(((bf16[128,2304]{0,1:T(8,128)(2,1)}), bf16[128,576]{0,1:T(8,128)(2,1)}) %reduce-scatter.17.cloned.1.call-update) | async-done | bytes 147472 | tf_op jit(solution)/shard_map/reduce_scatter | solution.py:41
  481.4 1.2 fusion.105
  482.7 7.2 %all-reduce.1 = (f32[128]{0:T(128)S(1)}, f32[128]{0:T(128)S(1)}, bf16[128]{0:T(256)(128)(2,1)S(1)}, bf16[128]{0:T(256)(128)(2,1)S(1)}) all-reduce(f32[128]{0:T(128)S(1)} %fusion.105, f32[128]{0:T(128)S(1)} %copy-done.55, f32[128]{0:T(128)S(1)} %copy-done.63, f32[128]{0:T(128)S(1)} %copy-done.62), channel_id=1, replica_groups=mesh['section'=8,'tensor'=4] {'tensor'}, use_global_device_ids=true, to_apply=%region_37.38 | all-reduce | flops 512 | bytes 3584 | tf_op jit(solution)/shard_map/psum | solution.py:47
  489.9 1.2 fusion.104
  491.1 8.0 %all_gather.39 = bf16[128,2304]{0,1:T(8,128)(2,1)S(1)} all-gather(bf16[128,576]{0,1:T(8,128)(2,1)S(1)} %fusion.104), channel_id=1, replica_groups=mesh['section'=8,'tensor'=4] {'tensor'}, dimensions={1}, use_global_device_ids=true | all-gather | bytes 737280 | tf_op jit(solution)/shard_map/all_gather | solution.py:35
  500.2 2.3 fusion.109
  502.5 6.8 %collective-permute-start.3 = (bf16[128,576]{0,1:T(8,128)(2,1)S(1)}, bf16[128,576]{0,1:T(8,128)(2,1)S(1)}, u32[]{:S(2)}, u32[]{:S(2)}) collective-permute-start(bf16[128,576]{0,1:T(8,128)(2,1)S(1)} %fusion.104), channel_id=1, source_target_pairs={{4,0},{8,4},{12,8},{16,12},{20,16},{24,20},{28,24},{5,1},{9,5},{13... | collective-permute-start | bytes 442376 | tf_op jit(solution)/shard_map/ppermute | solution.py:24
  509.3 13.3 %all-reduce.4 = (bf16[128]{0:T(256)(128)(2,1)S(1)}, bf16[128]{0:T(256)(128)(2,1)S(1)}) all-reduce(bf16[128]{0:T(256)(128)(2,1)S(1)} %get-tuple-element.16, bf16[128]{0:T(256)(128)(2,1)S(1)} %get-tuple-element.17), channel_id=1, replica_groups=mesh['section'=8,'tensor'=4] {'section'}, use_global_device_ids=true, to_apply=%region_46.47 | all-reduce | flops 256 | bytes 1024 | tf_op jit(solution)/shard_map/psum | solution.py:52
  525.6 1.8 fusion.115
  527.4 34.5 %all-reduce.16.cloned.1.call-done = (bf16[128,2304]{0,1:T(8,128)(2,1)}, bf16[128,2304]{0,1:T(8,128)(2,1)}) async-done(((bf16[128,2304]{0,1:T(8,128)(2,1)}, bf16[128,2304]{0,1:T(8,128)(2,1)}), (bf16[128,2304]{0,1:T(8,128)(2,1)}, bf16[128,2304]{0,1:T(8,128)(2,1)})) %all-reduce.16.cloned.1.call-update) | async-done | bytes 1179664 | tf_op jit(solution)/shard_map/psum | solution.py:29
  561.9 3.2 fusion.2
  565.1 1.6 fusion.3
  (205 shorter events, 26.9 us)
Async XLA Ops:
  8.0 9.5 %copy-start = (bf16[1,2304,3,1,128]{4,1,3,2,0:T(8,128)(2,1)S(1)}, bf16[1,2304,3,1,128]{4,1,3,2,0:T(8,128)(2,1)}, u32[]{:S(2)}) copy-start(bf16[1,2304,3,1,128]{4,1,3,2,0:T(8,128)(2,1)} %param.14) | copy-start | bytes 5308420
  8.0 41.9 %reduce-scatter.7.cloned.1.call-start = ((), (), s32[]{:S(2)}) async-start(), calls=%async_computation.6 | async-start | bytes 737280 | tf_op jit(solution)/shard_map/reduce_scatter | solution.py:41
  17.5 2.6 copy-start.2
  19.3 3.9 copy-start.1
  22.3 142.5 %all-reduce.14.cloned.1.call-start = ((), (), s32[]{:S(2)}) async-start(), calls=%async_computation.12 | async-start | bytes 4718592 | tf_op jit(solution)/shard_map/psum | solution.py:65
  22.4 307.4 %copy-start.30 = (s32[256]{0:T(256)}, s32[256]{0:T(256)S(1)}, u32[]{:S(2)}) copy-start(s32[256]{0:T(256)S(1)} %iota_add_fusion) | copy-start | bytes 3076
  26.5 184.1 %reduce-scatter.9.cloned.1.call-start = ((), (), s32[]{:S(2)}) async-start(), calls=%async_computation.7 | async-start | bytes 737280 | tf_op jit(solution)/shard_map/reduce_scatter | solution.py:41
  51.6 113.2 %collective-permute-start = (bf16[128,576]{0,1:T(8,128)(2,1)}, bf16[128,576]{0,1:T(8,128)(2,1)}, u32[]{:S(2)}, u32[]{:S(2)}) collective-permute-start(bf16[128,576]{0,1:T(8,128)(2,1)} %add_convert_fusion.1), channel_id=1, source_target_pairs={{0,4},{4,8},{8,12},{12,16},{16,20},{20,24},{24,28},{1,5},{5,9},{9,... | collective-permute-start | bytes 442376 | tf_op jit(solution)/shard_map/ppermute | solution.py:24
  181.1 99.2 %all-reduce.20.cloned.1.call-start = ((), (), s32[]{:S(2)}) async-start(), calls=%async_computation.15 | async-start | bytes 2359296 | tf_op jit(solution)/shard_map/psum | solution.py:29
  220.6 127.0 %reduce-scatter.11.cloned.1.call-start = ((), (), s32[]{:S(2)}) async-start(), calls=%async_computation.8 | async-start | bytes 737280 | tf_op jit(solution)/shard_map/reduce_scatter | solution.py:41
  280.3 2.8 copy-start.7
  280.3 2.8 copy-start.28
  281.9 2.3 copy-start.5
  281.9 2.3 copy-start.38
  281.9 2.3 copy-start.41
  282.5 1.7 copy-start.43
  283.1 3.4 copy-start.46
  284.2 2.3 copy-start.21
  313.8 54.4 %reduce-scatter.13.cloned.1.call-start = ((), (), s32[]{:S(2)}) async-start(), calls=%async_computation.9 | async-start | bytes 737280 | tf_op jit(solution)/shard_map/reduce_scatter | solution.py:41
  325.7 3.1 copy-start.3
  327.1 1.7 copy-start.9
  331.8 2.0 copy-start.25
  331.8 2.4 copy-start.37
  331.8 64.5 %reduce-scatter.15.cloned.1.call-start = ((), (), s32[]{:S(2)}) async-start(), calls=%async_computation.10 | async-start | bytes 737280 | tf_op jit(solution)/shard_map/reduce_scatter | solution.py:41
  335.8 85.3 %all-reduce.18.cloned.1.call-start = ((), (), s32[]{:S(2)}) async-start(), calls=%async_computation.14 | async-start | bytes 589824 | tf_op jit(solution)/shard_map/psum | solution.py:52
  345.8 24.5 %copy-start.4 = (bf16[1,1,128,2304]{2,3,1,0:T(8,128)(2,1)S(1)}, bf16[1,1,128,2304]{2,3,1,0:T(8,128)(2,1)}, u32[]{:S(2)}) copy-start(bf16[1,1,128,2304]{2,3,1,0:T(8,128)(2,1)} %copy-done.3) | copy-start | bytes 1769476
  347.5 23.9 %copy-start.36 = (bf16[1,2304]{1,0:T(2,128)(2,1)S(1)}, bf16[1,2304]{1,0:T(2,128)(2,1)}, u32[]{:S(2)}) copy-start(bf16[1,2304]{1,0:T(2,128)(2,1)} %param.16) | copy-start | bytes 13828
  368.2 113.2 %reduce-scatter.17.cloned.1.call-start = ((), (), s32[]{:S(2)}) async-start(), calls=%async_computation.11 | async-start | bytes 737280 | tf_op jit(solution)/shard_map/reduce_scatter | solution.py:41
  371.4 26.6 %copy-start.8 = (bf16[128,2304]{0,1:T(8,128)(2,1)S(1)}, bf16[128,2304]{0,1:T(8,128)(2,1)}, u32[]{:S(2)}) copy-start(bf16[128,2304]{0,1:T(8,128)(2,1)} %get-tuple-element.30) | copy-start | bytes 1769476
  372.3 67.6 %copy-start.33 = (f32[576]{0:T(1024)}, f32[576]{0:T(1024)S(1)}, u32[]{:S(2)}) copy-start(f32[576]{0:T(1024)S(1)} %dynamic_slice.28) | copy-start | bytes 6916
  373.4 25.8 %copy-start.6 = (bf16[128,2304]{0,1:T(8,128)(2,1)S(1)}, bf16[128,2304]{0,1:T(8,128)(2,1)}, u32[]{:S(2)}) copy-start(bf16[128,2304]{0,1:T(8,128)(2,1)} %get-tuple-element.31) | copy-start | bytes 1769476
  399.1 31.4 %copy-start.59 = (f32[128]{0:T(128)S(1)}, f32[128]{0:T(128)}, u32[]{:S(2)}) copy-start(f32[128]{0:T(128)} %copy-done.58) | copy-start | bytes 1540
  400.2 39.7 %copy-start.47 = (f32[128]{0:T(128)S(1)}, f32[128]{0:T(128)}, u32[]{:S(2)}) copy-start(f32[128]{0:T(128)} %copy-done.46) | copy-start | bytes 1540
  431.8 8.1 %copy-start.17 = (bf16[128,576]{0,1:T(8,128)(2,1)}, bf16[128,576]{0,1:T(8,128)(2,1)S(1)}, u32[]{:S(2)}) copy-start(bf16[128,576]{0,1:T(8,128)(2,1)S(1)} %fusion.100) | copy-start | bytes 442372
  431.8 8.0 %collective-permute-start.2 = (bf16[128,576]{0,1:T(8,128)(2,1)S(1)}, bf16[128,576]{0,1:T(8,128)(2,1)S(1)}, u32[]{:S(2)}, u32[]{:S(2)}) collective-permute-start(bf16[128,576]{0,1:T(8,128)(2,1)S(1)} %fusion.100), channel_id=1, source_target_pairs={{4,0},{8,4},{12,8},{16,12},{20,16},{24,20},{28,24},{5,1},{9,5},{13... | collective-permute-start | bytes 442376 | tf_op jit(solution)/shard_map/ppermute | solution.py:24
  438.6 13.7 %collective-permute-start.1 = (bf16[128,576]{0,1:T(8,128)(2,1)}, bf16[128,576]{0,1:T(8,128)(2,1)}, u32[]{:S(2)}, u32[]{:S(2)}) collective-permute-start(bf16[128,576]{0,1:T(8,128)(2,1)} %copy-done.15), channel_id=1, source_target_pairs={{0,4},{4,8},{8,12},{12,16},{16,20},{20,24},{24,28},{1,5},{5,9},{9,... | collective-permute-start | bytes 442376 | tf_op jit(solution)/shard_map/ppermute | solution.py:24
  439.9 10.0 %copy-start.35 = (f32[128,128]{0,1:T(8,128)S(1)}, f32[128,128]{0,1:T(8,128)}, u32[]{:S(2)}) copy-start(f32[128,128]{0,1:T(8,128)} %get-tuple-element.56) | copy-start | bytes 196612
  439.9 10.0 %copy-start.61 = (f32[128]{0:T(128)S(1)}, f32[128]{0:T(128)}, u32[]{:S(2)}) copy-start(f32[128]{0:T(128)} %get-tuple-element.55) | copy-start | bytes 1540
  441.2 9.1 %copy-start.11 = (bf16[128,576]{0,1:T(8,128)(2,1)}, bf16[128,576]{0,1:T(8,128)(2,1)S(1)}, u32[]{:S(2)}) copy-start(bf16[128,576]{0,1:T(8,128)(2,1)S(1)} %fusion.113) | copy-start | bytes 442372
  441.2 8.9 %copy-start.24 = (bf16[3,1,128,128]{3,2,0,1:T(8,128)(2,1)S(1)}, bf16[3,1,128,128]{3,2,0,1:T(8,128)(2,1)}, u32[]{:S(2)}) copy-start(bf16[3,1,128,128]{3,2,0,1:T(8,128)(2,1)} %fusion.39) | copy-start | bytes 294916
  452.1 1.9 copy-start.22
  452.1 1.9 copy-start.29
  452.1 1.9 copy-start.31
  452.1 1.9 copy-start.42
  452.1 1.9 copy-start.44
  452.2 1.9 copy-start.52
  452.2 109.7 %all-reduce.16.cloned.1.call-start = ((), (), s32[]{:S(2)}) async-start(), calls=%async_computation.13 | async-start | bytes 2359296 | tf_op jit(solution)/shard_map/psum | solution.py:29
  454.0 2.3 copy-start.18
  456.4 26.3 %copy-start.55 = (f32[128]{0:T(128)S(1)}, f32[128]{0:T(128)}, u32[]{:S(2)}) copy-start(f32[128]{0:T(128)} %get-tuple-element.8) | copy-start | bytes 1540
  456.4 26.3 %copy-start.62 = (f32[128]{0:T(128)S(1)}, f32[128]{0:T(128)}, u32[]{:S(2)}) copy-start(f32[128]{0:T(128)} %get-tuple-element.4) | copy-start | bytes 1540
  456.4 26.3 %copy-start.63 = (f32[128]{0:T(128)S(1)}, f32[128]{0:T(128)}, u32[]{:S(2)}) copy-start(f32[128]{0:T(128)} %get-tuple-element.11) | copy-start | bytes 1540
  456.4 33.5 %copy-start.12 = (bf16[128,576]{0,1:T(8,128)(2,1)S(1)}, bf16[128,576]{0,1:T(8,128)(2,1)}, u32[]{:S(2)}) copy-start(bf16[128,576]{0,1:T(8,128)(2,1)} %copy-done.11) | copy-start | bytes 442372
  456.4 33.5 %copy-start.57 = (f32[128]{0:T(128)S(1)}, f32[128]{0:T(128)}, u32[]{:S(2)}) copy-start(f32[128]{0:T(128)} %copy-done.56) | copy-start | bytes 1540
  456.4 33.5 %copy-start.64 = (f32[128]{0:T(128)S(1)}, f32[128]{0:T(128)}, u32[]{:S(2)}) copy-start(f32[128]{0:T(128)} %get-tuple-element.40) | copy-start | bytes 1540
  500.1 22.5 %copy-start.67 = (bf16[128]{0:T(256)(128)(2,1)S(1)}, bf16[128]{0:T(256)(128)(2,1)}, u32[]{:S(2)}) copy-start(bf16[128]{0:T(256)(128)(2,1)} %get-tuple-element.24) | copy-start | bytes 772
  500.1 23.1 %copy-start.66 = (bf16[128]{0:T(256)(128)(2,1)S(1)}, bf16[128]{0:T(256)(128)(2,1)}, u32[]{:S(2)}) copy-start(bf16[128]{0:T(256)(128)(2,1)} %get-tuple-element.25) | copy-start | bytes 772
  500.2 25.4 %copy-start.16 = (bf16[128,576]{0,1:T(8,128)(2,1)S(1)}, bf16[128,576]{0,1:T(8,128)(2,1)}, u32[]{:S(2)}) copy-start(bf16[128,576]{0,1:T(8,128)(2,1)} %get-tuple-element.28) | copy-start | bytes 442372
  500.2 25.4 %copy-start.34 = (f32[576]{0:T(1024)S(1)}, f32[576]{0:T(1024)}, u32[]{:S(2)}) copy-start(f32[576]{0:T(1024)} %copy-done.33) | copy-start | bytes 6916
  500.2 25.4 %copy-start.45 = (f32[128]{0:T(128)S(1)}, f32[128]{0:T(128)}, u32[]{:S(2)}) copy-start(f32[128]{0:T(128)} %copy-done.43) | copy-start | bytes 1540
  500.2 25.4 %copy-start.60 = (f32[128]{0:T(128)S(1)}, f32[128]{0:T(128)}, u32[]{:S(2)}) copy-start(f32[128]{0:T(128)} %get-tuple-element.38) | copy-start | bytes 1540
  500.2 61.7 %copy-start.54 = (s32[128]{0:T(128)S(1)}, s32[128]{0:T(128)}, u32[]{:S(2)}) copy-start(s32[128]{0:T(128)} %get-tuple-element.33) | copy-start | bytes 1540
  502.5 23.1 %collective-permute-start.3 = (bf16[128,576]{0,1:T(8,128)(2,1)S(1)}, bf16[128,576]{0,1:T(8,128)(2,1)S(1)}, u32[]{:S(2)}, u32[]{:S(2)}) collective-permute-start(bf16[128,576]{0,1:T(8,128)(2,1)S(1)} %fusion.104), channel_id=1, source_target_pairs={{4,0},{8,4},{12,8},{16,12},{20,16},{24,20},{28,24},{5,1},{9,5},{13... | collective-permute-start | bytes 442376 | tf_op jit(solution)/shard_map/ppermute | solution.py:24
  561.9 3.2 copy-start.14
  561.9 3.2 copy-start.53
  (18 other events, 16.4 us)
Sparse Core Ops, SparseCore 0:
  22.4 27.4 reduce-scatter.6
  181.2 29.3 reduce-scatter.8
  313.9 26.3 reduce-scatter.10
  343.0 25.1 reduce-scatter.12
  371.2 25.0 reduce-scatter.14
  452.3 29.0 reduce-scatter.16
Sparse Core Ops, SparseCore 1:
  30.0 134.7 all-reduce.13
  220.6 59.6 all-reduce.19
  368.3 52.7 all-reduce.17
  500.2 61.6 all-reduce.15
where the time goes:
time: 580 us; the launch traced here: 574 us
  waiting for transfers between devices  314 us (54%)
  blocking collectives  142 us (24%)
  matrix products  41.2 us (7%)
  other arithmetic  33.5 us (6%)
  between operations  17.8 us (3%)
  starting transfers between devices  15.2 us (3%)
  local copies, waits for them, and re-layouts  10.9 us (2%)
    psum x1, waiting for transfers between devices, reduce_lookup(): summed = lax.psum(parts, ('section', 'tensor'))  112 us
    reduce_scatter x6, waiting for transfers between devices, sum_width(): lax.psum_scatter(term.astype(jnp.bfloat16), 'tensor', scatter_dimension=1...  101 us
    all_gather x10, blocking collectives, widen(): lax.all_gather(for_sending(values), 'tensor', axis=1, tiled=True)  90 us
    psum x2, waiting for transfers between devices, broadcast(): return lax.psum(block, axis)  79.9 us
    psum x2, blocking collectives, sum_section(): lax.psum(for_sending(values), 'section')  29.2 us
    psum x3, blocking collectives, stat_width(): return lax.psum(values, 'tensor')  22.6 us
    psum x1, waiting for transfers between devices, sum_section(): lax.psum(for_sending(values), 'section')  20.8 us
    ppermute x4, starting transfers between devices, passed_along(): return lax.ppermute(block, axis, route)  14.7 us
  transfers between devices with their start and end apart: 14, of which 9 were waited for; matrix products, arithmetic and copies ran while one was open for 8% of the time, Pallas kernels for 0%

commit v1 on v0

v1 whole, which is shorter than its diff:
```python
import math

import jax
import jax.numpy as jnp
from jax import lax
from jax.sharding import PartitionSpec as P

EPS = 1e-06
ATTN_CAP = 50.0
LOGIT_CAP = 30.0
F32 = jnp.float32
BF16 = jnp.bfloat16


def mm(a, b, ca, cb):
    return lax.dot_general(a, b, (((ca,), (cb,)), ((), ())), preferred_element_type=F32)


def row_scale(x):
    return lax.rsqrt(jnp.mean(x * x, axis=-1, keepdims=True) + EPS)


def gather(x, axis):
    return lax.all_gather(x, "tensor", axis=axis, tiled=True)


def exchange(x):
    return lax.all_to_all(x, "tensor", 0, 0, tiled=True)


def hop(x, pairs):
    return lax.ppermute(x, "section", pairs)


def from_section(x, root):
    sections = lax.axis_size("section")
    pos = lax.axis_index("section")
    core = root % 2
    got = jnp.where(pos == root, x, jnp.zeros_like(x))
    for chip in range(sections // 2):
        if chip != root // 2:
            got = got + hop(x, [(root, 2 * chip + core)])
    other = hop(got, [(2 * c + core, 2 * c + 1 - core) for c in range(sections // 2)])
    return jnp.where(pos % 2 == core, got, other)


def to_section(x, root):
    sections = lax.axis_size("section")
    core = root % 2
    pair = hop(x.astype(BF16), [(2 * c + 1 - core, 2 * c + core) for c in range(sections // 2)])
    total = x + pair.astype(F32)
    sent = total.astype(BF16)
    for chip in range(sections // 2):
        if chip != root // 2:
            total = total + hop(sent, [(2 * chip + core, root)]).astype(F32)
    return total


def sum_pieces(term, rows, width):
    t = lax.axis_size("tensor")
    parts = term.astype(BF16).reshape(rows, t, width)
    got = lax.all_to_all(parts, "tensor", 1, 1, tiled=True)
    return jnp.sum(got.astype(F32), axis=1)


def sum_all(x):
    x = jnp.sum(lax.all_gather(x, "tensor", axis=0), axis=0)
    sections = lax.axis_size("section")
    step = 1
    while step < sections:
        x = x + hop(x, [(i, i ^ step) for i in range(sections)])
        step *= 2
    return x


def attend(xfull, gain, wq):
    scale = row_scale(xfull)
    normed = (xfull * scale * gain).astype(BF16)
    width = wq.shape[1] // 3
    qkv = mm(normed, wq, 1, 0).astype(BF16)
    q, k, v = qkv[:, :width], qkv[:, width : 2 * width], qkv[:, 2 * width :]
    capped = jnp.tanh(mm(q, k, 1, 1) * width**-0.5 / ATTN_CAP)
    places = lax.iota(jnp.int32, q.shape[0])
    causal = places[None, :] <= places[:, None]
    raised = jnp.where(causal, jnp.exp(ATTN_CAP * capped), 0.0)
    probs = (raised / jnp.sum(raised, axis=-1, keepdims=True)).astype(BF16)
    return scale, qkv, capped, probs


def mixed(qkv, probs):
    width = qkv.shape[1] // 3
    return mm(probs, qkv[:, 2 * width :], 1, 0).astype(BF16)


def back_attend(saved, da, wq):
    scale, qkv, capped, probs = saved
    width = wq.shape[1] // 3
    q, k, v = qkv[:, :width], qkv[:, width : 2 * width], qkv[:, 2 * width :]
    dprob = mm(da, v, 1, 1)
    pfull = probs.astype(F32)
    dscore = pfull * (dprob - jnp.sum(dprob * pfull, axis=-1, keepdims=True))
    dlogit = (dscore * (1.0 - capped * capped) * width**-0.5).astype(BF16)
    dq = mm(dlogit, k, 1, 0).astype(BF16)
    dk = mm(dlogit, q, 0, 0).astype(BF16)
    dv = mm(probs, da, 0, 0).astype(BF16)
    dqkv = jnp.concatenate([dq, dk, dv], axis=1)
    stat = jnp.sum(dqkv.astype(F32) * qkv.astype(F32), axis=1)
    return mm(dqkv, wq, 1, 1), stat


def back_sum(term, stat, rows, width):
    t = lax.axis_size("tensor")
    high = stat.astype(BF16)
    low = (stat - high.astype(F32)).astype(BF16)
    extra = jnp.zeros((16, t, width), BF16)
    extra = extra.at[0, :, :rows].set(high[None]).at[1, :, :rows].set(low[None])
    parts = jnp.concatenate([term.astype(BF16).reshape(rows, t, width), extra], axis=0)
    got = lax.all_to_all(parts, "tensor", 1, 1, tiled=True)
    total = jnp.sum(got.astype(F32), axis=1)
    return total[:rows], total[rows, :rows] + total[rows + 1, :rows]


def body(
    fwd_in, back_in, stash, w_qkv, w_out, norm_gain, final_gain, table, ids, back_ids, targets
):
    pos = lax.axis_index("section")
    sections = lax.axis_size("section")
    tpos = lax.axis_index("tensor")
    tcount = lax.axis_size("tensor")
    acts = fwd_in[0]
    cots = back_in[0]
    rows, piece = acts.shape
    full = piece * tcount
    vocab = table.shape[0]
    first_col = (pos * tcount + tpos) * vocab
    columns = first_col + lax.iota(jnp.int32, vocab)
    emb_scale = math.sqrt(full)
    gain = norm_gain[0].astype(F32)
    gain_piece = lax.dynamic_slice_in_dim(gain, tpos * piece, piece, 0)
    fgain = final_gain.astype(F32)
    fgain_piece = lax.dynamic_slice_in_dim(fgain, tpos * piece, piece, 0)
    wq = w_qkv[0].reshape(full, -1)
    head = wq.shape[1] // 3
    outw = w_out[0].reshape(head, full)
    is_first = pos == 0
    is_last = pos == sections - 1
    ticks = ids.shape[0]

    xfull0 = gather(acts, 1)
    wo = lax.all_to_all(outw, "tensor", 1, 0, tiled=True)
    bfull = gather(stash[:, 0], 2)
    bfull1 = jnp.where(is_last, xfull0, bfull[1])

    def both(a, cot):
        part = mm(cot, wo, 1, 1).astype(BF16).reshape(rows, tcount, head)
        own = jnp.broadcast_to(a[:, None], (rows, tcount, head))
        got = lax.all_to_all(
            jnp.concatenate([own, part], axis=2), "tensor", 1, 1, tiled=True
        )
        a_all = got[:, :, :head].reshape(rows, tcount * head)
        return a_all, jnp.sum(got[:, :, head:].astype(F32), axis=1).astype(BF16)

    def only_da(cot):
        part = mm(cot, wo, 1, 1).astype(BF16).reshape(rows, tcount, head)
        got = lax.all_to_all(part, "tensor", 1, 1, tiled=True)
        return jnp.sum(got.astype(F32), axis=1).astype(BF16)

    def layer_out(x, a_all):
        return (x.astype(F32) + mm(a_all, wo, 1, 0)).astype(BF16)

    def back_out(saved, da, cot, xpiece):
        scale = saved[0]
        dnorm, stat = back_sum(*back_attend(saved, da, wq), rows, piece)
        xp = xpiece.astype(F32)
        out = (
            cot.astype(F32)
            + scale * gain_piece * dnorm
            - xp * (scale * scale * stat[:, None] / full)
        )
        return out.astype(BF16)

    saved_f0 = attend(xfull0.astype(F32), gain, wq)
    a0 = mixed(saved_f0[1], saved_f0[3])
    saved_b0 = attend(bfull[0].astype(F32), gain, wq)
    saved_b1 = attend(bfull1.astype(F32), gain, wq)

    a_all, da0 = both(a0, cots)
    y0 = layer_out(acts, a_all)
    gin0 = back_out(saved_b0, da0, cots, stash[0, 0])

    all_ids = ids.reshape(-1)
    hits = (all_ids[:, None] == columns[None, :]).astype(BF16)
    found = sum_pieces(mm(hits, table, 1, 0), ticks * rows, piece)
    entering = (to_section(found, 0) * emb_scale).astype(BF16)

    acts1 = jnp.where(
        is_first, entering[:rows], hop(y0, [(i, i + 1) for i in range(sections - 1)])
    )
    cots1 = hop(gin0, [(i + 1, i) for i in range(sections - 1)])
    xfull1 = gather(acts1, 1)
    saved_f1 = attend(xfull1.astype(F32), gain, wq)
    a1 = mixed(saved_f1[1], saved_f1[3])
    a_all1, da1 = both(a1, cots1)
    y1 = layer_out(acts1, a_all1)

    hpiece = from_section(jnp.concatenate([y0, y1], axis=0), sections - 1)
    hidden = gather(hpiece, 1).astype(F32)
    hscale = row_scale(hidden)
    hnormed = (hidden * hscale * fgain).astype(BF16)
    raw = mm(hnormed, table, 1, 1)
    capped = jnp.tanh(raw / LOGIT_CAP)
    raised = jnp.exp(LOGIT_CAP * capped)
    slope = 1.0 - capped * capped
    hit = targets.reshape(-1)[:, None] == columns[None, :]
    others = jnp.where(hit, 0.0, raised)
    sums = sum_all(
        jnp.stack(
            [
                jnp.sum(others, axis=1),
                jnp.sum(others * slope * raw, axis=1),
                jnp.sum(jnp.where(hit, raw, 0.0), axis=1),
            ]
        )
    )
    rest, weighted, raw_hit = sums[0], sums[1], sums[2]
    capped_hit = jnp.tanh(raw_hit / LOGIT_CAP)
    total = rest + jnp.exp(LOGIT_CAP * capped_hit)
    losses = jnp.mean(
        (jnp.log(total) - LOGIT_CAP * capped_hit).reshape(ticks, rows), axis=1
    )
    dlog = (jnp.where(hit, -rest[:, None], raised) / total[:, None] * slope).astype(BF16)
    hstat = (weighted - rest * (1.0 - capped_hit * capped_hit) * raw_hit) / total
    dhid = to_section(sum_pieces(mm(dlog, table, 1, 0), ticks * rows, piece), sections - 1)
    cot_last = (
        hscale * fgain_piece * dhid
        - hpiece.astype(F32) * (hscale * hscale * hstat[:, None] / full)
    ).astype(BF16)
    grad = mm(dlog, hnormed, 0, 0)

    cots1 = jnp.where(is_last, cot_last[:rows], cots1)
    da1 = jnp.where(is_last, only_da(cots1), da1)
    bpiece1 = jnp.where(is_last, acts, stash[1, 0])
    gin1 = back_out(saved_b1, da1, cots1, bpiece1)

    leaving = gather(from_section(jnp.concatenate([gin0, gin1], axis=0), 0), 1)
    back_hits = (back_ids.reshape(-1)[:, None] == columns[None, :]).astype(BF16)
    grad = grad + mm(back_hits, leaving, 0, 0) * emb_scale

    acts2 = jnp.where(
        is_first, entering[rows:], hop(y1, [(i, i + 1) for i in range(sections - 1)])
    )
    cots2 = jnp.where(
        is_last, cot_last[rows:], hop(gin1, [(i + 1, i) for i in range(sections - 1)])
    )
    return (acts2[None], cots2[None], grad.astype(BF16), losses)


def solution(mesh):
    return jax.shard_map(
        body,
        mesh=mesh,
        in_specs=(
            P("section", None, "tensor"),
            P("section", None, "tensor"),
            P(None, "section", None, "tensor"),
            P("section", None, None, "tensor", None),
            P("section", "tensor", None, None),
            P("section", None),
            P(),
            P(("section", "tensor"), None),
            P(),
            P(),
            P(),
        ),
        out_specs=(
            P("section", None, "tensor"),
            P("section", None, "tensor"),
            P(("section", "tensor"), None),
            P(),
        ),
        check_vma=False,
    )
```

time: 580 us -> 347 us (0.60)
  waiting for transfers between devices: 314 us -> 91.7 us
  blocking collectives: 142 us -> 66.4 us
  starting transfers between devices: 15.2 us -> 70.4 us
  local copies, waits for them, and re-layouts: 10.9 us -> 34.2 us
  matrix products: 41.2 us -> 32.9 us
    psum x4 -> x0, waiting for transfers between devices: 213 us -> none  [the longest x1 112 us: reduce_lookup(): summed = lax.psum(parts, ('section', 'tensor'))]
    reduce_scatter x6 -> x0, waiting for transfers between devices: 101 us -> none  [sum_width(): lax.psum_scatter(term.astype(jnp.bfloat16), 'tensor', scatter_dimension=1...]
    all_gather x10 -> x3, blocking collectives: 90 us -> 33.2 us  [the longest x2 28 us: gather(): return lax.all_gather(x, 'tensor', axis=axis, tiled=True)]
    psum x5 -> x0, blocking collectives: 51.8 us -> none  [the longest x2 29.2 us: sum_section(): lax.psum(for_sending(values), 'section')]
    all_gather x0 -> x3, waiting for transfers between devices: none -> 44.4 us  [gather(): return lax.all_gather(x, 'tensor', axis=axis, tiled=True)]
    ppermute x4 -> x23, starting transfers between devices: 14.7 us -> 49 us  [hop(): return lax.ppermute(x, 'section', pairs)]
    all_to_all x0 -> x3, blocking collectives: none -> 33.2 us  [the longest x1 16.8 us: sum_pieces(): got = lax.all_to_all(parts, 'tensor', 1, 1, tiled=True)]
    ppermute x4 -> x23, waiting for transfers between devices: 0.01 us -> 31.2 us  [hop(): return lax.ppermute(x, 'section', pairs)]
  transfers between devices with their start and end apart: 14 -> 31, of which waited for: 9 -> 16; matrix products, arithmetic and copies ran while one was open for 8% -> 13% of each run, Pallas kernels for 0% -> 0%
where the time goes in v1:
time: 347 us; the launch traced here: 342 us
  waiting for transfers between devices  91.7 us (26%)
  starting transfers between devices  70.4 us (20%)
  blocking collectives  66.4 us (19%)
  local copies, waits for them, and re-layouts  34.2 us (10%)
  matrix products  32.9 us (9%)
  other arithmetic  31.9 us (9%)
  between operations  14.8 us (4%)
    ppermute x23, starting transfers between devices, hop(): return lax.ppermute(x, 'section', pairs)  49 us
    all_gather x3, waiting for transfers between devices, gather(): return lax.all_gather(x, 'tensor', axis=axis, tiled=True)  44.4 us
    dot_general x30, matrix products, mm(): lax.dot_general(a, b, (((ca,), (cb,)), ((), ())), preferred_element_type=...  32.9 us
    ppermute x23, waiting for transfers between devices, hop(): return lax.ppermute(x, 'section', pairs)  31.2 us
    all_gather x2, blocking collectives, gather(): return lax.all_gather(x, 'tensor', axis=axis, tiled=True)  28 us
    all_to_all x1, blocking collectives, sum_pieces(): got = lax.all_to_all(parts, 'tensor', 1, 1, tiled=True)  16.8 us
    unnamed x130, local copies, waits for them, and re-layouts  14.7 us
    all_to_all x1, waiting for transfers between devices, sum_pieces(): got = lax.all_to_all(parts, 'tensor', 1, 1, tiled=True)  13.2 us
  transfers between devices with their start and end apart: 31, of which 16 were waited for; matrix products, arithmetic and copies ran while one was open for 13% of the time, Pallas kernels for 0%

profile of v1, /device:TPU:29, one launch (start us, length us, event | category | flops | bytes accessed | tf_op | source)
XLA Modules:
  0.0 342.3 jit_solution(18278446067868255260)
XLA Ops:
  8.4 1.3 convolution_convert_fusion.1
  9.8 1.4 copy.83
  11.2 3.7 %all-to-all-start = ((bf16[256,4,576]{0,2,1:T(8,128)(2,1)}), bf16[256,4,576]{0,2,1:T(8,128)(2,1)S(1)}, u32[]{:S(2)}, u32[]{:S(2)}) async-start(bf16[256,4,576]{0,2,1:T(8,128)(2,1)} %bitcast.1), calls=%async_computation | async-start | bytes 2359296 | tf_op jit(solution)/shard_map/all_to_all | solution.py:62
  15.6 13.2 %all-to-all-done = bf16[256,4,576]{0,2,1:T(8,128)(2,1)S(1)} async-done(((bf16[256,4,576]{0,2,1:T(8,128)(2,1)}), bf16[256,4,576]{0,2,1:T(8,128)(2,1)S(1)}, u32[]{:S(2)}, u32[]{:S(2)}) %all-to-all-start) | async-done | bytes 1179680 | tf_op jit(solution)/shard_map/all_to_all | solution.py:62
  29.1 5.2 %collective-permute-start = (bf16[256,576]{0,1:T(8,128)(2,1)S(1)}, bf16[256,576]{0,1:T(8,128)(2,1)S(1)}, u32[]{:S(2)}, u32[]{:S(2)}) collective-permute-start(bf16[256,576]{0,1:T(8,128)(2,1)S(1)} %convert_element_type.304), channel_id=1, source_target_pairs={{4,0},{12,8},{20,16},{28,24},{5,1},{13,9},{21,17},{29,25},{6,2},{1... | collective-permute-start | bytes 884744 | tf_op jit(solution)/shard_map/ppermute | solution.py:32
  35.4 3.9 %all-to-all-start.1 = ((bf16[128,4,576]{0,2,1:T(8,128)(2,1)}), bf16[128,4,576]{0,2,1:T(8,128)(2,1)S(1)}, u32[]{:S(2)}, u32[]{:S(2)}) async-start(bf16[128,4,576]{0,2,1:T(8,128)(2,1)} %bitcast.7), calls=%async_computation.1 | async-start | bytes 1179648 | tf_op jit(solution)/shard_map/all_to_all | solution.py:150
  40.1 1.4 collective-permute-start.3
  41.5 1.4 collective-permute-start.2
  42.8 1.4 collective-permute-start.1
  44.2 15.7 %all-gather = bf16[1,128,2304]{1,2,0:T(8,128)(2,1)} all-gather(bf16[1,128,576]{1,2,0:T(8,128)(2,1)S(1)} %copy-done.13), channel_id=2, replica_groups=mesh['section'=8,'tensor'=4] {'tensor'}, dimensions={2}, use_global_device_ids=true | all-gather | bytes 737280 | tf_op jit(solution)/shard_map/all_gather | solution.py:24
  59.9 2.6 copy.84
  66.6 2.0 multiply_convert_fusion
  68.6 2.1 fusion.14
  73.1 5.1 %all-to-all-start.2 = ((bf16[128,4,256]{2,0,1:T(8,128)(2,1)}), bf16[128,4,256]{2,0,1:T(8,128)(2,1)}, u32[]{:S(2)}, u32[]{:S(2)}) async-start(bf16[128,4,256]{2,0,1:T(8,128)(2,1)} %pad_maximum_fusion.4), calls=%async_computation.2 | async-start | bytes 524288 | tf_op jit(solution)/shard_map/all_to_all | solution.py:157
  78.2 1.4 fusion.11
  80.2 2.2 convolution_convert_fusion.8
  83.0 1.3 fusion.93
  91.4 1.9 fusion.18
  95.1 1.4 copy.113
  96.5 2.1 copy.91
  100.3 1.3 broadcast.315
  101.6 2.8 scatter.26
  104.4 2.5 pad_maximum_fusion
  106.9 2.3 copy.93
  109.1 4.2 %all-to-all-start.3 = ((bf16[144,4,576]{2,0,1:T(8,128)(2,1)}), bf16[144,4,576]{2,0,1:T(8,128)(2,1)}, u32[]{:S(2)}, u32[]{:S(2)}) async-start(bf16[144,4,576]{2,0,1:T(8,128)(2,1)} %copy.93), calls=%async_computation.3 | async-start | bytes 1474560 | tf_op jit(solution)/shard_map/all_to_all | solution.py:118
  115.1 12.3 %all_gather.22 = bf16[128,2304]{0,1:T(8,128)(2,1)S(1)} all-gather(bf16[128,576]{0,1:T(8,128)(2,1)S(1)} %slice_select_fusion.2), channel_id=1, replica_groups=mesh['section'=8,'tensor'=4] {'tensor'}, dimensions={1}, use_global_device_ids=true | all-gather | bytes 737280 | tf_op jit(solution)/shard_map/all_gather | solution.py:24
  129.5 1.4 fusion.126
  132.9 1.8 copy.111
  136.0 4.5 %collective-permute-start.5 = (bf16[128,576]{0,1:T(8,128)(2,1)S(1)}, bf16[128,576]{0,1:T(8,128)(2,1)S(1)}, u32[]{:S(2)}, u32[]{:S(2)}) collective-permute-start(bf16[128,576]{0,1:T(8,128)(2,1)S(1)} %fusion.63), channel_id=1, source_target_pairs={{4,0},{8,4},{12,8},{16,12},{20,16},{24,20},{28,24},{5,1},{9,5},{13... | collective-permute-start | bytes 442376 | tf_op jit(solution)/shard_map/ppermute | solution.py:32
  141.9 6.9 %all_to_all.54 = bf16[128,4,256]{2,0,1:T(8,128)(2,1)S(1)} all-to-all(bf16[128,4,256]{2,0,1:T(8,128)(2,1)S(1)} %pad_maximum_fusion.5), channel_id=1, replica_groups=mesh['section'=8,'tensor'=4] {'tensor'}, dimensions={1} | all-to-all | bytes 524288 | tf_op jit(solution)/shard_map/all_to_all | solution.py:157
  150.2 8.7 %collective-permute-start.9 = (bf16[256,576]{0,1:T(8,128)(2,1)S(1)}, bf16[256,576]{0,1:T(8,128)(2,1)S(1)}, u32[]{:S(2)}, u32[]{:S(2)}) collective-permute-start(bf16[256,576]{0,1:T(8,128)(2,1)S(1)} %pad_maximum_fusion.2), channel_id=1, source_target_pairs={{28,20},{29,21},{30,22},{31,23}} | collective-permute-start | bytes 884744 | tf_op jit(solution)/shard_map/ppermute | solution.py:32
  159.0 1.3 collective-permute-start.8
  160.3 1.3 collective-permute-start.7
  162.6 3.2 collective-permute-done.8
  165.8 3.2 collective-permute-done.7
  168.9 1.8 add_add_fusion.1
  170.7 2.0 collective-permute-start.10
  173.5 1.7 broadcast_select_fusion.1
  176.0 27.6 %all-gather.8.cloned.1.call-done = bf16[256,2304]{0,1:T(8,128)(2,1)} async-done(((bf16[256,576]{0,1:T(8,128)(2,1)}), bf16[256,2304]{0,1:T(8,128)(2,1)}) %all-gather.8.cloned.1.call-update) | async-done | bytes 1179664 | tf_op jit(solution)/shard_map/all_gather | solution.py:24
  203.6 1.7 fusion.2
  205.9 2.0 fusion.70
  207.9 5.2 %all-gather.3 = f32[4,3,256]{2,1,0:T(4,128)S(1)} all-gather(f32[1,3,256]{2,1,0:T(4,128)S(1)} %maximum_bitcast_fusion), channel_id=4, replica_groups=mesh['section'=8,'tensor'=4] {'tensor'}, dimensions={0}, use_global_device_ids=true | all-gather | bytes 15360 | tf_op jit(solution)/shard_map/all_gather | solution.py:67
  213.7 2.7 collective-permute-start.11
  218.4 2.2 collective-permute-done.12
  220.8 3.1 collective-permute-done.13
  226.4 2.6 convolution_convert_fusion
  229.0 2.4 copy.96
  231.4 16.8 %all_to_all.55 = bf16[256,4,576]{0,2,1:T(8,128)(2,1)S(1)} all-to-all(bf16[256,4,576]{0,2,1:T(8,128)(2,1)} %bitcast.162), channel_id=1, replica_groups=mesh['section'=8,'tensor'=4] {'tensor'}, dimensions={1} | all-to-all | bytes 2359296 | tf_op jit(solution)/shard_map/all_to_all | solution.py:62
  248.4 1.4 collective-permute-start.14
  249.9 4.5 %collective-permute-done.14 = bf16[256,576]{0,1:T(8,128)(2,1)S(1)} collective-permute-done((bf16[256,576]{0,1:T(8,128)(2,1)S(1)}, bf16[256,576]{0,1:T(8,128)(2,1)S(1)}, u32[]{:S(2)}, u32[]{:S(2)}) %collective-permute-start.14) | collective-permute-done | bytes 294944 | tf_op jit(solution)/shard_map/ppermute | solution.py:32
  254.5 1.4 collective-permute-start.17
  259.7 1.3 fusion.94
  261.0 7.4 %collective-permute-done.17 = bf16[256,576]{0,1:T(8,128)(2,1)S(1)} collective-permute-done((bf16[256,576]{0,1:T(8,128)(2,1)S(1)}, bf16[256,576]{0,1:T(8,128)(2,1)S(1)}, u32[]{:S(2)}, u32[]{:S(2)}) %collective-permute-start.17) | collective-permute-done | bytes 294944 | tf_op jit(solution)/shard_map/ppermute | solution.py:32
  270.8 4.4 %all-to-all-start.6 = ((bf16[128,4,128]{2,0,1:T(8,128)(2,1)}), bf16[128,4,128]{2,0,1:T(8,128)(2,1)S(1)}, u32[]{:S(2)}, u32[]{:S(2)}) async-start(bf16[128,4,128]{2,0,1:T(8,128)(2,1)} %bitcast.153), calls=%async_computation.6 | async-start | bytes 262144 | tf_op jit(solution)/shard_map/all_to_all | solution.py:165
  276.1 2.1 all-to-all-done.6
  281.1 1.4 scatter.29
  283.4 9.5 %all_to_all.56 = bf16[144,4,576]{2,0,1:T(8,128)(2,1)S(1)} all-to-all(bf16[144,4,576]{2,0,1:T(8,128)(2,1)S(1)} %copy.103), channel_id=1, replica_groups=mesh['section'=8,'tensor'=4] {'tensor'}, dimensions={1} | all-to-all | bytes 1327104 | tf_op jit(solution)/shard_map/all_to_all | solution.py:118
  296.8 1.3 collective-permute-start.22
  298.1 2.2 collective-permute-done.22
  302.4 2.0 collective-permute-done.6
  305.2 2.1 fusion.58
  307.3 7.2 %collective-permute-start.18 = (bf16[128,576]{0,1:T(8,128)(2,1)S(1)}, bf16[128,576]{0,1:T(8,128)(2,1)S(1)}, u32[]{:S(2)}, u32[]{:S(2)}) collective-permute-start(bf16[128,576]{0,1:T(8,128)(2,1)S(1)} %copy-done.17), channel_id=1, source_target_pairs={{4,0},{8,4},{12,8},{16,12},{20,16},{24,20},{28,24},{5,1},{9,5},{13... | collective-permute-start | bytes 442376 | tf_op jit(solution)/shard_map/ppermute | solution.py:32
  316.2 16.8 %all-gather.10.cloned.1.call-done = bf16[256,2304]{0,1:T(8,128)(2,1)} async-done(((bf16[256,576]{0,1:T(8,128)(2,1)}), bf16[256,2304]{0,1:T(8,128)(2,1)}) %all-gather.10.cloned.1.call-update) | async-done | bytes 1179664 | tf_op jit(solution)/shard_map/all_gather | solution.py:24
  333.0 2.8 fusion.1
  (248 shorter events, 59.4 us)
Async XLA Ops:
  7.2 2.5 copy-start.50
  11.2 17.7 %all-to-all-start = ((bf16[256,4,576]{0,2,1:T(8,128)(2,1)}), bf16[256,4,576]{0,2,1:T(8,128)(2,1)S(1)}, u32[]{:S(2)}, u32[]{:S(2)}) async-start(bf16[256,4,576]{0,2,1:T(8,128)(2,1)} %bitcast.1), calls=%async_computation | async-start | bytes 2359296 | tf_op jit(solution)/shard_map/all_to_all | solution.py:62
  14.9 53.7 %all-gather.12.cloned.1.call-start = ((), (), s32[]{:S(2)}) async-start(), calls=%async_computation.10 | async-start | bytes 1474560 | tf_op jit(solution)/shard_map/all_gather | solution.py:24
  15.6 18.7 %copy-start.30 = (bf16[1,1,128,2304]{3,2,1,0:T(8,128)(2,1)S(1)}, bf16[1,1,128,2304]{3,2,1,0:T(8,128)(2,1)}, u32[]{:S(2)}) copy-start(bf16[1,1,128,2304]{3,2,1,0:T(8,128)(2,1)} %param.23) | copy-start | bytes 1769476
  29.1 10.2 %copy-start.1 = (f32[256,576]{0,1:T(8,128)}, f32[256,576]{0,1:T(8,128)S(1)}, u32[]{:S(2)}) copy-start(f32[256,576]{0,1:T(8,128)S(1)} %convert_reduce_fusion.1) | copy-start | bytes 1769476
  29.1 10.2 %collective-permute-start = (bf16[256,576]{0,1:T(8,128)(2,1)S(1)}, bf16[256,576]{0,1:T(8,128)(2,1)S(1)}, u32[]{:S(2)}, u32[]{:S(2)}) collective-permute-start(bf16[256,576]{0,1:T(8,128)(2,1)S(1)} %convert_element_type.304), channel_id=1, source_target_pairs={{4,0},{12,8},{20,16},{28,24},{5,1},{13,9},{21,17},{29,25},{6,2},{1... | collective-permute-start | bytes 884744 | tf_op jit(solution)/shard_map/ppermute | solution.py:32
  35.4 8.8 %copy-start.13 = (bf16[1,128,576]{1,2,0:T(8,128)(2,1)S(1)}, bf16[1,128,576]{1,2,0:T(8,128)(2,1)}, u32[]{:S(2)}) copy-start(bf16[1,128,576]{1,2,0:T(8,128)(2,1)} %param.19) | copy-start | bytes 442372
  35.4 29.2 %all-to-all-start.1 = ((bf16[128,4,576]{0,2,1:T(8,128)(2,1)}), bf16[128,4,576]{0,2,1:T(8,128)(2,1)S(1)}, u32[]{:S(2)}, u32[]{:S(2)}) async-start(bf16[128,4,576]{0,2,1:T(8,128)(2,1)} %bitcast.7), calls=%async_computation.1 | async-start | bytes 1179648 | tf_op jit(solution)/shard_map/all_to_all | solution.py:150
  39.3 4.9 %copy-start.27 = (bf16[256,576]{0,1:T(8,128)(2,1)}, bf16[256,576]{0,1:T(8,128)(2,1)S(1)}, u32[]{:S(2)}) copy-start(bf16[256,576]{0,1:T(8,128)(2,1)S(1)} %collective-permute-done) | copy-start | bytes 884740
  40.1 26.5 %collective-permute-start.3 = (bf16[256,576]{0,1:T(8,128)(2,1)}, bf16[256,576]{0,1:T(8,128)(2,1)}, u32[]{:S(2)}, u32[]{:S(2)}) collective-permute-start(bf16[256,576]{0,1:T(8,128)(2,1)} %fusion.56), channel_id=1, source_target_pairs={{24,0},{25,1},{26,2},{27,3}} | collective-permute-start | bytes 884744 | tf_op jit(solution)/shard_map/ppermute | solution.py:32
  41.5 25.1 %collective-permute-start.2 = (bf16[256,576]{0,1:T(8,128)(2,1)}, bf16[256,576]{0,1:T(8,128)(2,1)}, u32[]{:S(2)}, u32[]{:S(2)}) collective-permute-start(bf16[256,576]{0,1:T(8,128)(2,1)} %fusion.56), channel_id=1, source_target_pairs={{16,0},{17,1},{18,2},{19,3}} | collective-permute-start | bytes 884744 | tf_op jit(solution)/shard_map/ppermute | solution.py:32
  42.8 23.7 %collective-permute-start.1 = (bf16[256,576]{0,1:T(8,128)(2,1)}, bf16[256,576]{0,1:T(8,128)(2,1)}, u32[]{:S(2)}, u32[]{:S(2)}) collective-permute-start(bf16[256,576]{0,1:T(8,128)(2,1)} %fusion.56), channel_id=1, source_target_pairs={{8,0},{9,1},{10,2},{11,3}} | collective-permute-start | bytes 884744 | tf_op jit(solution)/shard_map/ppermute | solution.py:32
  59.9 2.7 copy-start.41
  64.0 70.8 %copy-start.39 = (f32[576]{0:T(1024)}, f32[576]{0:T(1024)S(1)}, u32[]{:S(2)}) copy-start(f32[576]{0:T(1024)S(1)} %dynamic-slice_reduce_fusion) | copy-start | bytes 6916
  66.6 4.2 %copy-start.43 = (f32[2304]{0:T(1024)S(1)}, f32[2304]{0:T(1024)}, u32[]{:S(2)}) copy-start(f32[2304]{0:T(1024)} %convert_reduce_fusion.4) | copy-start | bytes 27652
  73.1 11.2 %all-to-all-start.2 = ((bf16[128,4,256]{2,0,1:T(8,128)(2,1)}), bf16[128,4,256]{2,0,1:T(8,128)(2,1)}, u32[]{:S(2)}, u32[]{:S(2)}) async-start(bf16[128,4,256]{2,0,1:T(8,128)(2,1)} %pad_maximum_fusion.4), calls=%async_computation.2 | async-start | bytes 524288 | tf_op jit(solution)/shard_map/all_to_all | solution.py:157
  84.3 5.7 %copy-start.35 = (bf16[128,384]{1,0:T(8,128)(2,1)S(1)}, bf16[128,384]{1,0:T(8,128)(2,1)}, u32[]{:S(2)}) copy-start(bf16[128,384]{1,0:T(8,128)(2,1)} %copy-done.34) | copy-start | bytes 294916
  93.3 20.1 %collective-permute-start.4 = (bf16[128,576]{0,1:T(8,128)(2,1)}, bf16[128,576]{0,1:T(8,128)(2,1)}, u32[]{:S(2)}, u32[]{:S(2)}) collective-permute-start(bf16[128,576]{0,1:T(8,128)(2,1)} %fusion.18), channel_id=1, source_target_pairs={{0,4},{4,8},{8,12},{12,16},{16,20},{20,24},{24,28},{1,5},{5,9},{9,... | collective-permute-start | bytes 442376 | tf_op jit(solution)/shard_map/ppermute | solution.py:32
  109.1 21.7 %all-to-all-start.3 = ((bf16[144,4,576]{2,0,1:T(8,128)(2,1)}), bf16[144,4,576]{2,0,1:T(8,128)(2,1)}, u32[]{:S(2)}, u32[]{:S(2)}) async-start(bf16[144,4,576]{2,0,1:T(8,128)(2,1)} %copy.93), calls=%async_computation.3 | async-start | bytes 1474560 | tf_op jit(solution)/shard_map/all_to_all | solution.py:118
  113.3 90.2 %all-gather.8.cloned.1.call-start = ((), (), s32[]{:S(2)}) async-start(), calls=%async_computation.8 | async-start | bytes 1474560 | tf_op jit(solution)/shard_map/all_gather | solution.py:24
  129.5 3.4 copy-start.57
  130.9 3.9 %copy-start.60 = (f32[128]{0:T(128)S(1)}, f32[128]{0:T(128)}, u32[]{:S(2)}) copy-start(f32[128]{0:T(128)} %copy-done.59) | copy-start | bytes 1540
  136.0 12.9 %copy-start.20 = (bf16[128,576]{0,1:T(8,128)(2,1)}, bf16[128,576]{0,1:T(8,128)(2,1)S(1)}, u32[]{:S(2)}) copy-start(bf16[128,576]{0,1:T(8,128)(2,1)S(1)} %fusion.63) | copy-start | bytes 442372
  136.0 5.5 %collective-permute-start.5 = (bf16[128,576]{0,1:T(8,128)(2,1)S(1)}, bf16[128,576]{0,1:T(8,128)(2,1)S(1)}, u32[]{:S(2)}, u32[]{:S(2)}) collective-permute-start(bf16[128,576]{0,1:T(8,128)(2,1)S(1)} %fusion.63), channel_id=1, source_target_pairs={{4,0},{8,4},{12,8},{16,12},{20,16},{24,20},{28,24},{5,1},{9,5},{13... | collective-permute-start | bytes 442376 | tf_op jit(solution)/shard_map/ppermute | solution.py:32
  141.5 7.4 %copy-start.23 = (bf16[128,576]{0,1:T(8,128)(2,1)S(1)}, bf16[128,576]{0,1:T(8,128)(2,1)}, u32[]{:S(2)}) copy-start(bf16[128,576]{0,1:T(8,128)(2,1)} %copy-done.22) | copy-start | bytes 442372
  141.5 7.7 %copy-start.10 = (bf16[128,576]{0,1:T(8,128)(2,1)}, bf16[128,576]{0,1:T(8,128)(2,1)S(1)}, u32[]{:S(2)}) copy-start(bf16[128,576]{0,1:T(8,128)(2,1)S(1)} %collective-permute-done.5) | copy-start | bytes 442372
  149.2 19.7 %copy-start.18 = (bf16[128,576]{0,1:T(8,128)(2,1)}, bf16[128,576]{0,1:T(8,128)(2,1)S(1)}, u32[]{:S(2)}) copy-start(bf16[128,576]{0,1:T(8,128)(2,1)S(1)} %add_convert_fusion) | copy-start | bytes 442372
  150.2 12.4 %collective-permute-start.9 = (bf16[256,576]{0,1:T(8,128)(2,1)S(1)}, bf16[256,576]{0,1:T(8,128)(2,1)S(1)}, u32[]{:S(2)}, u32[]{:S(2)}) collective-permute-start(bf16[256,576]{0,1:T(8,128)(2,1)S(1)} %pad_maximum_fusion.2), channel_id=1, source_target_pairs={{28,20},{29,21},{30,22},{31,23}} | collective-permute-start | bytes 884744 | tf_op jit(solution)/shard_map/ppermute | solution.py:32
  159.0 6.8 %collective-permute-start.8 = (bf16[256,576]{0,1:T(8,128)(2,1)S(1)}, bf16[256,576]{0,1:T(8,128)(2,1)S(1)}, u32[]{:S(2)}, u32[]{:S(2)}) collective-permute-start(bf16[256,576]{0,1:T(8,128)(2,1)S(1)} %pad_maximum_fusion.2), channel_id=1, source_target_pairs={{28,12},{29,13},{30,14},{31,15}} | collective-permute-start | bytes 884744 | tf_op jit(solution)/shard_map/ppermute | solution.py:32
  160.3 8.6 %collective-permute-start.7 = (bf16[256,576]{0,1:T(8,128)(2,1)S(1)}, bf16[256,576]{0,1:T(8,128)(2,1)S(1)}, u32[]{:S(2)}, u32[]{:S(2)}) collective-permute-start(bf16[256,576]{0,1:T(8,128)(2,1)S(1)} %pad_maximum_fusion.2), channel_id=1, source_target_pairs={{28,4},{29,5},{30,6},{31,7}} | collective-permute-start | bytes 884744 | tf_op jit(solution)/shard_map/ppermute | solution.py:32
  170.7 2.8 collective-permute-start.10
  172.7 33.1 %copy-start.51 = (s32[256]{0:T(256)S(1)}, s32[256]{0:T(256)}, u32[]{:S(2)}) copy-start(s32[256]{0:T(256)} %copy-done.50) | copy-start | bytes 3076
  176.0 31.9 %copy-start.37 = (f32[2304]{0:T(1024)}, f32[2304]{0:T(1024)S(1)}, u32[]{:S(2)}) copy-start(f32[2304]{0:T(1024)S(1)} %convert_element_type.351) | copy-start | bytes 27652
  213.7 3.7 %collective-permute-start.11 = (f32[3,256]{1,0:T(4,128)}, f32[3,256]{1,0:T(4,128)S(1)}, u32[]{:S(2)}, u32[]{:S(2)}) collective-permute-start(f32[3,256]{1,0:T(4,128)} %reduce_sum.249), channel_id=1, source_target_pairs={{0,4},{4,0},{8,12},{12,8},{16,20},{20,16},{24,28},{28,24},{1,5},{5... | collective-permute-start | bytes 9224 | tf_op jit(solution)/shard_map/ppermute | solution.py:32
  218.1 2.5 collective-permute-start.12
  220.6 3.4 collective-permute-start.13
  248.3 10.2 %copy-start.6 = (bf16[1,128,2304]{1,2,0:T(8,128)(2,1)S(1)}, bf16[1,128,2304]{1,2,0:T(8,128)(2,1)}, u32[]{:S(2)}) copy-start(bf16[1,128,2304]{1,2,0:T(8,128)(2,1)} %all-gather) | copy-start | bytes 1769476
  248.3 10.2 %copy-start.25 = (bf16[2,1,128,2304]{2,3,1,0:T(8,128)(2,1)S(1)}, bf16[2,1,128,2304]{2,3,1,0:T(8,128)(2,1)}, u32[]{:S(2)}) copy-start(bf16[2,1,128,2304]{2,3,1,0:T(8,128)(2,1)} %all-gather.12.cloned.1.call-done) | copy-start | bytes 3538948
  248.3 10.2 %copy-start.44 = (f32[2304]{0:T(1024)S(1)}, f32[2304]{0:T(1024)}, u32[]{:S(2)}) copy-start(f32[2304]{0:T(1024)} %convert_reduce_fusion.4) | copy-start | bytes 27652
  248.4 6.0 %collective-permute-start.14 = (bf16[256,576]{0,1:T(8,128)(2,1)S(1)}, bf16[256,576]{0,1:T(8,128)(2,1)S(1)}, u32[]{:S(2)}, u32[]{:S(2)}) collective-permute-start(bf16[256,576]{0,1:T(8,128)(2,1)S(1)} %convert_element_type.356), channel_id=1, source_target_pairs={{0,4},{8,12},{16,20},{24,28},{1,5},{9,13},{17,21},{25,29},{2,6},{1... | collective-permute-start | bytes 884744 | tf_op jit(solution)/shard_map/ppermute | solution.py:32
  254.5 13.9 %copy-start.4 = (bf16[256,576]{0,1:T(8,128)(2,1)S(1)}, bf16[256,576]{0,1:T(8,128)(2,1)}, u32[]{:S(2)}) copy-start(bf16[256,576]{0,1:T(8,128)(2,1)} %broadcast_select_fusion.1) | copy-start | bytes 884740
  254.5 13.9 %copy-start.46 = (f32[256]{0:T(256)S(1)}, f32[256]{0:T(256)}, u32[]{:S(2)}) copy-start(f32[256]{0:T(256)} %copy-done.45) | copy-start | bytes 3076
  254.5 13.9 %collective-permute-start.17 = (bf16[256,576]{0,1:T(8,128)(2,1)S(1)}, bf16[256,576]{0,1:T(8,128)(2,1)S(1)}, u32[]{:S(2)}, u32[]{:S(2)}) collective-permute-start(bf16[256,576]{0,1:T(8,128)(2,1)S(1)} %fusion.57), channel_id=1, source_target_pairs={{20,28},{21,29},{22,30},{23,31}} | collective-permute-start | bytes 884744 | tf_op jit(solution)/shard_map/ppermute | solution.py:32
  255.9 12.5 %collective-permute-start.16 = (bf16[256,576]{0,1:T(8,128)(2,1)S(1)}, bf16[256,576]{0,1:T(8,128)(2,1)S(1)}, u32[]{:S(2)}, u32[]{:S(2)}) collective-permute-start(bf16[256,576]{0,1:T(8,128)(2,1)S(1)} %fusion.57), channel_id=1, source_target_pairs={{12,28},{13,29},{14,30},{15,31}} | collective-permute-start | bytes 884744 | tf_op jit(solution)/shard_map/ppermute | solution.py:32
  257.2 11.2 %collective-permute-start.15 = (bf16[256,576]{0,1:T(8,128)(2,1)S(1)}, bf16[256,576]{0,1:T(8,128)(2,1)S(1)}, u32[]{:S(2)}, u32[]{:S(2)}) collective-permute-start(bf16[256,576]{0,1:T(8,128)(2,1)S(1)} %fusion.57), channel_id=1, source_target_pairs={{4,28},{5,29},{6,30},{7,31}} | collective-permute-start | bytes 884744 | tf_op jit(solution)/shard_map/ppermute | solution.py:32
  259.7 9.1 %copy-start.32 = (bf16[128,384]{1,0:T(8,128)(2,1)}, bf16[128,384]{1,0:T(8,128)(2,1)S(1)}, u32[]{:S(2)}) copy-start(bf16[128,384]{1,0:T(8,128)(2,1)S(1)} %convolution_convert_fusion.7) | copy-start | bytes 294916
  269.4 8.9 %copy-start.58 = (f32[128]{0:T(128)S(1)}, f32[128]{0:T(128)}, u32[]{:S(2)}) copy-start(f32[128]{0:T(128)} %get-tuple-element.77) | copy-start | bytes 1540
  270.1 9.2 %copy-start.33 = (bf16[128,384]{1,0:T(8,128)(2,1)S(1)}, bf16[128,384]{1,0:T(8,128)(2,1)}, u32[]{:S(2)}) copy-start(bf16[128,384]{1,0:T(8,128)(2,1)} %copy-done.32) | copy-start | bytes 294916
  270.1 9.2 %copy-start.36 = (f32[128,128]{0,1:T(8,128)S(1)}, f32[128,128]{0,1:T(8,128)}, u32[]{:S(2)}) copy-start(f32[128,128]{0,1:T(8,128)} %get-tuple-element.78) | copy-start | bytes 196612
  270.8 7.5 %all-to-all-start.6 = ((bf16[128,4,128]{2,0,1:T(8,128)(2,1)}), bf16[128,4,128]{2,0,1:T(8,128)(2,1)S(1)}, u32[]{:S(2)}, u32[]{:S(2)}) async-start(bf16[128,4,128]{2,0,1:T(8,128)(2,1)} %bitcast.153), calls=%async_computation.6 | async-start | bytes 262144 | tf_op jit(solution)/shard_map/all_to_all | solution.py:165
  275.2 57.8 %all-gather.10.cloned.1.call-start = ((), (), s32[]{:S(2)}) async-start(), calls=%async_computation.9 | async-start | bytes 1474560 | tf_op jit(solution)/shard_map/all_gather | solution.py:24
  294.2 6.8 %copy-start.16 = (bf16[128,576]{0,1:T(8,128)(2,1)}, bf16[128,576]{0,1:T(8,128)(2,1)S(1)}, u32[]{:S(2)}) copy-start(bf16[128,576]{0,1:T(8,128)(2,1)S(1)} %subtract_convert_fusion.1) | copy-start | bytes 442372
  294.3 6.8 %copy-start.19 = (bf16[128,576]{0,1:T(8,128)(2,1)S(1)}, bf16[128,576]{0,1:T(8,128)(2,1)}, u32[]{:S(2)}) copy-start(bf16[128,576]{0,1:T(8,128)(2,1)} %copy-done.18) | copy-start | bytes 442372
  294.3 10.1 %copy-start.26 = (bf16[256,576]{0,1:T(8,128)(2,1)S(1)}, bf16[256,576]{0,1:T(8,128)(2,1)}, u32[]{:S(2)}) copy-start(bf16[256,576]{0,1:T(8,128)(2,1)} %multiply_convert_fusion) | copy-start | bytes 884740
  294.3 2.2 collective-permute-start.21
  295.1 1.4 collective-permute-start.20
  295.8 0.7 collective-permute-start.19
  296.7 8.3 %copy-start.48 = (f32[1,256]{1,0:T(1,128)S(1)}, f32[1,256]{1,0:T(1,128)}, u32[]{:S(2)}) copy-start(f32[1,256]{1,0:T(1,128)} %copy-done.47) | copy-start | bytes 3076
  296.7 8.3 %copy-start.54 = (f32[1,256]{1,0:T(1,128)S(1)}, f32[1,256]{1,0:T(1,128)}, u32[]{:S(2)}) copy-start(f32[1,256]{1,0:T(1,128)} %get-tuple-element.57) | copy-start | bytes 3076
  296.7 8.4 %copy-start.38 = (f32[2304]{0:T(1024)S(1)}, f32[2304]{0:T(1024)}, u32[]{:S(2)}) copy-start(f32[2304]{0:T(1024)} %copy-done.37) | copy-start | bytes 27652
  296.8 3.6 %collective-permute-start.22 = (bf16[256,576]{0,1:T(8,128)(2,1)S(1)}, bf16[256,576]{0,1:T(8,128)(2,1)S(1)}, u32[]{:S(2)}, u32[]{:S(2)}) collective-permute-start(bf16[256,576]{0,1:T(8,128)(2,1)S(1)} %add_add_fusion), channel_id=1, source_target_pairs={{0,4},{8,12},{16,20},{24,28},{1,5},{9,13},{17,21},{25,29},{2,6},{1... | collective-permute-start | bytes 884744 | tf_op jit(solution)/shard_map/ppermute | solution.py:32
  301.1 3.3 collective-permute-start.6
  305.2 10.3 %copy-start.9 = (bf16[256,576]{0,1:T(8,128)(2,1)S(1)}, bf16[256,576]{0,1:T(8,128)(2,1)}, u32[]{:S(2)}) copy-start(bf16[256,576]{0,1:T(8,128)(2,1)} %copy-done.7) | copy-start | bytes 884740
  307.3 8.2 %collective-permute-start.18 = (bf16[128,576]{0,1:T(8,128)(2,1)S(1)}, bf16[128,576]{0,1:T(8,128)(2,1)S(1)}, u32[]{:S(2)}, u32[]{:S(2)}) collective-permute-start(bf16[128,576]{0,1:T(8,128)(2,1)S(1)} %copy-done.17), channel_id=1, source_target_pairs={{4,0},{8,4},{12,8},{16,12},{20,16},{24,20},{28,24},{5,1},{9,5},{13... | collective-permute-start | bytes 442376 | tf_op jit(solution)/shard_map/ppermute | solution.py:32
  (29 other events, 36.7 us)
Sparse Core Ops, SparseCore 0:
  17.6 37.0 all-gather.11
  175.4 28.1 all-gather.7
  301.2 31.7 all-gather.9

commit v2 on v0

v2 whole, which is shorter than its diff:
```python
import functools
import math

import jax
import jax.numpy as jnp
from jax import lax
from jax.experimental import pallas as pl
from jax.experimental.pallas import tpu as pltpu
from jax.sharding import PartitionSpec as P

EPS = 1e-06
ATTN_CAP = 50.0
LOGIT_CAP = 30.0
F32 = jnp.float32
BF16 = jnp.bfloat16
EXTRA = 16


def dot(a, b, ca=1, cb=0):
    return lax.dot_general(a, b, (((ca,), (cb,)), ((), ())), preferred_element_type=F32)


def call(body, outs, args, name, flops=0, scratch=()):
    moved = sum(x.size * x.dtype.itemsize for x in args)
    moved += sum(math.prod(s) * jnp.dtype(d).itemsize for s, d in outs)
    vmem = pl.BlockSpec(memory_space=pltpu.VMEM)
    got = pl.pallas_call(
        body,
        out_shape=[jax.ShapeDtypeStruct(s, d) for s, d in outs],
        in_specs=[pl.BlockSpec(memory_space=pltpu.SMEM)] + [vmem] * (len(args) - 1),
        out_specs=[vmem] * len(outs),
        scratch_shapes=list(scratch),
        cost_estimate=pl.CostEstimate(flops=flops, bytes_accessed=moved, transcendentals=0),
        compiler_params=pltpu.CompilerParams(vmem_limit_bytes=24 << 20),
        name=name,
    )(*args)
    return got[0] if len(outs) == 1 else got


def block_of(here, d, size):
    return pl.ds(pl.multiple_of((here[0] ^ d) * size, size), size)


def rows_of(row, count):
    return jnp.broadcast_to(row, (count, row.shape[1]))


def split_rows(values):
    count = len(values)
    place = lax.broadcasted_iota(jnp.int32, (EXTRA, values[0].shape[1]), 0)
    out = jnp.zeros(place.shape, F32)
    for i, row in enumerate(values):
        high = row.astype(BF16).astype(F32)
        out = jnp.where(place == i, high, out)
        out = jnp.where(place == count + i, row - high, out)
    return out.astype(BF16)


def join_rows(extra, count):
    return [extra[i : i + 1, :] + extra[count + i : count + i + 1, :] for i in range(count)]


def tree_sum(parts):
    parts = list(parts)
    while len(parts) > 1:
        pairs = [parts[i] + parts[i + 1] for i in range(0, len(parts) - 1, 2)]
        parts = pairs + parts[len(parts) - len(parts) % 2 :]
    return parts[0]


def total_of(refs):
    return tree_sum([r[...].astype(F32) for r in refs])


def turn_column(row_ref, out_ref):
    full, width = out_ref.shape
    for at in range(0, full, width):
        part = jnp.broadcast_to(row_ref[0:1, at : at + width].astype(F32), (width, width))
        out_ref[at : at + width, :] = part.T.astype(BF16)


def prepare_kernel(n, here, x_ref, w_ref, gain_ref, fgain_ref, *refs):
    outs, (gcol_ref, fcol_ref, turned) = refs[:n], refs[n:]
    size = x_ref.shape[0]
    turned[...] = w_ref[...].T
    for d in range(n):
        outs[d][:size, :] = x_ref[...]
        outs[d][size:, :] = turned[block_of(here, d, size), :]
    turn_column(gain_ref, gcol_ref)
    turn_column(fgain_ref, fcol_ref)


def attend(x, gain, wq_ref):
    scale = lax.rsqrt(jnp.mean(x * x, axis=0, keepdims=True) + EPS)
    normed = (x * scale * gain).astype(BF16).T
    q = dot(normed, wq_ref[0]).astype(BF16)
    k = dot(normed, wq_ref[1]).astype(BF16)
    v = dot(normed, wq_ref[2]).astype(BF16)
    qt = q.T
    capped = jnp.tanh(dot(k, qt) * q.shape[1] ** -0.5 / ATTN_CAP)
    key = lax.broadcasted_iota(jnp.int32, capped.shape, 0)
    query = lax.broadcasted_iota(jnp.int32, capped.shape, 1)
    raised = jnp.where(key <= query, jnp.exp(ATTN_CAP * capped), 0.0)
    probs = (raised / jnp.sum(raised, axis=0, keepdims=True)).astype(BF16)
    return scale, qt, k, v, capped, probs


def forward_kernel(n, size, here, *refs):
    xs, (gain_ref, wq_ref, out, xfull) = refs[:n], refs[n:]
    for d in range(n):
        xfull[block_of(here, d, size), :] = xs[d][:size, :]
    x = xfull[...].astype(F32)
    _, _, _, v, _, probs = attend(x, gain_ref[...].astype(F32), wq_ref)
    out[...] = dot(v.T, probs).astype(BF16)


def forward_parts_kernel(n, size, here, *refs):
    xs, (gain_ref, wq_ref, cot_ref), outs, xfull = refs[:n], refs[n : n + 3], refs[n + 3 : -1], refs[-1]
    head = wq_ref.shape[-1]
    forward_kernel(n, size, here, *xs, gain_ref, wq_ref, outs[0].at[:head, :], xfull)
    for d in range(n):
        if d > 0:
            outs[d][:head, :] = outs[0][:head, :]
        part = dot(xs[d][size : 2 * size, :], cot_ref[...], 0, 0)
        outs[d][head:, :] = part.astype(BF16)


def recompute_kernel(n, tick, here, *refs):
    bs, refs = refs[:n], refs[n:]
    xs, refs = refs[: n * tick], refs[n * tick :]
    gain_ref, wq_ref, qkv_ref, v_ref, capped_ref, probs_ref, scale_ref, xfull = refs
    size = bs[0].shape[0]
    for d in range(n):
        block = bs[d][...]
        if tick > 0:
            block = jnp.where(here[2] == here[3] - 1, xs[d][:size, :], block)
        xfull[block_of(here, d, size), :] = block
    x = xfull[...].astype(F32)
    scale, qt, k, v, capped, probs = attend(x, gain_ref[...].astype(F32), wq_ref)
    qkv_ref[0] = qt
    qkv_ref[1] = k.T
    qkv_ref[2] = v.T
    v_ref[...] = v
    capped_ref[...] = capped
    probs_ref[...] = probs
    scale_ref[...] = rows_of(scale, 8)


def parts_kernel(n, size, here, cot_ref, *refs):
    wos, outs = refs[:n], refs[n:]
    for d in range(n):
        outs[d][...] = dot(wos[d][size : 2 * size, :], cot_ref[...], 0, 0).astype(BF16)


def layer_out_kernel(n, size, here, x_ref, first_ref, *refs):
    got, wos, (out, send_ref, own_ref) = refs[:n], refs[n : 2 * n], refs[2 * n :]
    head = wos[0].shape[1]
    total = x_ref[...].astype(F32)
    for d in range(n):
        total = total + dot(wos[d][size : 2 * size, :], got[d][:head, :])
    y = total.astype(BF16)
    out[...] = y
    send = jnp.where(here[2] % 2 == 0, first_ref[...], y)
    send_ref[...] = send
    own_ref[...] = jnp.where(here[2] >= here[3] - 2, send, jnp.zeros_like(send))


def back_kernel(n, here, *refs):
    got, refs = refs[:n], refs[n:]
    qkv_ref, v_ref, capped_ref, probs_ref, wq_ref = refs[:5]
    outs = refs[5:]
    head = v_ref.shape[1]
    first = got[0].shape[0] - head
    da = sum(g[first:, :].astype(F32) for g in got).astype(BF16)
    probs = probs_ref[...]
    pfull = probs.astype(F32)
    dprob = dot(v_ref[...], da)
    dscore = pfull * (dprob - jnp.sum(dprob * pfull, axis=0, keepdims=True))
    capped = capped_ref[...]
    dlogit = (dscore * (1.0 - capped * capped) * head**-0.5).astype(BF16)
    grads = (
        dot(qkv_ref[1], dlogit).astype(BF16),
        dot(qkv_ref[0], dlogit, 1, 1).astype(BF16),
        dot(da, probs, 1, 1).astype(BF16),
    )
    stat = sum(
        jnp.sum(g.astype(F32) * qkv_ref[i].astype(F32), axis=0, keepdims=True)
        for i, g in enumerate(grads)
    )
    stat = split_rows([stat])
    size = outs[0].shape[0] - EXTRA
    for d in range(n):
        at = block_of(here, d, size)
        term = sum(dot(wq_ref[i, at, :], g) for i, g in enumerate(grads))
        outs[d][:size, :] = term.astype(BF16)
        outs[d][size:, :] = stat


def back_out_kernel(n, full, lasts, here, *refs):
    got, refs = refs[:n], refs[n:]
    scale_ref, gain_ref, x_ref, last_x_ref, cot_ref, other_ref, out = refs
    size = x_ref.shape[0]
    total = total_of(got)
    (stat,) = join_rows(total[size:, :], 1)
    scale = scale_ref[0:1, :]
    gain = gain_ref[block_of(here, 0, size), :].astype(F32)
    x = jnp.where(here[2] == here[3] - 1, last_x_ref[...], x_ref[...]).astype(F32)
    dx = (
        cot_ref[...].astype(F32)
        + scale * gain * total[:size, :]
        - x * (scale * scale * stat / full)
    )
    out[...] = jnp.where(here[2] >= here[3] - lasts, dx.astype(BF16), other_ref[...])


def lookup_kernel(here, ids_ref, targets_ref, table_ref, turned_ref, *outs):
    turned_ref[...] = table_ref[...].T
    vocab = turned_ref.shape[1]
    ticks, rows = ids_ref.shape
    column = here[1] + lax.broadcasted_iota(jnp.int32, (vocab, rows), 0)
    even = here[2] % 2 == 0
    for t in range(ticks):
        ids, targets = ids_ref[t : t + 1, :], targets_ref[t : t + 1, :]
        wanted = (jnp.where(even, ids, targets), jnp.where(even, targets, ids))
        for out, row in zip(outs, wanted):
            hits = (column == row).astype(F32).astype(BF16)
            out[:, t * rows : (t + 1) * rows] = dot(turned_ref[...], hits).astype(BF16)


def pair_kernel(here, keep_ref, got_ref, *outs):
    size = outs[0].shape[0]
    for d, out in enumerate(outs):
        at = block_of(here, d, size)
        out[...] = (keep_ref[at, :].astype(F32) + got_ref[at, :].astype(F32)).astype(BF16)


def assemble_kernel(n, here, *refs):
    parts, out = refs[:n], refs[n]
    for d in range(n):
        out[block_of(here, d, parts[d].shape[0]), :] = parts[d][...]


def pick_kernel(here, even_ref, odd_ref, send_ref, own_ref):
    send = jnp.where(here[2] % 2 == 0, even_ref[...], odd_ref[...])
    send_ref[...] = send
    own_ref[...] = jnp.where(here[2] < 2, send, jnp.zeros_like(send))


def enter_kernel(tick, emb_scale, here, y_ref, *refs):
    found, out = refs[:-1], refs[-1]
    rows = y_ref.shape[1]
    entering = tree_sum([f[:, tick * rows : (tick + 1) * rows].astype(F32) for f in found])
    entering = (entering * emb_scale).astype(BF16)
    out[...] = jnp.where(here[2] == 0, entering, y_ref[...])


def head_kernel(n, flip, here, h_ref, gain_ref, table_ref, turned_ref, target_ref, *refs):
    normed_ref, raw_ref, scale_ref, out = refs
    size = out.shape[0] // n - EXTRA
    h = h_ref[...].astype(F32)
    scale = lax.rsqrt(jnp.mean(h * h, axis=0, keepdims=True) + EPS)
    normed = (h * scale * gain_ref[...].astype(F32)).astype(BF16)
    normed_ref[...] = normed
    raw = dot(table_ref[...], normed)
    raw_ref[...] = raw
    scale_ref[...] = rows_of(scale, 8)
    column = here[1] + lax.broadcasted_iota(jnp.int32, raw.shape, 0)
    target = jnp.where(here[2] % 2 == flip, target_ref[0:1, :], target_ref[1:2, :])
    hit = column == target
    capped = jnp.tanh(raw / LOGIT_CAP)
    others = jnp.where(hit, 0.0, jnp.exp(LOGIT_CAP * capped))
    weighted = others * (1.0 - capped * capped)
    extra = split_rows(
        [
            jnp.sum(others, axis=0, keepdims=True),
            jnp.sum(weighted * raw, axis=0, keepdims=True),
            jnp.sum(jnp.where(hit, raw, 0.0), axis=0, keepdims=True),
        ]
    )
    weighted = weighted.astype(BF16)
    for d in range(n):
        at = d * (size + EXTRA)
        term = dot(turned_ref[block_of(here, d, size), :], weighted)
        out[at : at + size, :] = term.astype(BF16)
        out[at + size : at + size + EXTRA, :] = extra


def add_terms(total, out):
    size = out.shape[0] - EXTRA
    out[:size, :] = total[:size, :].astype(BF16)
    out[size:, :] = split_rows(join_rows(total[size:, :], 3))


def pair_terms_kernel(here, keep_ref, got_ref, *outs):
    step = outs[0].shape[0]
    for d, out in enumerate(outs):
        cut = slice(d * step, (d + 1) * step)
        add_terms(keep_ref[cut, :].astype(F32) + got_ref[cut, :].astype(F32), out)


def sum_kernel(here, *refs):
    add_terms(total_of(refs[:-1]), refs[-1])


def cot_kernel(tick, full, here, total_ref, scale_ref, h_ref, gain_ref, *refs):
    found, (out, sums_ref) = refs[:-2], refs[-2:]
    size, rows = h_ref.shape
    gain = gain_ref[block_of(here, 0, size), :].astype(F32)
    rest, weighted, raw_hit = join_rows(total_ref[size:, :].astype(F32), 3)
    capped = jnp.tanh(raw_hit / LOGIT_CAP)
    slope = 1.0 - capped * capped
    whole = rest + jnp.exp(LOGIT_CAP * capped)
    target = tree_sum([f[:, tick * rows : (tick + 1) * rows].astype(F32) for f in found])
    dhid = (total_ref[:size, :].astype(F32) - target * (rest * slope)) / whole
    stat = (weighted - rest * slope * raw_hit) / whole
    scale = scale_ref[0:1, :]
    out[...] = (
        scale * gain * dhid - h_ref[...].astype(F32) * (scale * scale * stat / full)
    ).astype(BF16)
    place = lax.broadcasted_iota(jnp.int32, (8, rows), 0)
    sums = jnp.where(place == 0, rest, jnp.where(place == 1, raw_hit, 0.0))
    sums_ref[...] = jnp.where(here[2] == here[3] - 1, sums, 0.0)


def grad_kernel(ticks, emb_scale, here, ids_ref, targets_ref, sums_ref, *refs):
    out, loss_ref = refs[-2:]
    vocab, rows = refs[0].shape
    column = here[1] + lax.broadcasted_iota(jnp.int32, (vocab, rows), 0)
    place = lax.broadcasted_iota(jnp.int32, loss_ref.shape, 0)
    losses = jnp.zeros(loss_ref.shape, F32)
    for t in range(ticks):
        rest, raw_hit = sums_ref[8 * t : 8 * t + 1, :], sums_ref[8 * t + 1 : 8 * t + 2, :]
        logit = LOGIT_CAP * jnp.tanh(raw_hit / LOGIT_CAP)
        loss = jnp.mean(jnp.log(rest + jnp.exp(logit)) - logit, axis=1, keepdims=True)
        losses = jnp.where(place == t, jnp.broadcast_to(loss, losses.shape), losses)
    loss_ref[...] = losses
    dlogs, hits = [], []
    for flip in range(2):
        first = here[2] % 2 == flip
        sums = jnp.where(first, sums_ref[0:8, :], sums_ref[8:16, :])
        rest, raw_hit = sums[0:1, :], sums[1:2, :]
        whole = rest + jnp.exp(LOGIT_CAP * jnp.tanh(raw_hit / LOGIT_CAP))
        capped = jnp.tanh(refs[3 * flip][...] / LOGIT_CAP)
        hit = column == jnp.where(first, targets_ref[0:1, :], targets_ref[1:2, :])
        top = jnp.where(hit, -rest, jnp.exp(LOGIT_CAP * capped))
        dlogs.append((top / whole * (1.0 - capped * capped)).astype(BF16))
        hit = column == jnp.where(first, ids_ref[0:1, :], ids_ref[1:2, :])
        hits.append(hit.astype(F32).astype(BF16))
    full = out.shape[1]
    step = 256 if full % 256 == 0 else full
    for at in range(0, full, step):
        cut = slice(at, at + step)
        looked = sum(dot(hits[i], refs[3 * i + 2][cut, :], 1, 1) for i in range(2))
        heads = sum(dot(dlogs[i], refs[3 * i + 1][cut, :], 1, 1) for i in range(2))
        out[:, cut] = (heads + looked * emb_scale).astype(BF16)


def last_cots_kernel(here, gin_ref, cot_ref, out):
    out[...] = jnp.where(here[2] == here[3] - 1, cot_ref[...], gin_ref[...])


def after(x, *others):
    return lax.optimization_barrier((x, *others))[0]


def hop(x, pairs):
    return lax.ppermute(x, "section", pairs)


def swap(blocks, sections=None):
    n = lax.axis_size("tensor")
    if sections is None:
        return [blocks[0]] + [
            lax.ppermute(blocks[d], "tensor", [(i, i ^ d) for i in range(n)])
            for d in range(1, n)
        ]
    out = [blocks[0]]
    for d in range(1, n):
        pairs = [(s * n + i, s * n + (i ^ d)) for s in sections for i in range(n)]
        out.append(lax.ppermute(blocks[d], ("section", "tensor"), pairs))
    return out


def share(x):
    return swap([x] * lax.axis_size("tensor"))


def other_chips(root):
    core = root % 2
    return [
        2 * c + core for c in range(lax.axis_size("section") // 2) if c != root // 2
    ]


def along_chips(x, root):
    return [hop(x, [(root, s)]) for s in other_chips(root)]


def across(root):
    return [(s, s ^ 1) for s in [root] + other_chips(root)]


def from_chip(own, send, root):
    for s in other_chips(root):
        own = own + hop(send, [(root, s), (root ^ 1, s ^ 1)])
    return own


def to_chips(x, even_root, odd_root):
    sources = zip(other_chips(even_root), other_chips(odd_root))
    return [x] + [hop(x, [(a, even_root), (b, odd_root)]) for a, b in sources]


def other_core(x):
    return hop(x, [(i, i ^ 1) for i in range(lax.axis_size("section"))])


def body(
    fwd_in, back_in, stash, w_qkv, w_out, norm_gain, final_gain, table, ids, back_ids, targets
):
    pos = lax.axis_index("section")
    sections = lax.axis_size("section")
    tpos = lax.axis_index("tensor")
    n = lax.axis_size("tensor")
    rows, piece = fwd_in.shape[1:]
    full = piece * n
    vocab = table.shape[0]
    ticks = ids.shape[0]
    head = w_qkv.shape[-1]
    last = sections - 1
    emb_scale = math.sqrt(full)
    here = jnp.stack([tpos, (pos * n + tpos) * vocab, pos, jnp.full_like(pos, sections)])
    here = here.astype(jnp.int32)
    up = [(i, i + 1) for i in range(last)]
    down = [(i + 1, i) for i in range(last)]

    acts = fwd_in[0].T
    cots = back_in[0].T
    held0, held1 = stash[0, 0].T, stash[1, 0].T
    wq = w_qkv[0, :, :, 0, :].transpose(1, 0, 2)

    work = (2 * full * rows * 3 * head) + 4 * rows * rows * head
    act = ((piece, rows), BF16)
    wide = ((full, rows), BF16)
    message = ((piece + EXTRA, rows), BF16)
    whole_x = [pltpu.VMEM((full, rows), BF16)]

    *first, gain, fgain = call(
        functools.partial(prepare_kernel, n),
        [((2 * piece, rows), BF16)] * n + [wide] * 2,
        [here, acts, w_out[0, 0], norm_gain, final_gain[None]],
        "prepare",
        scratch=[pltpu.VMEM((full, head), BF16)],
    )
    base = swap(first)
    turned, *rows_found = call(
        lookup_kernel,
        [((full, vocab), BF16)] + [((full, ticks * rows), BF16)] * 2,
        [here, ids, targets, after(table, gain)],
        "lookup",
        4 * full * rows * vocab * ticks,
    )

    def look_up(keep, send):
        found = call(
            pair_kernel,
            [((piece, ticks * rows), BF16)] * n,
            [here, keep, other_core(send)],
            "pair",
        )
        return tree_sum([b.astype(F32) for b in swap(found)]).astype(BF16)

    found = look_up(*rows_found)

    def layer_out(x, got, earlier):
        return call(
            functools.partial(layer_out_kernel, n, piece),
            [act] * 3,
            [here, x, earlier, *got, *base],
            "layer_out",
            2 * piece * rows * head * n,
        )

    def back(got, saved):
        return call(
            functools.partial(back_kernel, n),
            [message] * n,
            [here, *got, *saved[:4], wq],
            "back",
            work,
        )

    def back_out(got, saved, x, last_x, cot, other=None):
        return call(
            functools.partial(back_out_kernel, n, full, sections if other is None else 1),
            [act],
            [here, *got, saved[4], gain, x, last_x, cot, cot if other is None else other],
            "back_out",
        )

    def parts(cot):
        return call(
            functools.partial(parts_kernel, n, piece),
            [((head, rows), BF16)] * n,
            [here, cot, *base],
            "parts",
        )

    def assemble(parts):
        return call(functools.partial(assemble_kernel, n), [wide], [here, *parts], "assemble")

    def run_head(h, flip):
        return call(
            functools.partial(head_kernel, n, flip),
            [wide, ((vocab, rows), F32), ((8, rows), F32), ((n * message[0][0], rows), BF16)],
            [here, h, fgain, table, turned, targets],
            "head",
            4 * full * rows * vocab,
        )

    def recompute(bs, tick):
        return call(
            functools.partial(recompute_kernel, n, tick),
            [
                ((3, head, rows), BF16),
                ((rows, head), BF16),
                ((rows, rows), F32),
                ((rows, rows), BF16),
                ((8, rows), F32),
            ],
            [here, *bs, *(base if tick > 0 else []), gain, wq],
            "recompute",
            work,
            whole_x,
        )

    messages = call(
        functools.partial(forward_parts_kernel, n, piece),
        [((2 * head, rows), BF16)] * n,
        [here, *after(base, found), gain, wq, cots],
        "forward",
        work,
        whole_x,
    )
    looked = to_chips(found, 0, last)
    got0 = swap(messages)
    y0, _, _ = layer_out(acts, got0, acts)
    y0_even = hop(y0, [(last, last - 1)])
    saved0 = recompute(share(after(held0, y0)), 0)
    terms0 = back(got0, saved0)

    acts1 = call(
        functools.partial(enter_kernel, 0, emb_scale),
        [act],
        [here, hop(y0, up), *looked],
        "enter",
    )
    a1 = call(
        functools.partial(forward_kernel, n, piece),
        [((head, rows), BF16)],
        [here, *after(share(acts1), terms0[0]), gain, wq],
        "forward",
        work,
        whole_x,
    )
    y1, h_send, h_own = layer_out(acts1, share(a1), y0_even)

    gin0 = back_out(swap(after(terms0, y1)), saved0, held0, held0, cots)
    saved1 = recompute(share(after(held1, y1)), 1)
    cots1 = hop(gin0, down)
    h_mine = after(from_chip(h_own, h_send, last), gin0, saved1[1])
    h_mine = assemble(share(h_mine))
    h_other = other_core(h_mine)

    normed_a, raw_a, scale_a, terms_a = run_head(h_mine, 0)
    normed_b, raw_b, scale_b, terms_b = run_head(h_other, 1)
    y1_up = hop(after(y1, h_mine), up)
    parts1 = swap(parts(after(cots1, raw_b)))
    acts2 = call(
        functools.partial(enter_kernel, 1, emb_scale),
        [act],
        [here, y1_up, *looked],
        "enter",
    )
    terms = call(
        pair_terms_kernel,
        [message] * n,
        [here, after(terms_a, acts2), other_core(terms_b)],
        "pair_terms",
    )
    gin1 = back_out(
        swap(back(after(parts1, terms), saved1)), saved1, held1, acts, cots1
    )
    total = call(sum_kernel, [message], [here, *swap(terms)], "sum")
    g_send, g_own = call(pick_kernel, [act] * 2, [here, gin0, hop(gin1, [(0, 1)])], "pick")
    total = to_chips(total, last - 1, last)
    total = call(sum_kernel, [message], [here, *after(total, g_own)], "sum")

    def cot_of(tick, total, scale, h):
        return call(
            functools.partial(cot_kernel, tick, full),
            [act, ((8, rows), F32)],
            [here, total, scale, h, fgain, *looked],
            "cot",
        )

    cot0, sums0 = cot_of(0, hop(total, [(last - 1, last)]), scale_b, y0)

    late_parts = parts(cot0)
    late_terms = back(swap(late_parts, [last]), saved1)
    leaving_a = assemble(share(after(from_chip(g_own, g_send, 0), late_parts[0])))
    leaving_b = other_core(leaving_a)
    cot1, sums1 = cot_of(1, after(total, late_parts[0]), scale_a, y1)
    sums = jnp.concatenate([sums0, sums1], axis=0)
    for part in along_chips(sums, last):
        sums = sums + part
    late_terms = after(swap(late_terms, [last]), leaving_a, sums)
    late = back_out(late_terms, saved1, held1, acts, cot0, gin1)
    late_down = hop(late, down)
    sums = after(sums, late)
    sums = sums + hop(sums, across(last))
    grad, losses = call(
        functools.partial(grad_kernel, ticks, emb_scale),
        [((vocab, full), BF16), ((8, rows), F32)],
        [
            *(here, back_ids, targets, sums),
            *(raw_a, normed_a, leaving_a),
            *(raw_b, normed_b, leaving_b),
        ],
        "grad",
        8 * full * rows * vocab,
    )
    cots2 = call(last_cots_kernel, [act], [here, late_down, cot1], "last_cots")
    return (acts2.T[None], cots2.T[None], grad, losses[:ticks, 0])


def solution(mesh):
    return jax.shard_map(
        body,
        mesh=mesh,
        in_specs=(
            P("section", None, "tensor"),
            P("section", None, "tensor"),
            P(None, "section", None, "tensor"),
            P("section", None, None, "tensor", None),
            P("section", "tensor", None, None),
            P("section", None),
            P(),
            P(("section", "tensor"), None),
            P(),
            P(),
            P(),
        ),
        out_specs=(
            P("section", None, "tensor"),
            P("section", None, "tensor"),
            P(("section", "tensor"), None),
            P(),
        ),
        check_vma=False,
    )
```

time: 580 us -> 209 us (0.36)
  waiting for transfers between devices: 314 us -> 62.7 us
  blocking collectives: 142 us -> 0 us
  starting transfers between devices: 15.2 us -> 100 us
  matrix products: 41.2 us -> 0 us
  Pallas kernels: 0 us -> 36.9 us
  other arithmetic: 33.5 us -> 0.31 us
  between operations: 17.8 us -> 1.37 us
    psum x4 -> x0, waiting for transfers between devices: 213 us -> none  [the longest x1 112 us: reduce_lookup(): summed = lax.psum(parts, ('section', 'tensor'))]
    reduce_scatter x6 -> x0, waiting for transfers between devices: 101 us -> none  [sum_width(): lax.psum_scatter(term.astype(jnp.bfloat16), 'tensor', scatter_dimension=1...]
    all_gather x10 -> x0, blocking collectives: 90 us -> none  [widen(): lax.all_gather(for_sending(values), 'tensor', axis=1, tiled=True)]
    ppermute x4 -> x72, starting transfers between devices: 14.7 us -> 100 us  [the longest x27 44.9 us: hop(): return lax.ppermute(x, 'section', pairs)]
    ppermute x4 -> x72, waiting for transfers between devices: 0.01 us -> 62.7 us  [the longest x39 38.9 us: swap(): lax.ppermute(blocks[d], 'tensor', [(i, i ^ d) for i in range(n)])]
    psum x5 -> x0, blocking collectives: 51.8 us -> none  [the longest x2 29.2 us: sum_section(): lax.psum(for_sending(values), 'section')]
    dot_general x32 -> x0, matrix products: 41.2 us -> none  [the longest x4 5.66 us: attend(): jnp.einsum('rd,dchk->chrk', normed, weights, preferred_element_type=jnp.f...]
    pallas_call x0 -> x31, Pallas kernels: none -> 36.9 us  [call(): pl.pallas_call(body, out_shape=[jax.ShapeDtypeStruct(s, d) for s, d in ou...]
  transfers between devices with their start and end apart: 14 -> 72, of which waited for: 9 -> 27; matrix products, arithmetic and copies ran while one was open for 8% -> 0% of each run, Pallas kernels for 0% -> 11%
where the time goes in v2:
time: 209 us; the launch traced here: 208 us
  starting transfers between devices  100 us (48%)
  waiting for transfers between devices  62.7 us (30%)
  Pallas kernels  36.9 us (18%)
  local copies, waits for them, and re-layouts  6.68 us (3%)
    ppermute x27, starting transfers between devices, hop(): return lax.ppermute(x, 'section', pairs)  44.9 us
    ppermute x39, waiting for transfers between devices, swap(): lax.ppermute(blocks[d], 'tensor', [(i, i ^ d) for i in range(n)])  38.9 us
    ppermute x39, starting transfers between devices, swap(): lax.ppermute(blocks[d], 'tensor', [(i, i ^ d) for i in range(n)])  38.4 us
    pallas_call x31, Pallas kernels, call(): pl.pallas_call(body, out_shape=[jax.ShapeDtypeStruct(s, d) for s, d in ou...  36.9 us
    ppermute x27, waiting for transfers between devices, hop(): return lax.ppermute(x, 'section', pairs)  19.9 us
    ppermute x6, starting transfers between devices, swap(): out.append(lax.ppermute(blocks[d], ('section', 'tensor'), pairs))  16.7 us
    unnamed x27, local copies, waits for them, and re-layouts  5.33 us
  transfers between devices with their start and end apart: 72, of which 27 were waited for; matrix products, arithmetic and copies ran while one was open for 0% of the time, Pallas kernels for 11%

profile of v2, /device:TPU:29, one launch (start us, length us, event | category | flops | bytes accessed | tf_op | source)
XLA Modules:
  0.0 208.0 jit_solution(16057049488531964325)
XLA Ops:
  7.8 2.0 lookup.1
  10.5 2.5 %collective-permute-done.3.got_ref = bf16[2304,256]{1,0:T(8,128)(2,1)S(1)} collective-permute-done((bf16[2304,256]{1,0:T(8,128)(2,1)S(1)}, bf16[2304,256]{1,0:T(8,128)(2,1)S(1)}, u32[]{:S(2)}, u32[]{:S(2)}) %collective-permute-start.3) | collective-permute-done | bytes 1179680 | tf_op jit(solution)/shard_map/ppermute | solution.py:367
  18.0 5.1 %collective-permute-done.6 = bf16[576,256]{1,0:T(8,128)(2,1)S(1)} collective-permute-done((bf16[576,256]{1,0:T(8,128)(2,1)S(1)}, bf16[576,256]{1,0:T(8,128)(2,1)S(1)}, u32[]{:S(2)}, u32[]{:S(2)}) %collective-permute-start.6) | collective-permute-done | bytes 294944 | tf_op jit(solution)/shard_map/ppermute | solution.py:374
  24.2 5.8 %collective-permute-done.5 = bf16[576,256]{1,0:T(8,128)(2,1)S(1)} collective-permute-done((bf16[576,256]{1,0:T(8,128)(2,1)S(1)}, bf16[576,256]{1,0:T(8,128)(2,1)S(1)}, u32[]{:S(2)}, u32[]{:S(2)}) %collective-permute-start.5) | collective-permute-done | bytes 294944 | tf_op jit(solution)/shard_map/ppermute | solution.py:374
  30.2 4.5 %collective-permute-done.refs_1_.refs_5_ = bf16[1152,128]{1,0:T(8,128)(2,1)S(1)} collective-permute-done((bf16[1152,128]{1,0:T(8,128)(2,1)S(1)}, bf16[1152,128]{1,0:T(8,128)(2,1)S(1)}, u32[]{:S(2)}, u32[]{:S(2)}) %collective-permute-start) | collective-permute-done | bytes 294944 | tf_op jit(solution)/shard_map/ppermute | solution.py:374
  34.8 2.3 %collective-permute-done.1.refs_2_.refs_6_ = bf16[1152,128]{1,0:T(8,128)(2,1)S(1)} collective-permute-done((bf16[1152,128]{1,0:T(8,128)(2,1)S(1)}, bf16[1152,128]{1,0:T(8,128)(2,1)S(1)}, u32[]{:S(2)}, u32[]{:S(2)}) %collective-permute-start.1) | collective-permute-done | bytes 294944 | tf_op jit(solution)/shard_map/ppermute | solution.py:374
  37.0 5.0 %collective-permute-done.2.refs_3_.refs_7_ = bf16[1152,128]{1,0:T(8,128)(2,1)S(1)} collective-permute-done((bf16[1152,128]{1,0:T(8,128)(2,1)S(1)}, bf16[1152,128]{1,0:T(8,128)(2,1)S(1)}, u32[]{:S(2)}, u32[]{:S(2)}) %collective-permute-start.2) | collective-permute-done | bytes 294944 | tf_op jit(solution)/shard_map/ppermute | solution.py:374
  42.0 2.0 forward.2
  46.8 1.3 collective-permute-start.11
  48.1 1.3 collective-permute-start.12
  49.4 1.3 collective-permute-start.13
  50.7 1.6 layer_out.2
  52.3 1.3 collective-permute-start.10
  53.6 1.3 collective-permute-start.18
  54.9 3.0 %collective-permute-done.10.y_ref = bf16[576,128]{1,0:T(8,128)(2,1)S(1)} collective-permute-done((bf16[576,128]{1,0:T(8,128)(2,1)S(1)}, bf16[576,128]{1,0:T(8,128)(2,1)S(1)}, u32[]{:S(2)}, u32[]{:S(2)}) %collective-permute-start.10) | collective-permute-done | bytes 147488 | tf_op jit(solution)/shard_map/ppermute | solution.py:367
  58.1 2.3 %collective-permute-start.20 = (bf16[576,128]{1,0:T(8,128)(2,1)S(1)}, bf16[576,128]{1,0:T(8,128)(2,1)S(1)}, u32[]{:S(2)}, u32[]{:S(2)}) collective-permute-start(bf16[576,128]{1,0:T(8,128)(2,1)S(1)} %get-tuple-element.130.refs_0_.refs_6_.refs_7_), channel_id=1, source_target_pairs={{0,3},{1,2},{2,1},{3,0},{4,7},{5,6},{6,5},{7,4},{8,11},{9,10},{10,... | collective-permute-start | bytes 442376 | tf_op jit(solution)/shard_map/ppermute | solution.py:374
  60.3 2.0 collective-permute-done.13.refs_3_
  65.7 9.9 %collective-permute-start.14 = (bf16[576,128]{1,0:T(8,128)(2,1)S(1)}, bf16[576,128]{1,0:T(8,128)(2,1)S(1)}, u32[]{:S(2)}, u32[]{:S(2)}) collective-permute-start(bf16[576,128]{1,0:T(8,128)(2,1)S(1)} %get-tuple-element.129.h_ref), channel_id=1, source_target_pairs={{28,24},{29,25},{30,26},{31,27}} | collective-permute-start | bytes 442376 | tf_op jit(solution)/shard_map/ppermute | solution.py:367
  75.6 1.6 recompute.2
  77.3 1.5 back.3
  78.8 1.8 forward.3.refs_0_
  81.3 2.0 collective-permute-start.23
  88.5 1.3 collective-permute-start.26
  89.8 1.3 collective-permute-start.25
  91.1 1.5 collective-permute-start.24
  95.0 1.8 recompute.3
  98.3 5.1 %collective-permute-done.29.refs_3_ = bf16[592,128]{1,0:T(8,128)(2,1)S(1)} collective-permute-done((bf16[592,128]{1,0:T(8,128)(2,1)S(1)}, bf16[592,128]{1,0:T(8,128)(2,1)S(1)}, u32[]{:S(2)}, u32[]{:S(2)}) %collective-permute-start.29) | collective-permute-done | bytes 151584 | tf_op jit(solution)/shard_map/ppermute | solution.py:374
  104.9 2.0 collective-permute-start.35
  106.9 1.3 collective-permute-done.33.refs_1_
  108.6 1.6 collective-permute-done.35.refs_3_
  110.8 5.3 %collective-permute-start.37 = (bf16[2304,128]{1,0:T(8,128)(2,1)S(1)}, bf16[2304,128]{1,0:T(8,128)(2,1)S(1)}, u32[]{:S(2)}, u32[]{:S(2)}) collective-permute-start(bf16[2304,128]{1,0:T(8,128)(2,1)S(1)} %assemble.2.h_ref), channel_id=1, source_target_pairs={{0,4},{4,0},{8,12},{12,8},{16,20},{20,16},{24,28},{28,24},{1,5},{5... | collective-permute-start | bytes 1769480 | tf_op jit(solution)/shard_map/ppermute | solution.py:367
  116.1 1.6 collective-permute-done.37.h_ref
  117.8 1.8 head.3
  121.3 3.0 %collective-permute-start.45 = (bf16[576,128]{1,0:T(8,128)(2,1)S(1)}, bf16[576,128]{1,0:T(8,128)(2,1)S(1)}, u32[]{:S(2)}, u32[]{:S(2)}) collective-permute-start(bf16[576,128]{1,0:T(8,128)(2,1)S(1)} %back_out.3.even_ref), channel_id=1, source_target_pairs={{4,0},{8,4},{12,8},{16,12},{20,16},{24,20},{28,24},{5,1},{9,5},{13... | collective-permute-start | bytes 442376 | tf_op jit(solution)/shard_map/ppermute | solution.py:367
  124.3 1.8 head.2
  126.2 1.3 enter.3
  129.4 1.3 collective-permute-start.46
  133.1 1.6 collective-permute-start.41
  135.8 1.5 back.4
  137.9 2.1 %collective-permute-start.51 = (bf16[592,128]{1,0:T(8,128)(2,1)S(1)}, bf16[592,128]{1,0:T(8,128)(2,1)S(1)}, u32[]{:S(2)}, u32[]{:S(2)}) collective-permute-start(bf16[592,128]{1,0:T(8,128)(2,1)S(1)} %get-tuple-element.180), channel_id=1, source_target_pairs={{0,3},{1,2},{2,1},{3,0},{4,7},{5,6},{6,5},{7,4},{8,11},{9,10},{10,... | collective-permute-start | bytes 454664 | tf_op jit(solution)/shard_map/ppermute | solution.py:374
  140.6 1.3 collective-permute-start.42
  142.7 3.4 %collective-permute-done.50.refs_2_ = bf16[592,128]{1,0:T(8,128)(2,1)S(1)} collective-permute-done((bf16[592,128]{1,0:T(8,128)(2,1)S(1)}, bf16[592,128]{1,0:T(8,128)(2,1)S(1)}, u32[]{:S(2)}, u32[]{:S(2)}) %collective-permute-start.50) | collective-permute-done | bytes 151584 | tf_op jit(solution)/shard_map/ppermute | solution.py:374
  147.5 1.3 collective-permute-start.43
  148.8 1.3 collective-permute-start.44
  150.7 1.3 collective-permute-start.62
  153.4 1.4 collective-permute-done.43.refs_2_
  154.8 1.8 collective-permute-done.44.refs_3_
  157.2 1.3 collective-permute-start.53
  158.7 6.6 %collective-permute-done.53.total_ref = bf16[592,128]{1,0:T(8,128)(2,1)S(1)} collective-permute-done((bf16[592,128]{1,0:T(8,128)(2,1)S(1)}, bf16[592,128]{1,0:T(8,128)(2,1)S(1)}, u32[]{:S(2)}, u32[]{:S(2)}) %collective-permute-start.53) | collective-permute-done | bytes 151584 | tf_op jit(solution)/shard_map/ppermute | solution.py:367
  167.9 2.5 %collective-permute-start.64 = (bf16[576,128]{1,0:T(8,128)(2,1)S(1)}, bf16[576,128]{1,0:T(8,128)(2,1)S(1)}, u32[]{:S(2)}, u32[]{:S(2)}) collective-permute-start(bf16[576,128]{1,0:T(8,128)(2,1)S(1)} %add_add_fusion.refs_0_), channel_id=1, source_target_pairs={{0,2},{1,3},{2,0},{3,1},{4,6},{5,7},{6,4},{7,5},{8,10},{9,11},{10,... | collective-permute-start | bytes 442376 | tf_op jit(solution)/shard_map/ppermute | solution.py:374
  171.3 2.2 %collective-permute-start.54 = (bf16[128,128]{1,0:T(8,128)(2,1)S(1)}, bf16[128,128]{1,0:T(8,128)(2,1)S(1)}, u32[]{:S(2)}, u32[]{:S(2)}) collective-permute-start(bf16[128,128]{1,0:T(8,128)(2,1)S(1)} %get-tuple-element.190), channel_id=1, source_target_pairs={{28,29},{29,28},{30,31},{31,30}} | collective-permute-start | bytes 98312 | tf_op jit(solution)/shard_map/ppermute | solution.py:380
  173.5 3.3 %collective-permute-start.55 = (bf16[128,128]{1,0:T(8,128)(2,1)S(1)}, bf16[128,128]{1,0:T(8,128)(2,1)S(1)}, u32[]{:S(2)}, u32[]{:S(2)}) collective-permute-start(bf16[128,128]{1,0:T(8,128)(2,1)S(1)} %get-tuple-element.191), channel_id=1, source_target_pairs={{28,30},{29,31},{30,28},{31,29}} | collective-permute-start | bytes 98312 | tf_op jit(solution)/shard_map/ppermute | solution.py:380
  177.6 2.8 %collective-permute-start.56 = (bf16[128,128]{1,0:T(8,128)(2,1)S(1)}, bf16[128,128]{1,0:T(8,128)(2,1)S(1)}, u32[]{:S(2)}, u32[]{:S(2)}) collective-permute-start(bf16[128,128]{1,0:T(8,128)(2,1)S(1)} %get-tuple-element.192), channel_id=1, source_target_pairs={{28,31},{29,30},{30,29},{31,28}} | collective-permute-start | bytes 98312 | tf_op jit(solution)/shard_map/ppermute | solution.py:380
  181.2 1.3 collective-permute-start.68
  182.5 1.3 collective-permute-start.67
  183.8 1.3 collective-permute-start.66
  185.1 1.5 back.5
  186.6 2.2 %collective-permute-start.57 = (bf16[592,128]{1,0:T(8,128)(2,1)S(1)}, bf16[592,128]{1,0:T(8,128)(2,1)S(1)}, u32[]{:S(2)}, u32[]{:S(2)}) collective-permute-start(bf16[592,128]{1,0:T(8,128)(2,1)S(1)} %get-tuple-element.194), channel_id=1, source_target_pairs={{28,29},{29,28},{30,31},{31,30}} | collective-permute-start | bytes 454664 | tf_op jit(solution)/shard_map/ppermute | solution.py:380
  188.8 3.3 %collective-permute-start.58 = (bf16[592,128]{1,0:T(8,128)(2,1)S(1)}, bf16[592,128]{1,0:T(8,128)(2,1)S(1)}, u32[]{:S(2)}, u32[]{:S(2)}) collective-permute-start(bf16[592,128]{1,0:T(8,128)(2,1)S(1)} %get-tuple-element.195), channel_id=1, source_target_pairs={{28,30},{29,31},{30,28},{31,29}} | collective-permute-start | bytes 454664 | tf_op jit(solution)/shard_map/ppermute | solution.py:380
  192.2 2.8 %collective-permute-start.59 = (bf16[592,128]{1,0:T(8,128)(2,1)S(1)}, bf16[592,128]{1,0:T(8,128)(2,1)S(1)}, u32[]{:S(2)}, u32[]{:S(2)}) collective-permute-start(bf16[592,128]{1,0:T(8,128)(2,1)S(1)} %get-tuple-element.196), channel_id=1, source_target_pairs={{28,31},{29,30},{30,29},{31,28}} | collective-permute-start | bytes 454664 | tf_op jit(solution)/shard_map/ppermute | solution.py:380
  195.1 3.9 %collective-permute-done.59.refs_3_ = bf16[592,128]{1,0:T(8,128)(2,1)S(1)} collective-permute-done((bf16[592,128]{1,0:T(8,128)(2,1)S(1)}, bf16[592,128]{1,0:T(8,128)(2,1)S(1)}, u32[]{:S(2)}, u32[]{:S(2)}) %collective-permute-start.59) | collective-permute-done | bytes 151584 | tf_op jit(solution)/shard_map/ppermute | solution.py:380
  199.7 1.3 collective-permute-start.69
  201.0 1.3 collective-permute-start.70
  204.4 3.0 %grad.1 = (bf16[256,2304]{1,0:T(8,128)(2,1)}, f32[8,128]{1,0:T(8,128)S(1)}) custom-call(s32[4]{0:T(128)S(1)} %pad_add_fusion.here, s32[2,128]{1,0:T(2,128)S(1)} %copy-done.10, s32[2,128]{1,0:T(2,128)S(1)} %copy-done.8, f32[16,128]{1,0:T(8,128)S(1)} %add.55.sums_ref, f32[256,128]{1,0:T(8,128)S(1)} %get-tuple-element.209.refs_0_, ...), custom_call_target="tpu_custom_call" | custom-call | flops 603979776 | bytes 3815440 | tf_op jit(solution)/shard_map/grad/pallas_call | solution.py:27
  (148 shorter events, 54.3 us)
Async XLA Ops:
  13.8 9.2 %collective-permute-start.6 = (bf16[576,256]{1,0:T(8,128)(2,1)S(1)}, bf16[576,256]{1,0:T(8,128)(2,1)S(1)}, u32[]{:S(2)}, u32[]{:S(2)}) collective-permute-start(bf16[576,256]{1,0:T(8,128)(2,1)S(1)} %get-tuple-element.120), channel_id=1, source_target_pairs={{0,3},{1,2},{2,1},{3,0},{4,7},{5,6},{6,5},{7,4},{8,11},{9,10},{10,... | collective-permute-start | bytes 884744 | tf_op jit(solution)/shard_map/ppermute | solution.py:374
  15.1 15.0 %collective-permute-start.5 = (bf16[576,256]{1,0:T(8,128)(2,1)S(1)}, bf16[576,256]{1,0:T(8,128)(2,1)S(1)}, u32[]{:S(2)}, u32[]{:S(2)}) collective-permute-start(bf16[576,256]{1,0:T(8,128)(2,1)S(1)} %get-tuple-element.119), channel_id=1, source_target_pairs={{0,2},{1,3},{2,0},{3,1},{4,6},{5,7},{6,4},{7,5},{8,10},{9,11},{10,... | collective-permute-start | bytes 884744 | tf_op jit(solution)/shard_map/ppermute | solution.py:374
  16.3 13.8 %collective-permute-start.4 = (bf16[576,256]{1,0:T(8,128)(2,1)S(1)}, bf16[576,256]{1,0:T(8,128)(2,1)S(1)}, u32[]{:S(2)}, u32[]{:S(2)}) collective-permute-start(bf16[576,256]{1,0:T(8,128)(2,1)S(1)} %get-tuple-element.118), channel_id=1, source_target_pairs={{0,1},{1,0},{2,3},{3,2},{4,5},{5,4},{6,7},{7,6},{8,9},{9,8},{10,11... | collective-permute-start | bytes 884744 | tf_op jit(solution)/shard_map/ppermute | solution.py:374
  16.6 18.2 %collective-permute-start = (bf16[1152,128]{1,0:T(8,128)(2,1)S(1)}, bf16[1152,128]{1,0:T(8,128)(2,1)S(1)}, u32[]{:S(2)}, u32[]{:S(2)}) collective-permute-start(bf16[1152,128]{1,0:T(8,128)(2,1)S(1)} %get-tuple-element.110), channel_id=1, source_target_pairs={{0,1},{1,0},{2,3},{3,2},{4,5},{5,4},{6,7},{7,6},{8,9},{9,8},{10,11... | collective-permute-start | bytes 884744 | tf_op jit(solution)/shard_map/ppermute | solution.py:374
  17.8 19.3 %collective-permute-start.1 = (bf16[1152,128]{1,0:T(8,128)(2,1)S(1)}, bf16[1152,128]{1,0:T(8,128)(2,1)S(1)}, u32[]{:S(2)}, u32[]{:S(2)}) collective-permute-start(bf16[1152,128]{1,0:T(8,128)(2,1)S(1)} %get-tuple-element.111), channel_id=1, source_target_pairs={{0,2},{1,3},{2,0},{3,1},{4,6},{5,7},{6,4},{7,5},{8,10},{9,11},{10,... | collective-permute-start | bytes 884744 | tf_op jit(solution)/shard_map/ppermute | solution.py:374
  23.1 19.0 %collective-permute-start.2 = (bf16[1152,128]{1,0:T(8,128)(2,1)S(1)}, bf16[1152,128]{1,0:T(8,128)(2,1)S(1)}, u32[]{:S(2)}, u32[]{:S(2)}) collective-permute-start(bf16[1152,128]{1,0:T(8,128)(2,1)S(1)} %get-tuple-element.112), channel_id=1, source_target_pairs={{0,3},{1,2},{2,1},{3,0},{4,7},{5,6},{6,5},{7,4},{8,11},{9,10},{10,... | collective-permute-start | bytes 884744 | tf_op jit(solution)/shard_map/ppermute | solution.py:374
  44.1 5.3 %collective-permute-start.7 = (bf16[256,128]{1,0:T(8,128)(2,1)S(1)}, bf16[256,128]{1,0:T(8,128)(2,1)S(1)}, u32[]{:S(2)}, u32[]{:S(2)}) collective-permute-start(bf16[256,128]{1,0:T(8,128)(2,1)S(1)} %get-tuple-element.126), channel_id=1, source_target_pairs={{0,1},{1,0},{2,3},{3,2},{4,5},{5,4},{6,7},{7,6},{8,9},{9,8},{10,11... | collective-permute-start | bytes 196616 | tf_op jit(solution)/shard_map/ppermute | solution.py:374
  45.3 5.3 %collective-permute-start.8 = (bf16[256,128]{1,0:T(8,128)(2,1)S(1)}, bf16[256,128]{1,0:T(8,128)(2,1)S(1)}, u32[]{:S(2)}, u32[]{:S(2)}) collective-permute-start(bf16[256,128]{1,0:T(8,128)(2,1)S(1)} %get-tuple-element.127), channel_id=1, source_target_pairs={{0,2},{1,3},{2,0},{3,1},{4,6},{5,7},{6,4},{7,5},{8,10},{9,11},{10,... | collective-permute-start | bytes 196616 | tf_op jit(solution)/shard_map/ppermute | solution.py:374
  45.6 5.1 %collective-permute-start.9 = (bf16[256,128]{1,0:T(8,128)(2,1)S(1)}, bf16[256,128]{1,0:T(8,128)(2,1)S(1)}, u32[]{:S(2)}, u32[]{:S(2)}) collective-permute-start(bf16[256,128]{1,0:T(8,128)(2,1)S(1)} %get-tuple-element.128), channel_id=1, source_target_pairs={{0,3},{1,2},{2,1},{3,0},{4,7},{5,6},{6,5},{7,4},{8,11},{9,10},{10,... | collective-permute-start | bytes 196616 | tf_op jit(solution)/shard_map/ppermute | solution.py:374
  46.8 11.3 %collective-permute-start.11 = (bf16[576,256]{1,0:T(8,128)(2,1)S(1)}, bf16[576,256]{1,0:T(8,128)(2,1)S(1)}, u32[]{:S(2)}, u32[]{:S(2)}) collective-permute-start(bf16[576,256]{1,0:T(8,128)(2,1)S(1)} %add_convert_fusion.refs_0_), channel_id=1, source_target_pairs={{8,0},{4,28},{9,1},{5,29},{10,2},{6,30},{11,3},{7,31}} | collective-permute-start | bytes 884744 | tf_op jit(solution)/shard_map/ppermute | solution.py:367
  48.1 12.3 %collective-permute-start.12 = (bf16[576,256]{1,0:T(8,128)(2,1)S(1)}, bf16[576,256]{1,0:T(8,128)(2,1)S(1)}, u32[]{:S(2)}, u32[]{:S(2)}) collective-permute-start(bf16[576,256]{1,0:T(8,128)(2,1)S(1)} %add_convert_fusion.refs_0_), channel_id=1, source_target_pairs={{16,0},{12,28},{17,1},{13,29},{18,2},{14,30},{19,3},{15,31}} | collective-permute-start | bytes 884744 | tf_op jit(solution)/shard_map/ppermute | solution.py:367
  49.4 13.0 %collective-permute-start.13 = (bf16[576,256]{1,0:T(8,128)(2,1)S(1)}, bf16[576,256]{1,0:T(8,128)(2,1)S(1)}, u32[]{:S(2)}, u32[]{:S(2)}) collective-permute-start(bf16[576,256]{1,0:T(8,128)(2,1)S(1)} %add_convert_fusion.refs_0_), channel_id=1, source_target_pairs={{24,0},{20,28},{25,1},{21,29},{26,2},{22,30},{27,3},{23,31}} | collective-permute-start | bytes 884744 | tf_op jit(solution)/shard_map/ppermute | solution.py:367
  52.3 5.7 %collective-permute-start.10 = (bf16[576,128]{1,0:T(8,128)(2,1)S(1)}, bf16[576,128]{1,0:T(8,128)(2,1)S(1)}, u32[]{:S(2)}, u32[]{:S(2)}) collective-permute-start(bf16[576,128]{1,0:T(8,128)(2,1)S(1)} %get-tuple-element.129.h_ref), channel_id=1, source_target_pairs={{0,4},{4,8},{8,12},{12,16},{16,20},{20,24},{24,28},{1,5},{5,9},{9,... | collective-permute-start | bytes 442376 | tf_op jit(solution)/shard_map/ppermute | solution.py:367
  53.6 10.9 %collective-permute-start.18 = (bf16[576,128]{1,0:T(8,128)(2,1)S(1)}, bf16[576,128]{1,0:T(8,128)(2,1)S(1)}, u32[]{:S(2)}, u32[]{:S(2)}) collective-permute-start(bf16[576,128]{1,0:T(8,128)(2,1)S(1)} %get-tuple-element.130.refs_0_.refs_6_.refs_7_), channel_id=1, source_target_pairs={{0,1},{1,0},{2,3},{3,2},{4,5},{5,4},{6,7},{7,6},{8,9},{9,8},{10,11... | collective-permute-start | bytes 442376 | tf_op jit(solution)/shard_map/ppermute | solution.py:374
  57.9 7.8 %collective-permute-start.19 = (bf16[576,128]{1,0:T(8,128)(2,1)S(1)}, bf16[576,128]{1,0:T(8,128)(2,1)S(1)}, u32[]{:S(2)}, u32[]{:S(2)}) collective-permute-start(bf16[576,128]{1,0:T(8,128)(2,1)S(1)} %get-tuple-element.130.refs_0_.refs_6_.refs_7_), channel_id=1, source_target_pairs={{0,2},{1,3},{2,0},{3,1},{4,6},{5,7},{6,4},{7,5},{8,10},{9,11},{10,... | collective-permute-start | bytes 442376 | tf_op jit(solution)/shard_map/ppermute | solution.py:374
  58.1 17.6 %collective-permute-start.20 = (bf16[576,128]{1,0:T(8,128)(2,1)S(1)}, bf16[576,128]{1,0:T(8,128)(2,1)S(1)}, u32[]{:S(2)}, u32[]{:S(2)}) collective-permute-start(bf16[576,128]{1,0:T(8,128)(2,1)S(1)} %get-tuple-element.130.refs_0_.refs_6_.refs_7_), channel_id=1, source_target_pairs={{0,3},{1,2},{2,1},{3,0},{4,7},{5,6},{6,5},{7,4},{8,11},{9,10},{10,... | collective-permute-start | bytes 442376 | tf_op jit(solution)/shard_map/ppermute | solution.py:374
  63.0 15.8 %collective-permute-start.15 = (bf16[576,128]{1,0:T(8,128)(2,1)S(1)}, bf16[576,128]{1,0:T(8,128)(2,1)S(1)}, u32[]{:S(2)}, u32[]{:S(2)}) collective-permute-start(bf16[576,128]{1,0:T(8,128)(2,1)S(1)} %enter.2.refs_0_.x_ref), channel_id=1, source_target_pairs={{0,1},{1,0},{2,3},{3,2},{4,5},{5,4},{6,7},{7,6},{8,9},{9,8},{10,11... | collective-permute-start | bytes 442376 | tf_op jit(solution)/shard_map/ppermute | solution.py:374
  64.3 14.5 %collective-permute-start.16 = (bf16[576,128]{1,0:T(8,128)(2,1)S(1)}, bf16[576,128]{1,0:T(8,128)(2,1)S(1)}, u32[]{:S(2)}, u32[]{:S(2)}) collective-permute-start(bf16[576,128]{1,0:T(8,128)(2,1)S(1)} %enter.2.refs_0_.x_ref), channel_id=1, source_target_pairs={{0,2},{1,3},{2,0},{3,1},{4,6},{5,7},{6,4},{7,5},{8,10},{9,11},{10,... | collective-permute-start | bytes 442376 | tf_op jit(solution)/shard_map/ppermute | solution.py:374
  64.5 14.3 %collective-permute-start.17 = (bf16[576,128]{1,0:T(8,128)(2,1)S(1)}, bf16[576,128]{1,0:T(8,128)(2,1)S(1)}, u32[]{:S(2)}, u32[]{:S(2)}) collective-permute-start(bf16[576,128]{1,0:T(8,128)(2,1)S(1)} %enter.2.refs_0_.x_ref), channel_id=1, source_target_pairs={{0,3},{1,2},{2,1},{3,0},{4,7},{5,6},{6,5},{7,4},{8,11},{9,10},{10,... | collective-permute-start | bytes 442376 | tf_op jit(solution)/shard_map/ppermute | solution.py:374
  65.7 17.6 %collective-permute-start.14 = (bf16[576,128]{1,0:T(8,128)(2,1)S(1)}, bf16[576,128]{1,0:T(8,128)(2,1)S(1)}, u32[]{:S(2)}, u32[]{:S(2)}) collective-permute-start(bf16[576,128]{1,0:T(8,128)(2,1)S(1)} %get-tuple-element.129.h_ref), channel_id=1, source_target_pairs={{28,24},{29,25},{30,26},{31,27}} | collective-permute-start | bytes 442376 | tf_op jit(solution)/shard_map/ppermute | solution.py:367
  85.8 5.3 %collective-permute-start.30 = (bf16[576,128]{1,0:T(8,128)(2,1)S(1)}, bf16[576,128]{1,0:T(8,128)(2,1)S(1)}, u32[]{:S(2)}, u32[]{:S(2)}) collective-permute-start(bf16[576,128]{1,0:T(8,128)(2,1)S(1)} %get-tuple-element.151.refs_0_.refs_6_), channel_id=1, source_target_pairs={{0,1},{1,0},{2,3},{3,2},{4,5},{5,4},{6,7},{7,6},{8,9},{9,8},{10,11... | collective-permute-start | bytes 442376 | tf_op jit(solution)/shard_map/ppermute | solution.py:374
  86.9 5.7 %collective-permute-start.31 = (bf16[576,128]{1,0:T(8,128)(2,1)S(1)}, bf16[576,128]{1,0:T(8,128)(2,1)S(1)}, u32[]{:S(2)}, u32[]{:S(2)}) collective-permute-start(bf16[576,128]{1,0:T(8,128)(2,1)S(1)} %get-tuple-element.151.refs_0_.refs_6_), channel_id=1, source_target_pairs={{0,2},{1,3},{2,0},{3,1},{4,6},{5,7},{6,4},{7,5},{8,10},{9,11},{10,... | collective-permute-start | bytes 442376 | tf_op jit(solution)/shard_map/ppermute | solution.py:374
  88.2 6.1 %collective-permute-start.32 = (bf16[576,128]{1,0:T(8,128)(2,1)S(1)}, bf16[576,128]{1,0:T(8,128)(2,1)S(1)}, u32[]{:S(2)}, u32[]{:S(2)}) collective-permute-start(bf16[576,128]{1,0:T(8,128)(2,1)S(1)} %get-tuple-element.151.refs_0_.refs_6_), channel_id=1, source_target_pairs={{0,3},{1,2},{2,1},{3,0},{4,7},{5,6},{6,5},{7,4},{8,11},{9,10},{10,... | collective-permute-start | bytes 442376 | tf_op jit(solution)/shard_map/ppermute | solution.py:374
  88.5 8.3 %collective-permute-start.26 = (bf16[576,128]{1,0:T(8,128)(2,1)S(1)}, bf16[576,128]{1,0:T(8,128)(2,1)S(1)}, u32[]{:S(2)}, u32[]{:S(2)}) collective-permute-start(bf16[576,128]{1,0:T(8,128)(2,1)S(1)} %get-tuple-element.142), channel_id=1, source_target_pairs={{28,20},{24,16},{29,21},{25,17},{30,22},{26,18},{31,23},{27,19}} | collective-permute-start | bytes 442376 | tf_op jit(solution)/shard_map/ppermute | solution.py:367
  89.8 8.2 %collective-permute-start.25 = (bf16[576,128]{1,0:T(8,128)(2,1)S(1)}, bf16[576,128]{1,0:T(8,128)(2,1)S(1)}, u32[]{:S(2)}, u32[]{:S(2)}) collective-permute-start(bf16[576,128]{1,0:T(8,128)(2,1)S(1)} %get-tuple-element.142), channel_id=1, source_target_pairs={{28,12},{24,8},{29,13},{25,9},{30,14},{26,10},{31,15},{27,11}} | collective-permute-start | bytes 442376 | tf_op jit(solution)/shard_map/ppermute | solution.py:367
  91.1 6.9 %collective-permute-start.24 = (bf16[576,128]{1,0:T(8,128)(2,1)S(1)}, bf16[576,128]{1,0:T(8,128)(2,1)S(1)}, u32[]{:S(2)}, u32[]{:S(2)}) collective-permute-start(bf16[576,128]{1,0:T(8,128)(2,1)S(1)} %get-tuple-element.142), channel_id=1, source_target_pairs={{28,4},{24,0},{29,5},{25,1},{30,6},{26,2},{31,7},{27,3}} | collective-permute-start | bytes 442376 | tf_op jit(solution)/shard_map/ppermute | solution.py:367
  92.6 5.4 %collective-permute-start.27 = (bf16[592,128]{1,0:T(8,128)(2,1)S(1)}, bf16[592,128]{1,0:T(8,128)(2,1)S(1)}, u32[]{:S(2)}, u32[]{:S(2)}) collective-permute-start(bf16[592,128]{1,0:T(8,128)(2,1)S(1)} %get-tuple-element.147), channel_id=1, source_target_pairs={{0,1},{1,0},{2,3},{3,2},{4,5},{5,4},{6,7},{7,6},{8,9},{9,8},{10,11... | collective-permute-start | bytes 454664 | tf_op jit(solution)/shard_map/ppermute | solution.py:374
  94.3 4.0 %collective-permute-start.28 = (bf16[592,128]{1,0:T(8,128)(2,1)S(1)}, bf16[592,128]{1,0:T(8,128)(2,1)S(1)}, u32[]{:S(2)}, u32[]{:S(2)}) collective-permute-start(bf16[592,128]{1,0:T(8,128)(2,1)S(1)} %get-tuple-element.148), channel_id=1, source_target_pairs={{0,2},{1,3},{2,0},{3,1},{4,6},{5,7},{6,4},{7,5},{8,10},{9,11},{10,... | collective-permute-start | bytes 454664 | tf_op jit(solution)/shard_map/ppermute | solution.py:374
  96.8 6.6 %collective-permute-start.29 = (bf16[592,128]{1,0:T(8,128)(2,1)S(1)}, bf16[592,128]{1,0:T(8,128)(2,1)S(1)}, u32[]{:S(2)}, u32[]{:S(2)}) collective-permute-start(bf16[592,128]{1,0:T(8,128)(2,1)S(1)} %get-tuple-element.149), channel_id=1, source_target_pairs={{0,3},{1,2},{2,1},{3,0},{4,7},{5,6},{6,5},{7,4},{8,11},{9,10},{10,... | collective-permute-start | bytes 454664 | tf_op jit(solution)/shard_map/ppermute | solution.py:374
  104.2 4.1 %collective-permute-start.33 = (bf16[576,128]{1,0:T(8,128)(2,1)S(1)}, bf16[576,128]{1,0:T(8,128)(2,1)S(1)}, u32[]{:S(2)}, u32[]{:S(2)}) collective-permute-start(bf16[576,128]{1,0:T(8,128)(2,1)S(1)} %add_add_fusion.1.refs_0_), channel_id=1, source_target_pairs={{0,1},{1,0},{2,3},{3,2},{4,5},{5,4},{6,7},{7,6},{8,9},{9,8},{10,11... | collective-permute-start | bytes 442376 | tf_op jit(solution)/shard_map/ppermute | solution.py:374
  104.6 4.0 %collective-permute-start.34 = (bf16[576,128]{1,0:T(8,128)(2,1)S(1)}, bf16[576,128]{1,0:T(8,128)(2,1)S(1)}, u32[]{:S(2)}, u32[]{:S(2)}) collective-permute-start(bf16[576,128]{1,0:T(8,128)(2,1)S(1)} %add_add_fusion.1.refs_0_), channel_id=1, source_target_pairs={{0,2},{1,3},{2,0},{3,1},{4,6},{5,7},{6,4},{7,5},{8,10},{9,11},{10,... | collective-permute-start | bytes 442376 | tf_op jit(solution)/shard_map/ppermute | solution.py:374
  104.9 5.3 %collective-permute-start.35 = (bf16[576,128]{1,0:T(8,128)(2,1)S(1)}, bf16[576,128]{1,0:T(8,128)(2,1)S(1)}, u32[]{:S(2)}, u32[]{:S(2)}) collective-permute-start(bf16[576,128]{1,0:T(8,128)(2,1)S(1)} %add_add_fusion.1.refs_0_), channel_id=1, source_target_pairs={{0,3},{1,2},{2,1},{3,0},{4,7},{5,6},{6,5},{7,4},{8,11},{9,10},{10,... | collective-permute-start | bytes 442376 | tf_op jit(solution)/shard_map/ppermute | solution.py:374
  110.8 6.9 %collective-permute-start.37 = (bf16[2304,128]{1,0:T(8,128)(2,1)S(1)}, bf16[2304,128]{1,0:T(8,128)(2,1)S(1)}, u32[]{:S(2)}, u32[]{:S(2)}) collective-permute-start(bf16[2304,128]{1,0:T(8,128)(2,1)S(1)} %assemble.2.h_ref), channel_id=1, source_target_pairs={{0,4},{4,0},{8,12},{12,8},{16,20},{20,16},{24,28},{28,24},{1,5},{5... | collective-permute-start | bytes 1769480 | tf_op jit(solution)/shard_map/ppermute | solution.py:367
  119.6 7.9 %collective-permute-start.38 = (bf16[2368,128]{1,0:T(8,128)(2,1)S(1)}, bf16[2368,128]{1,0:T(8,128)(2,1)S(1)}, u32[]{:S(2)}, u32[]{:S(2)}) collective-permute-start(bf16[2368,128]{1,0:T(8,128)(2,1)S(1)} %get-tuple-element.159), channel_id=1, source_target_pairs={{0,4},{4,0},{8,12},{12,8},{16,20},{20,16},{24,28},{28,24},{1,5},{5... | collective-permute-start | bytes 1818632 | tf_op jit(solution)/shard_map/ppermute | solution.py:367
  120.0 6.2 %collective-permute-start.36 = (bf16[576,128]{1,0:T(8,128)(2,1)S(1)}, bf16[576,128]{1,0:T(8,128)(2,1)S(1)}, u32[]{:S(2)}, u32[]{:S(2)}) collective-permute-start(bf16[576,128]{1,0:T(8,128)(2,1)S(1)} %get-tuple-element.154.h_ref), channel_id=1, source_target_pairs={{0,4},{4,8},{8,12},{12,16},{16,20},{20,24},{24,28},{1,5},{5,9},{9,... | collective-permute-start | bytes 442376 | tf_op jit(solution)/shard_map/ppermute | solution.py:367
  121.3 7.1 %collective-permute-start.45 = (bf16[576,128]{1,0:T(8,128)(2,1)S(1)}, bf16[576,128]{1,0:T(8,128)(2,1)S(1)}, u32[]{:S(2)}, u32[]{:S(2)}) collective-permute-start(bf16[576,128]{1,0:T(8,128)(2,1)S(1)} %back_out.3.even_ref), channel_id=1, source_target_pairs={{4,0},{8,4},{12,8},{16,12},{20,16},{24,20},{28,24},{5,1},{9,5},{13... | collective-permute-start | bytes 442376 | tf_op jit(solution)/shard_map/ppermute | solution.py:367
  128.2 9.7 %collective-permute-start.39 = (bf16[592,128]{1,0:T(8,128)(2,1)S(1)}, bf16[592,128]{1,0:T(8,128)(2,1)S(1)}, u32[]{:S(2)}, u32[]{:S(2)}) collective-permute-start(bf16[592,128]{1,0:T(8,128)(2,1)S(1)} %get-tuple-element.161), channel_id=1, source_target_pairs={{0,1},{1,0},{2,3},{3,2},{4,5},{5,4},{6,7},{7,6},{8,9},{9,8},{10,11... | collective-permute-start | bytes 454664 | tf_op jit(solution)/shard_map/ppermute | solution.py:374
  130.7 4.0 %collective-permute-start.47 = (bf16[128,128]{1,0:T(8,128)(2,1)S(1)}, bf16[128,128]{1,0:T(8,128)(2,1)S(1)}, u32[]{:S(2)}, u32[]{:S(2)}) collective-permute-start(bf16[128,128]{1,0:T(8,128)(2,1)S(1)} %get-tuple-element.168), channel_id=1, source_target_pairs={{0,2},{1,3},{2,0},{3,1},{4,6},{5,7},{6,4},{7,5},{8,10},{9,11},{10,... | collective-permute-start | bytes 98312 | tf_op jit(solution)/shard_map/ppermute | solution.py:374
  131.7 4.1 %collective-permute-start.48 = (bf16[128,128]{1,0:T(8,128)(2,1)S(1)}, bf16[128,128]{1,0:T(8,128)(2,1)S(1)}, u32[]{:S(2)}, u32[]{:S(2)}) collective-permute-start(bf16[128,128]{1,0:T(8,128)(2,1)S(1)} %get-tuple-element.169), channel_id=1, source_target_pairs={{0,3},{1,2},{2,1},{3,0},{4,7},{5,6},{6,5},{7,4},{8,11},{9,10},{10,... | collective-permute-start | bytes 98312 | tf_op jit(solution)/shard_map/ppermute | solution.py:374
  132.1 7.9 %collective-permute-start.40 = (bf16[592,128]{1,0:T(8,128)(2,1)S(1)}, bf16[592,128]{1,0:T(8,128)(2,1)S(1)}, u32[]{:S(2)}, u32[]{:S(2)}) collective-permute-start(bf16[592,128]{1,0:T(8,128)(2,1)S(1)} %get-tuple-element.162), channel_id=1, source_target_pairs={{0,2},{1,3},{2,0},{3,1},{4,6},{5,7},{6,4},{7,5},{8,10},{9,11},{10,... | collective-permute-start | bytes 454664 | tf_op jit(solution)/shard_map/ppermute | solution.py:374
  133.1 6.8 %collective-permute-start.41 = (bf16[592,128]{1,0:T(8,128)(2,1)S(1)}, bf16[592,128]{1,0:T(8,128)(2,1)S(1)}, u32[]{:S(2)}, u32[]{:S(2)}) collective-permute-start(bf16[592,128]{1,0:T(8,128)(2,1)S(1)} %get-tuple-element.163), channel_id=1, source_target_pairs={{0,3},{1,2},{2,1},{3,0},{4,7},{5,6},{6,5},{7,4},{8,11},{9,10},{10,... | collective-permute-start | bytes 454664 | tf_op jit(solution)/shard_map/ppermute | solution.py:374
  137.3 5.4 %collective-permute-start.49 = (bf16[592,128]{1,0:T(8,128)(2,1)S(1)}, bf16[592,128]{1,0:T(8,128)(2,1)S(1)}, u32[]{:S(2)}, u32[]{:S(2)}) collective-permute-start(bf16[592,128]{1,0:T(8,128)(2,1)S(1)} %get-tuple-element.178), channel_id=1, source_target_pairs={{0,1},{1,0},{2,3},{3,2},{4,5},{5,4},{6,7},{7,6},{8,9},{9,8},{10,11... | collective-permute-start | bytes 454664 | tf_op jit(solution)/shard_map/ppermute | solution.py:374
  137.3 8.8 %collective-permute-start.50 = (bf16[592,128]{1,0:T(8,128)(2,1)S(1)}, bf16[592,128]{1,0:T(8,128)(2,1)S(1)}, u32[]{:S(2)}, u32[]{:S(2)}) collective-permute-start(bf16[592,128]{1,0:T(8,128)(2,1)S(1)} %get-tuple-element.179), channel_id=1, source_target_pairs={{0,2},{1,3},{2,0},{3,1},{4,6},{5,7},{6,4},{7,5},{8,10},{9,11},{10,... | collective-permute-start | bytes 454664 | tf_op jit(solution)/shard_map/ppermute | solution.py:374
  137.9 8.2 %collective-permute-start.51 = (bf16[592,128]{1,0:T(8,128)(2,1)S(1)}, bf16[592,128]{1,0:T(8,128)(2,1)S(1)}, u32[]{:S(2)}, u32[]{:S(2)}) collective-permute-start(bf16[592,128]{1,0:T(8,128)(2,1)S(1)} %get-tuple-element.180), channel_id=1, source_target_pairs={{0,3},{1,2},{2,1},{3,0},{4,7},{5,6},{6,5},{7,4},{8,11},{9,10},{10,... | collective-permute-start | bytes 454664 | tf_op jit(solution)/shard_map/ppermute | solution.py:374
  140.6 12.1 %collective-permute-start.42 = (bf16[592,128]{1,0:T(8,128)(2,1)S(1)}, bf16[592,128]{1,0:T(8,128)(2,1)S(1)}, u32[]{:S(2)}, u32[]{:S(2)}) collective-permute-start(bf16[592,128]{1,0:T(8,128)(2,1)S(1)} %sum.2.refs_0_), channel_id=1, source_target_pairs={{0,24},{4,28},{1,25},{5,29},{2,26},{6,30},{3,27},{7,31}} | collective-permute-start | bytes 454664 | tf_op jit(solution)/shard_map/ppermute | solution.py:367
  147.5 7.3 %collective-permute-start.43 = (bf16[592,128]{1,0:T(8,128)(2,1)S(1)}, bf16[592,128]{1,0:T(8,128)(2,1)S(1)}, u32[]{:S(2)}, u32[]{:S(2)}) collective-permute-start(bf16[592,128]{1,0:T(8,128)(2,1)S(1)} %sum.2.refs_0_), channel_id=1, source_target_pairs={{8,24},{12,28},{9,25},{13,29},{10,26},{14,30},{11,27},{15,31}} | collective-permute-start | bytes 454664 | tf_op jit(solution)/shard_map/ppermute | solution.py:367
  148.8 7.8 %collective-permute-start.44 = (bf16[592,128]{1,0:T(8,128)(2,1)S(1)}, bf16[592,128]{1,0:T(8,128)(2,1)S(1)}, u32[]{:S(2)}, u32[]{:S(2)}) collective-permute-start(bf16[592,128]{1,0:T(8,128)(2,1)S(1)} %sum.2.refs_0_), channel_id=1, source_target_pairs={{16,24},{20,28},{17,25},{21,29},{18,26},{22,30},{19,27},{23,31}} | collective-permute-start | bytes 454664 | tf_op jit(solution)/shard_map/ppermute | solution.py:367
  150.7 7.9 %collective-permute-start.62 = (bf16[576,128]{1,0:T(8,128)(2,1)S(1)}, bf16[576,128]{1,0:T(8,128)(2,1)S(1)}, u32[]{:S(2)}, u32[]{:S(2)}) collective-permute-start(bf16[576,128]{1,0:T(8,128)(2,1)S(1)} %get-tuple-element.197), channel_id=1, source_target_pairs={{0,24},{4,28},{1,25},{5,29},{2,26},{6,30},{3,27},{7,31}} | collective-permute-start | bytes 442376 | tf_op jit(solution)/shard_map/ppermute | solution.py:367
  152.0 6.6 %collective-permute-start.61 = (bf16[576,128]{1,0:T(8,128)(2,1)S(1)}, bf16[576,128]{1,0:T(8,128)(2,1)S(1)}, u32[]{:S(2)}, u32[]{:S(2)}) collective-permute-start(bf16[576,128]{1,0:T(8,128)(2,1)S(1)} %get-tuple-element.197), channel_id=1, source_target_pairs={{0,16},{4,20},{1,17},{5,21},{2,18},{6,22},{3,19},{7,23}} | collective-permute-start | bytes 442376 | tf_op jit(solution)/shard_map/ppermute | solution.py:367
  152.7 5.9 %collective-permute-start.60 = (bf16[576,128]{1,0:T(8,128)(2,1)S(1)}, bf16[576,128]{1,0:T(8,128)(2,1)S(1)}, u32[]{:S(2)}, u32[]{:S(2)}) collective-permute-start(bf16[576,128]{1,0:T(8,128)(2,1)S(1)} %get-tuple-element.197), channel_id=1, source_target_pairs={{0,8},{4,12},{1,9},{5,13},{2,10},{6,14},{3,11},{7,15}} | collective-permute-start | bytes 442376 | tf_op jit(solution)/shard_map/ppermute | solution.py:367
  157.2 8.0 %collective-permute-start.53 = (bf16[592,128]{1,0:T(8,128)(2,1)S(1)}, bf16[592,128]{1,0:T(8,128)(2,1)S(1)}, u32[]{:S(2)}, u32[]{:S(2)}) collective-permute-start(bf16[592,128]{1,0:T(8,128)(2,1)S(1)} %sum.3.total_ref), channel_id=1, source_target_pairs={{24,28},{25,29},{26,30},{27,31}} | collective-permute-start | bytes 454664 | tf_op jit(solution)/shard_map/ppermute | solution.py:367
  166.9 10.7 %collective-permute-start.63 = (bf16[576,128]{1,0:T(8,128)(2,1)S(1)}, bf16[576,128]{1,0:T(8,128)(2,1)S(1)}, u32[]{:S(2)}, u32[]{:S(2)}) collective-permute-start(bf16[576,128]{1,0:T(8,128)(2,1)S(1)} %add_add_fusion.refs_0_), channel_id=1, source_target_pairs={{0,1},{1,0},{2,3},{3,2},{4,5},{5,4},{6,7},{7,6},{8,9},{9,8},{10,11... | collective-permute-start | bytes 442376 | tf_op jit(solution)/shard_map/ppermute | solution.py:374
  167.9 12.6 %collective-permute-start.64 = (bf16[576,128]{1,0:T(8,128)(2,1)S(1)}, bf16[576,128]{1,0:T(8,128)(2,1)S(1)}, u32[]{:S(2)}, u32[]{:S(2)}) collective-permute-start(bf16[576,128]{1,0:T(8,128)(2,1)S(1)} %add_add_fusion.refs_0_), channel_id=1, source_target_pairs={{0,2},{1,3},{2,0},{3,1},{4,6},{5,7},{6,4},{7,5},{8,10},{9,11},{10,... | collective-permute-start | bytes 442376 | tf_op jit(solution)/shard_map/ppermute | solution.py:374
  170.4 10.1 %collective-permute-start.65 = (bf16[576,128]{1,0:T(8,128)(2,1)S(1)}, bf16[576,128]{1,0:T(8,128)(2,1)S(1)}, u32[]{:S(2)}, u32[]{:S(2)}) collective-permute-start(bf16[576,128]{1,0:T(8,128)(2,1)S(1)} %add_add_fusion.refs_0_), channel_id=1, source_target_pairs={{0,3},{1,2},{2,1},{3,0},{4,7},{5,6},{6,5},{7,4},{8,11},{9,10},{10,... | collective-permute-start | bytes 442376 | tf_op jit(solution)/shard_map/ppermute | solution.py:374
  171.3 11.2 %collective-permute-start.54 = (bf16[128,128]{1,0:T(8,128)(2,1)S(1)}, bf16[128,128]{1,0:T(8,128)(2,1)S(1)}, u32[]{:S(2)}, u32[]{:S(2)}) collective-permute-start(bf16[128,128]{1,0:T(8,128)(2,1)S(1)} %get-tuple-element.190), channel_id=1, source_target_pairs={{28,29},{29,28},{30,31},{31,30}} | collective-permute-start | bytes 98312 | tf_op jit(solution)/shard_map/ppermute | solution.py:380
  173.5 10.3 %collective-permute-start.55 = (bf16[128,128]{1,0:T(8,128)(2,1)S(1)}, bf16[128,128]{1,0:T(8,128)(2,1)S(1)}, u32[]{:S(2)}, u32[]{:S(2)}) collective-permute-start(bf16[128,128]{1,0:T(8,128)(2,1)S(1)} %get-tuple-element.191), channel_id=1, source_target_pairs={{28,30},{29,31},{30,28},{31,29}} | collective-permute-start | bytes 98312 | tf_op jit(solution)/shard_map/ppermute | solution.py:380
  177.6 7.5 %collective-permute-start.56 = (bf16[128,128]{1,0:T(8,128)(2,1)S(1)}, bf16[128,128]{1,0:T(8,128)(2,1)S(1)}, u32[]{:S(2)}, u32[]{:S(2)}) collective-permute-start(bf16[128,128]{1,0:T(8,128)(2,1)S(1)} %get-tuple-element.192), channel_id=1, source_target_pairs={{28,31},{29,30},{30,29},{31,28}} | collective-permute-start | bytes 98312 | tf_op jit(solution)/shard_map/ppermute | solution.py:380
  181.1 23.3 %collective-permute-start.71 = (bf16[2304,128]{1,0:T(8,128)(2,1)S(1)}, bf16[2304,128]{1,0:T(8,128)(2,1)S(1)}, u32[]{:S(2)}, u32[]{:S(2)}) collective-permute-start(bf16[2304,128]{1,0:T(8,128)(2,1)S(1)} %assemble.3.refs_2_), channel_id=1, source_target_pairs={{0,4},{4,0},{8,12},{12,8},{16,20},{20,16},{24,28},{28,24},{1,5},{5... | collective-permute-start | bytes 1769480 | tf_op jit(solution)/shard_map/ppermute | solution.py:367
  181.2 7.6 %collective-permute-start.68 = (f32[16,128]{1,0:T(8,128)S(1)}, f32[16,128]{1,0:T(8,128)S(1)}, u32[]{:S(2)}, u32[]{:S(2)}) collective-permute-start(f32[16,128]{1,0:T(8,128)S(1)} %constant_dynamic-update-slice_fusion), channel_id=1, source_target_pairs={{28,20},{29,21},{30,22},{31,23}} | collective-permute-start | bytes 24584 | tf_op jit(solution)/shard_map/ppermute | solution.py:367
  182.5 9.7 %collective-permute-start.67 = (f32[16,128]{1,0:T(8,128)S(1)}, f32[16,128]{1,0:T(8,128)S(1)}, u32[]{:S(2)}, u32[]{:S(2)}) collective-permute-start(f32[16,128]{1,0:T(8,128)S(1)} %constant_dynamic-update-slice_fusion), channel_id=1, source_target_pairs={{28,12},{29,13},{30,14},{31,15}} | collective-permute-start | bytes 24584 | tf_op jit(solution)/shard_map/ppermute | solution.py:367
  183.8 11.2 %collective-permute-start.66 = (f32[16,128]{1,0:T(8,128)S(1)}, f32[16,128]{1,0:T(8,128)S(1)}, u32[]{:S(2)}, u32[]{:S(2)}) collective-permute-start(f32[16,128]{1,0:T(8,128)S(1)} %constant_dynamic-update-slice_fusion), channel_id=1, source_target_pairs={{28,4},{29,5},{30,6},{31,7}} | collective-permute-start | bytes 24584 | tf_op jit(solution)/shard_map/ppermute | solution.py:367
  186.6 8.4 %collective-permute-start.57 = (bf16[592,128]{1,0:T(8,128)(2,1)S(1)}, bf16[592,128]{1,0:T(8,128)(2,1)S(1)}, u32[]{:S(2)}, u32[]{:S(2)}) collective-permute-start(bf16[592,128]{1,0:T(8,128)(2,1)S(1)} %get-tuple-element.194), channel_id=1, source_target_pairs={{28,29},{29,28},{30,31},{31,30}} | collective-permute-start | bytes 454664 | tf_op jit(solution)/shard_map/ppermute | solution.py:380
  188.8 6.2 %collective-permute-start.58 = (bf16[592,128]{1,0:T(8,128)(2,1)S(1)}, bf16[592,128]{1,0:T(8,128)(2,1)S(1)}, u32[]{:S(2)}, u32[]{:S(2)}) collective-permute-start(bf16[592,128]{1,0:T(8,128)(2,1)S(1)} %get-tuple-element.195), channel_id=1, source_target_pairs={{28,30},{29,31},{30,28},{31,29}} | collective-permute-start | bytes 454664 | tf_op jit(solution)/shard_map/ppermute | solution.py:380
  192.2 6.8 %collective-permute-start.59 = (bf16[592,128]{1,0:T(8,128)(2,1)S(1)}, bf16[592,128]{1,0:T(8,128)(2,1)S(1)}, u32[]{:S(2)}, u32[]{:S(2)}) collective-permute-start(bf16[592,128]{1,0:T(8,128)(2,1)S(1)} %get-tuple-element.196), channel_id=1, source_target_pairs={{28,31},{29,30},{30,29},{31,28}} | collective-permute-start | bytes 454664 | tf_op jit(solution)/shard_map/ppermute | solution.py:380
  (21 other events, 140.8 us)

commit v3 on v2

--- a/solution.py
+++ b/solution.py
@@ -146,10 +146,11 @@
     scale_ref[...] = rows_of(scale, 8)
 
 
-def parts_kernel(n, size, here, cot_ref, *refs):
+def parts_kernel(n, size, here, cot_ref, last_cot_ref, *refs):
     wos, outs = refs[:n], refs[n:]
-    for d in range(n):
-        outs[d][...] = dot(wos[d][size : 2 * size, :], cot_ref[...], 0, 0).astype(BF16)
+    cot = jnp.where(here[2] == here[3] - 1, last_cot_ref[...], cot_ref[...])
+    for d in range(n):
+        outs[d][...] = dot(wos[d][size : 2 * size, :], cot, 0, 0).astype(BF16)
 
 
 def layer_out_kernel(n, size, here, x_ref, first_ref, *refs):
@@ -196,21 +197,22 @@
         outs[d][size:, :] = stat
 
 
-def back_out_kernel(n, full, lasts, here, *refs):
+def back_out_kernel(n, full, here, *refs):
     got, refs = refs[:n], refs[n:]
-    scale_ref, gain_ref, x_ref, last_x_ref, cot_ref, other_ref, out = refs
+    scale_ref, gain_ref, x_ref, last_x_ref, cot_ref, last_cot_ref, out = refs
     size = x_ref.shape[0]
     total = total_of(got)
     (stat,) = join_rows(total[size:, :], 1)
     scale = scale_ref[0:1, :]
     gain = gain_ref[block_of(here, 0, size), :].astype(F32)
-    x = jnp.where(here[2] == here[3] - 1, last_x_ref[...], x_ref[...]).astype(F32)
-    dx = (
-        cot_ref[...].astype(F32)
+    is_last = here[2] == here[3] - 1
+    x = jnp.where(is_last, last_x_ref[...], x_ref[...]).astype(F32)
+    cot = jnp.where(is_last, last_cot_ref[...], cot_ref[...]).astype(F32)
+    out[...] = (
+        cot
         + scale * gain * total[:size, :]
         - x * (scale * scale * stat / full)
-    )
-    out[...] = jnp.where(here[2] >= here[3] - lasts, dx.astype(BF16), other_ref[...])
+    ).astype(BF16)
 
 
 def lookup_kernel(here, ids_ref, targets_ref, table_ref, turned_ref, *outs):
@@ -227,11 +229,12 @@
             out[:, t * rows : (t + 1) * rows] = dot(turned_ref[...], hits).astype(BF16)
 
 
-def pair_kernel(here, keep_ref, got_ref, *outs):
-    size = outs[0].shape[0]
-    for d, out in enumerate(outs):
-        at = block_of(here, d, size)
-        out[...] = (keep_ref[at, :].astype(F32) + got_ref[at, :].astype(F32)).astype(BF16)
+def pair_kernel(n, here, keep_ref, got_ref, *outs):
+    size, rows = outs[0].shape
+    for i, out in enumerate(outs):
+        at, t = block_of(here, i % n, size), i // n
+        cut = slice(t * rows, (t + 1) * rows)
+        out[...] = (keep_ref[at, cut].astype(F32) + got_ref[at, cut].astype(F32)).astype(BF16)
 
 
 def assemble_kernel(n, here, *refs):
@@ -246,11 +249,9 @@
     own_ref[...] = jnp.where(here[2] < 2, send, jnp.zeros_like(send))
 
 
-def enter_kernel(tick, emb_scale, here, y_ref, *refs):
+def enter_kernel(emb_scale, here, y_ref, *refs):
     found, out = refs[:-1], refs[-1]
-    rows = y_ref.shape[1]
-    entering = tree_sum([f[:, tick * rows : (tick + 1) * rows].astype(F32) for f in found])
-    entering = (entering * emb_scale).astype(BF16)
+    entering = (total_of(found) * emb_scale).astype(BF16)
     out[...] = jnp.where(here[2] == 0, entering, y_ref[...])
 
 
@@ -302,7 +303,7 @@
     add_terms(total_of(refs[:-1]), refs[-1])
 
 
-def cot_kernel(tick, full, here, total_ref, scale_ref, h_ref, gain_ref, *refs):
+def cot_kernel(full, here, total_ref, scale_ref, h_ref, gain_ref, *refs):
     found, (out, sums_ref) = refs[:-2], refs[-2:]
     size, rows = h_ref.shape
     gain = gain_ref[block_of(here, 0, size), :].astype(F32)
@@ -310,8 +311,7 @@
     capped = jnp.tanh(raw_hit / LOGIT_CAP)
     slope = 1.0 - capped * capped
     whole = rest + jnp.exp(LOGIT_CAP * capped)
-    target = tree_sum([f[:, tick * rows : (tick + 1) * rows].astype(F32) for f in found])
-    dhid = (total_ref[:size, :].astype(F32) - target * (rest * slope)) / whole
+    dhid = (total_ref[:size, :].astype(F32) - total_of(found) * (rest * slope)) / whole
     stat = (weighted - rest * slope * raw_hit) / whole
     scale = scale_ref[0:1, :]
     out[...] = (
@@ -367,18 +367,11 @@
     return lax.ppermute(x, "section", pairs)
 
 
-def swap(blocks, sections=None):
+def swap(blocks):
     n = lax.axis_size("tensor")
-    if sections is None:
-        return [blocks[0]] + [
-            lax.ppermute(blocks[d], "tensor", [(i, i ^ d) for i in range(n)])
-            for d in range(1, n)
-        ]
-    out = [blocks[0]]
-    for d in range(1, n):
-        pairs = [(s * n + i, s * n + (i ^ d)) for s in sections for i in range(n)]
-        out.append(lax.ppermute(blocks[d], ("section", "tensor"), pairs))
-    return out
+    return [blocks[0]] + [
+        lax.ppermute(blocks[d], "tensor", [(i, i ^ d) for i in range(n)]) for d in range(1, n)
+    ]
 
 
 def share(x):
@@ -390,14 +383,6 @@
     return [
         2 * c + core for c in range(lax.axis_size("section") // 2) if c != root // 2
     ]
-
-
-def along_chips(x, root):
-    return [hop(x, [(root, s)]) for s in other_chips(root)]
-
-
-def across(root):
-    return [(s, s ^ 1) for s in [root] + other_chips(root)]
 
 
 def from_chip(own, send, root):
@@ -461,16 +446,14 @@
         4 * full * rows * vocab * ticks,
     )
 
-    def look_up(keep, send):
-        found = call(
-            pair_kernel,
-            [((piece, ticks * rows), BF16)] * n,
-            [here, keep, other_core(send)],
-            "pair",
-        )
-        return tree_sum([b.astype(F32) for b in swap(found)]).astype(BF16)
-
-    found = look_up(*rows_found)
+    keep, send = rows_found
+    found = call(
+        functools.partial(pair_kernel, n), [act] * (n * ticks), [here, keep, other_core(send)], "pair"
+    )
+
+    def rows_of_tick(found, *others):
+        found = after(swap(found), *others)
+        return tree_sum([b.astype(F32) for b in found]).astype(BF16)
 
     def layer_out(x, got, earlier):
         return call(
@@ -490,20 +473,12 @@
             work,
         )
 
-    def back_out(got, saved, x, last_x, cot, other=None):
+    def back_out(got, saved, x, last_x, cot, last_cot):
         return call(
-            functools.partial(back_out_kernel, n, full, sections if other is None else 1),
+            functools.partial(back_out_kernel, n, full),
             [act],
-            [here, *got, saved[4], gain, x, last_x, cot, cot if other is None else other],
+            [here, *got, saved[4], gain, x, last_x, cot, last_cot],
             "back_out",
-        )
-
-    def parts(cot):
-        return call(
-            functools.partial(parts_kernel, n, piece),
-            [((head, rows), BF16)] * n,
-            [here, cot, *base],
-            "parts",
         )
 
     def assemble(parts):
@@ -537,22 +512,23 @@
     messages = call(
         functools.partial(forward_parts_kernel, n, piece),
         [((2 * head, rows), BF16)] * n,
-        [here, *after(base, found), gain, wq, cots],
+        [here, *base, gain, wq, cots],
         "forward",
         work,
         whole_x,
     )
-    looked = to_chips(found, 0, last)
     got0 = swap(messages)
     y0, _, _ = layer_out(acts, got0, acts)
+    found0 = rows_of_tick(after(found[:n], y0))
+    looked0 = to_chips(found0, 0, last)
     y0_even = hop(y0, [(last, last - 1)])
-    saved0 = recompute(share(after(held0, y0)), 0)
+    saved0 = recompute(share(after(held0, found0)), 0)
     terms0 = back(got0, saved0)
 
     acts1 = call(
-        functools.partial(enter_kernel, 0, emb_scale),
+        functools.partial(enter_kernel, emb_scale),
         [act],
-        [here, hop(y0, up), *looked],
+        [here, hop(y0, up), *looked0],
         "enter",
     )
     a1 = call(
@@ -565,72 +541,73 @@
     )
     y1, h_send, h_own = layer_out(acts1, share(a1), y0_even)
 
-    gin0 = back_out(swap(after(terms0, y1)), saved0, held0, held0, cots)
-    saved1 = recompute(share(after(held1, y1)), 1)
+    gin0 = back_out(swap(after(terms0, y1)), saved0, held0, held0, cots, cots)
+    saved1 = recompute(share(after(held1, a1)), 1)
     cots1 = hop(gin0, down)
-    h_mine = after(from_chip(h_own, h_send, last), gin0, saved1[1])
-    h_mine = assemble(share(h_mine))
+    h_mine = after(from_chip(h_own, h_send, last), saved1[1])
+    h_mine = assemble(after(share(h_mine), gin0))
     h_other = other_core(h_mine)
 
     normed_a, raw_a, scale_a, terms_a = run_head(h_mine, 0)
     normed_b, raw_b, scale_b, terms_b = run_head(h_other, 1)
     y1_up = hop(after(y1, h_mine), up)
-    parts1 = swap(parts(after(cots1, raw_b)))
-    acts2 = call(
-        functools.partial(enter_kernel, 1, emb_scale),
-        [act],
-        [here, y1_up, *looked],
-        "enter",
-    )
     terms = call(
         pair_terms_kernel,
         [message] * n,
-        [here, after(terms_a, acts2), other_core(terms_b)],
+        [here, after(terms_a, y1_up, cots1), other_core(terms_b)],
         "pair_terms",
     )
-    gin1 = back_out(
-        swap(back(after(parts1, terms), saved1)), saved1, held1, acts, cots1
-    )
     total = call(sum_kernel, [message], [here, *swap(terms)], "sum")
-    g_send, g_own = call(pick_kernel, [act] * 2, [here, gin0, hop(gin1, [(0, 1)])], "pick")
-    total = to_chips(total, last - 1, last)
-    total = call(sum_kernel, [message], [here, *after(total, g_own)], "sum")
-
-    def cot_of(tick, total, scale, h):
+    found1 = rows_of_tick(after(found[n:], total))
+    total = after(to_chips(total, last - 1, last), found1)
+    total = call(sum_kernel, [message], [here, *total], "sum")
+    looked1 = to_chips(after(found1, total), 0, last)
+
+    def cot_of(total, scale, h, looked):
         return call(
-            functools.partial(cot_kernel, tick, full),
+            functools.partial(cot_kernel, full),
             [act, ((8, rows), F32)],
             [here, total, scale, h, fgain, *looked],
             "cot",
         )
 
-    cot0, sums0 = cot_of(0, hop(total, [(last - 1, last)]), scale_b, y0)
-
-    late_parts = parts(cot0)
-    late_terms = back(swap(late_parts, [last]), saved1)
-    leaving_a = assemble(share(after(from_chip(g_own, g_send, 0), late_parts[0])))
+    cot0, sums0 = cot_of(hop(total, [(last - 1, last)]), scale_b, y0, looked0)
+
+    cot_parts = call(
+        functools.partial(parts_kernel, n, piece),
+        [((head, rows), BF16)] * n,
+        [here, cots1, cot0, *base],
+        "parts",
+    )
+    terms1 = back(after(swap(cot_parts), looked1), saved1)
+    cot1, sums1 = cot_of(after(total, terms1[0]), scale_a, y1, looked1)
+    sums = jnp.concatenate([sums0, sums1], axis=0)
+    sums = sums + hop(sums, [(last, last - 1)])
+    gin1 = back_out(after(swap(terms1), sums), saved1, held1, acts, cots1, cot0)
+    g_send, g_own = call(pick_kernel, [act] * 2, [here, gin0, hop(gin1, [(0, 1)])], "pick")
+    sums = from_chip(sums, sums, last)
+    leaving_a = share(from_chip(g_own, g_send, 0))
+    gin1_down = hop(gin1, down)
+    acts2 = call(
+        functools.partial(enter_kernel, emb_scale),
+        [act],
+        [here, y1_up, *after(looked1, gin1)],
+        "enter",
+    )
+    leaving_a = assemble(after(leaving_a, acts2, sums, gin1_down))
     leaving_b = other_core(leaving_a)
-    cot1, sums1 = cot_of(1, after(total, late_parts[0]), scale_a, y1)
-    sums = jnp.concatenate([sums0, sums1], axis=0)
-    for part in along_chips(sums, last):
-        sums = sums + part
-    late_terms = after(swap(late_terms, [last]), leaving_a, sums)
-    late = back_out(late_terms, saved1, held1, acts, cot0, gin1)
-    late_down = hop(late, down)
-    sums = after(sums, late)
-    sums = sums + hop(sums, across(last))
+    cots2 = call(last_cots_kernel, [act], [here, after(gin1_down, leaving_a), cot1], "last_cots")
     grad, losses = call(
         functools.partial(grad_kernel, ticks, emb_scale),
         [((vocab, full), BF16), ((8, rows), F32)],
         [
             *(here, back_ids, targets, sums),
             *(raw_a, normed_a, leaving_a),
-            *(raw_b, normed_b, leaving_b),
+            *(raw_b, normed_b, after(leaving_b, cots2)),
         ],
         "grad",
         8 * full * rows * vocab,
     )
-    cots2 = call(last_cots_kernel, [act], [here, late_down, cot1], "last_cots")
     return (acts2.T[None], cots2.T[None], grad, losses[:ticks, 0])
 
 

time: 209 us -> 192 us (0.919)
  waiting for transfers between devices: 62.7 us -> 54.2 us
  starting transfers between devices: 100 us -> 94.1 us
  Pallas kernels: 36.9 us -> 33.9 us
    ppermute x6 -> x0, starting transfers between devices: 16.7 us -> none  [swap(): out.append(lax.ppermute(blocks[d], ('section', 'tensor'), pairs))]
    ppermute x27 -> x30, starting transfers between devices: 44.9 us -> 55.4 us  [hop(): return lax.ppermute(x, 'section', pairs)]
    ppermute x6 -> x0, waiting for transfers between devices: 3.94 us -> none  [swap(): out.append(lax.ppermute(blocks[d], ('section', 'tensor'), pairs))]
    pallas_call x31 -> x28, Pallas kernels: 36.9 us -> 33.9 us  [call(): pl.pallas_call(body, out_shape=[jax.ShapeDtypeStruct(s, d) for s, d in ou...]
    ppermute x39 -> x42, waiting for transfers between devices: 38.9 us -> 35.8 us  [swap(): lax.ppermute(blocks[d], 'tensor', [(i, i ^ d) for i in range(n)])]
    ppermute x27 -> x30, waiting for transfers between devices: 19.9 us -> 18.4 us  [hop(): return lax.ppermute(x, 'section', pairs)]
    ppermute x39 -> x42, starting transfers between devices: 38.4 us -> 38.7 us  [swap(): lax.ppermute(blocks[d], 'tensor', [(i, i ^ d) for i in range(n)])]
  transfers between devices with their start and end apart: 72 -> 72, of which waited for: 27 -> 32; matrix products, arithmetic and copies ran while one was open for 0% -> 0% of each run, Pallas kernels for 11% -> 10%
where the time goes in v3:
time: 192 us; the launch traced here: 191 us
  starting transfers between devices  94.1 us (49%)
  waiting for transfers between devices  54.2 us (28%)
  Pallas kernels  33.9 us (18%)
  local copies, waits for them, and re-layouts  6.81 us (4%)
    ppermute x30, starting transfers between devices, hop(): return lax.ppermute(x, 'section', pairs)  55.4 us
    ppermute x42, starting transfers between devices, swap(): lax.ppermute(blocks[d], 'tensor', [(i, i ^ d) for i in range(n)])  38.7 us
    ppermute x42, waiting for transfers between devices, swap(): lax.ppermute(blocks[d], 'tensor', [(i, i ^ d) for i in range(n)])  35.8 us
    pallas_call x28, Pallas kernels, call(): pl.pallas_call(body, out_shape=[jax.ShapeDtypeStruct(s, d) for s, d in ou...  33.9 us
    ppermute x30, waiting for transfers between devices, hop(): return lax.ppermute(x, 'section', pairs)  18.4 us
    unnamed x27, local copies, waits for them, and re-layouts  5.46 us
  transfers between devices with their start and end apart: 72, of which 32 were waited for; matrix products, arithmetic and copies ran while one was open for 0% of the time, Pallas kernels for 10%

profile of v3, /device:TPU:29, one launch (start us, length us, event | category | flops | bytes accessed | tf_op | source)
XLA Modules:
  0.0 190.5 jit_solution(7018398298665223835)
XLA Ops:
  5.2 1.4 copy-done.1
  8.0 2.0 %lookup.1 = (bf16[2304,256]{1,0:T(8,128)(2,1)S(1)}, bf16[2304,256]{1,0:T(8,128)(2,1)S(1)}, bf16[2304,256]{1,0:T(8,128)(2,1)S(1)}) custom-call(s32[4]{0:T(128)S(1)} %pad_add_fusion.here, s32[2,128]{1,0:T(2,128)S(1)} %copy-done.11, s32[2,128]{1,0:T(2,128)S(1)} %copy-done.7, bf16[256,2304]{1,0:T(8,128)(2,1)S(1)} %copy-done.1), custom_call_target="tpu_custom_call" | custom-call | flops 603979776 | bytes 4720656 | tf_op jit(solution)/shard_map/lookup/pallas_call | solution.py:27
  13.3 5.9 %collective-permute-done.refs_1_.refs_5_ = bf16[1152,128]{1,0:T(8,128)(2,1)S(1)} collective-permute-done((bf16[1152,128]{1,0:T(8,128)(2,1)S(1)}, bf16[1152,128]{1,0:T(8,128)(2,1)S(1)}, u32[]{:S(2)}, u32[]{:S(2)}) %collective-permute-start) | collective-permute-done | bytes 294944 | tf_op jit(solution)/shard_map/ppermute | solution.py:373
  19.3 7.2 %collective-permute-done.1.refs_2_.refs_6_ = bf16[1152,128]{1,0:T(8,128)(2,1)S(1)} collective-permute-done((bf16[1152,128]{1,0:T(8,128)(2,1)S(1)}, bf16[1152,128]{1,0:T(8,128)(2,1)S(1)}, u32[]{:S(2)}, u32[]{:S(2)}) %collective-permute-start.1) | collective-permute-done | bytes 294944 | tf_op jit(solution)/shard_map/ppermute | solution.py:373
  26.5 2.0 %forward.2 = (bf16[256,128]{1,0:T(8,128)(2,1)S(1)}, bf16[256,128]{1,0:T(8,128)(2,1)S(1)}, bf16[256,128]{1,0:T(8,128)(2,1)S(1)}, bf16[256,128]{1,0:T(8,128)(2,1)S(1)}) custom-call(s32[4]{0:T(128)S(1)} %pad_add_fusion.here, bf16[1152,128]{1,0:T(8,128)(2,1)S(1)} %get-tuple-element.129.refs_0_.refs_4_, ...), custom_call_target="tpu_custom_call" | custom-call | flops 234881024 | bytes 3948560 | tf_op jit(solution)/shard_map/forward/pallas_call | solution.py:27
  32.0 2.2 %collective-permute-done.5.refs_3_ = bf16[256,128]{1,0:T(8,128)(2,1)S(1)} collective-permute-done((bf16[256,128]{1,0:T(8,128)(2,1)S(1)}, bf16[256,128]{1,0:T(8,128)(2,1)S(1)}, u32[]{:S(2)}, u32[]{:S(2)}) %collective-permute-start.5) | collective-permute-done | bytes 65568 | tf_op jit(solution)/shard_map/ppermute | solution.py:373
  34.2 1.6 layer_out.2
  39.3 1.3 collective-permute-start.6
  41.6 1.7 collective-permute-done.8
  43.7 1.3 collective-permute-start.11
  45.1 1.3 collective-permute-start.12
  46.4 1.3 collective-permute-start.13
  49.1 2.5 %collective-permute-done.11.refs_1_ = bf16[576,128]{1,0:T(8,128)(2,1)S(1)} collective-permute-done((bf16[576,128]{1,0:T(8,128)(2,1)S(1)}, bf16[576,128]{1,0:T(8,128)(2,1)S(1)}, u32[]{:S(2)}, u32[]{:S(2)}) %collective-permute-start.11) | collective-permute-done | bytes 147488 | tf_op jit(solution)/shard_map/ppermute | solution.py:367
  53.1 1.5 collective-permute-done.13.refs_3_
  55.2 1.5 collective-permute-start.15
  56.7 1.3 collective-permute-start.17
  58.0 4.1 %collective-permute-start.14 = (bf16[576,128]{1,0:T(8,128)(2,1)S(1)}, bf16[576,128]{1,0:T(8,128)(2,1)S(1)}, u32[]{:S(2)}, u32[]{:S(2)}) collective-permute-start(bf16[576,128]{1,0:T(8,128)(2,1)S(1)} %get-tuple-element.138.h_ref), channel_id=1, source_target_pairs={{28,24},{29,25},{30,26},{31,27}} | collective-permute-start | bytes 442376 | tf_op jit(solution)/shard_map/ppermute | solution.py:367
  62.1 1.6 recompute.2
  63.7 1.5 back.2
  65.3 1.8 forward.3.refs_0_
  68.9 1.3 collective-permute-start.23
  71.5 1.8 collective-permute-start.29
  74.2 1.3 collective-permute-start.24
  75.5 1.3 collective-permute-start.25
  76.8 1.5 collective-permute-start.26
  79.6 1.8 recompute.3
  81.4 1.5 collective-permute-start.35
  84.2 1.4 collective-permute-start.32
  87.1 2.7 %collective-permute-done.30.refs_1_ = bf16[576,128]{1,0:T(8,128)(2,1)S(1)} collective-permute-done((bf16[576,128]{1,0:T(8,128)(2,1)S(1)}, bf16[576,128]{1,0:T(8,128)(2,1)S(1)}, u32[]{:S(2)}, u32[]{:S(2)}) %collective-permute-start.30) | collective-permute-done | bytes 147488 | tf_op jit(solution)/shard_map/ppermute | solution.py:373
  89.8 1.4 collective-permute-done.32.refs_3_
  91.8 6.1 %collective-permute-start.38 = (bf16[2304,128]{1,0:T(8,128)(2,1)S(1)}, bf16[2304,128]{1,0:T(8,128)(2,1)S(1)}, u32[]{:S(2)}, u32[]{:S(2)}) collective-permute-start(bf16[2304,128]{1,0:T(8,128)(2,1)S(1)} %assemble.2.h_ref), channel_id=1, source_target_pairs={{0,4},{4,0},{8,12},{12,8},{16,20},{20,16},{24,28},{28,24},{1,5},{5... | collective-permute-start | bytes 1769480 | tf_op jit(solution)/shard_map/ppermute | solution.py:367
  97.9 1.6 collective-permute-done.38.h_ref
  99.5 1.8 head.3
  101.8 2.0 %collective-permute-start.37 = (bf16[576,128]{1,0:T(8,128)(2,1)S(1)}, bf16[576,128]{1,0:T(8,128)(2,1)S(1)}, u32[]{:S(2)}, u32[]{:S(2)}) collective-permute-start(bf16[576,128]{1,0:T(8,128)(2,1)S(1)} %back_out.2.even_ref), channel_id=1, source_target_pairs={{4,0},{8,4},{12,8},{16,12},{20,16},{24,20},{28,24},{5,1},{9,5},{13... | collective-permute-start | bytes 442376 | tf_op jit(solution)/shard_map/ppermute | solution.py:367
  103.8 1.3 collective-permute-start.36
  105.1 1.8 head.2
  110.5 1.4 collective-permute-done.40.refs_1_
  112.4 1.9 collective-permute-done.42.refs_3_
  117.6 1.3 collective-permute-start.46
  118.8 1.3 collective-permute-start.47
  120.2 1.3 collective-permute-start.48
  121.7 4.7 %collective-permute-done.46.refs_1_ = bf16[592,128]{1,0:T(8,128)(2,1)S(1)} collective-permute-done((bf16[592,128]{1,0:T(8,128)(2,1)S(1)}, bf16[592,128]{1,0:T(8,128)(2,1)S(1)}, u32[]{:S(2)}, u32[]{:S(2)}) %collective-permute-start.46) | collective-permute-done | bytes 151584 | tf_op jit(solution)/shard_map/ppermute | solution.py:367
  126.4 1.3 collective-permute-done.47.refs_2_
  127.6 1.3 collective-permute-done.48.refs_3_
  129.6 1.3 collective-permute-start.52
  130.9 1.3 collective-permute-start.49
  132.2 1.3 collective-permute-start.50
  133.5 1.3 collective-permute-start.51
  134.8 3.8 %collective-permute-done.52.total_ref = bf16[592,128]{1,0:T(8,128)(2,1)S(1)} collective-permute-done((bf16[592,128]{1,0:T(8,128)(2,1)S(1)}, bf16[592,128]{1,0:T(8,128)(2,1)S(1)}, u32[]{:S(2)}, u32[]{:S(2)}) %collective-permute-start.52) | collective-permute-done | bytes 151584 | tf_op jit(solution)/shard_map/ppermute | solution.py:367
  143.9 2.1 %collective-permute-done.55.refs_3_ = bf16[128,128]{1,0:T(8,128)(2,1)S(1)} collective-permute-done((bf16[128,128]{1,0:T(8,128)(2,1)S(1)}, bf16[128,128]{1,0:T(8,128)(2,1)S(1)}, u32[]{:S(2)}, u32[]{:S(2)}) %collective-permute-start.55) | collective-permute-done | bytes 32800 | tf_op jit(solution)/shard_map/ppermute | solution.py:373
  146.0 1.5 back.3
  148.4 1.7 collective-permute-start.58
  150.9 6.1 %collective-permute-start.59 = (f32[16,128]{1,0:T(8,128)S(1)}, f32[16,128]{1,0:T(8,128)S(1)}, u32[]{:S(2)}, u32[]{:S(2)}) collective-permute-start(f32[16,128]{1,0:T(8,128)S(1)} %constant_dynamic-update-slice_fusion), channel_id=1, source_target_pairs={{28,24},{29,25},{30,26},{31,27}} | collective-permute-start | bytes 24584 | tf_op jit(solution)/shard_map/ppermute | solution.py:367
  161.2 1.3 collective-permute-start.64
  162.5 5.8 %collective-permute-start.68 = (f32[16,128]{1,0:T(8,128)S(1)}, f32[16,128]{1,0:T(8,128)S(1)}, u32[]{:S(2)}, u32[]{:S(2)}) collective-permute-start(f32[16,128]{1,0:T(8,128)S(1)} %add.61), channel_id=1, source_target_pairs={{28,4},{24,0},{29,5},{25,1},{30,6},{26,2},{31,7},{27,3}} | collective-permute-start | bytes 24584 | tf_op jit(solution)/shard_map/ppermute | solution.py:367
  168.3 1.3 collective-permute-start.69
  169.7 1.3 collective-permute-start.70
  171.0 3.2 %collective-permute-start.60 = (bf16[576,128]{1,0:T(8,128)(2,1)S(1)}, bf16[576,128]{1,0:T(8,128)(2,1)S(1)}, u32[]{:S(2)}, u32[]{:S(2)}) collective-permute-start(bf16[576,128]{1,0:T(8,128)(2,1)S(1)} %back_out.3), channel_id=1, source_target_pairs={{4,0},{8,4},{12,8},{16,12},{20,16},{24,20},{28,24},{5,1},{9,5},{13... | collective-permute-start | bytes 442376 | tf_op jit(solution)/shard_map/ppermute | solution.py:367
  177.0 1.3 enter.3
  178.3 1.5 collective-permute-done.65.refs_1_
  180.6 2.7 %collective-permute-done.67.refs_3_ = bf16[576,128]{1,0:T(8,128)(2,1)S(1)} collective-permute-done((bf16[576,128]{1,0:T(8,128)(2,1)S(1)}, bf16[576,128]{1,0:T(8,128)(2,1)S(1)}, u32[]{:S(2)}, u32[]{:S(2)}) %collective-permute-start.67) | collective-permute-done | bytes 147488 | tf_op jit(solution)/shard_map/ppermute | solution.py:373
  183.9 1.4 collective-permute-start.71
  185.3 1.2 last_cots.1
  186.9 3.0 %grad.1 = (bf16[256,2304]{1,0:T(8,128)(2,1)}, f32[8,128]{1,0:T(8,128)S(1)}) custom-call(s32[4]{0:T(128)S(1)} %pad_add_fusion.here, s32[2,128]{1,0:T(2,128)S(1)} %copy-done.10, s32[2,128]{1,0:T(2,128)S(1)} %copy-done.8, f32[16,128]{1,0:T(8,128)S(1)} %add_add_fusion.2.sums_ref, f32[256,128]{1,0:T(8,128)S(1)} %get-tuple-element.247.refs_0_, ...), custom_call_target="tpu_custom_call" | custom-call | flops 603979776 | bytes 3815440 | tf_op jit(solution)/shard_map/grad/pallas_call | solution.py:27
  (146 shorter events, 55.1 us)
Async XLA Ops:
  9.9 25.8 %collective-permute-start.7 = (bf16[2304,256]{1,0:T(8,128)(2,1)S(1)}, bf16[2304,256]{1,0:T(8,128)(2,1)S(1)}, u32[]{:S(2)}, u32[]{:S(2)}) collective-permute-start(bf16[2304,256]{1,0:T(8,128)(2,1)S(1)} %get-tuple-element.141), channel_id=1, source_target_pairs={{0,4},{4,0},{8,12},{12,8},{16,20},{20,16},{24,28},{28,24},{1,5},{5... | collective-permute-start | bytes 3538952 | tf_op jit(solution)/shard_map/ppermute | solution.py:367
  10.7 8.6 %collective-permute-start = (bf16[1152,128]{1,0:T(8,128)(2,1)S(1)}, bf16[1152,128]{1,0:T(8,128)(2,1)S(1)}, u32[]{:S(2)}, u32[]{:S(2)}) collective-permute-start(bf16[1152,128]{1,0:T(8,128)(2,1)S(1)} %get-tuple-element.130), channel_id=1, source_target_pairs={{0,1},{1,0},{2,3},{3,2},{4,5},{5,4},{6,7},{7,6},{8,9},{9,8},{10,11... | collective-permute-start | bytes 884744 | tf_op jit(solution)/shard_map/ppermute | solution.py:373
  11.9 14.6 %collective-permute-start.1 = (bf16[1152,128]{1,0:T(8,128)(2,1)S(1)}, bf16[1152,128]{1,0:T(8,128)(2,1)S(1)}, u32[]{:S(2)}, u32[]{:S(2)}) collective-permute-start(bf16[1152,128]{1,0:T(8,128)(2,1)S(1)} %get-tuple-element.131), channel_id=1, source_target_pairs={{0,2},{1,3},{2,0},{3,1},{4,6},{5,7},{6,4},{7,5},{8,10},{9,11},{10,... | collective-permute-start | bytes 884744 | tf_op jit(solution)/shard_map/ppermute | solution.py:373
  12.1 14.3 %collective-permute-start.2 = (bf16[1152,128]{1,0:T(8,128)(2,1)S(1)}, bf16[1152,128]{1,0:T(8,128)(2,1)S(1)}, u32[]{:S(2)}, u32[]{:S(2)}) collective-permute-start(bf16[1152,128]{1,0:T(8,128)(2,1)S(1)} %get-tuple-element.132), channel_id=1, source_target_pairs={{0,3},{1,2},{2,1},{3,0},{4,7},{5,6},{6,5},{7,4},{8,11},{9,10},{10,... | collective-permute-start | bytes 884744 | tf_op jit(solution)/shard_map/ppermute | solution.py:373
  30.1 4.1 %collective-permute-start.5 = (bf16[256,128]{1,0:T(8,128)(2,1)S(1)}, bf16[256,128]{1,0:T(8,128)(2,1)S(1)}, u32[]{:S(2)}, u32[]{:S(2)}) collective-permute-start(bf16[256,128]{1,0:T(8,128)(2,1)S(1)} %get-tuple-element.137), channel_id=1, source_target_pairs={{0,3},{1,2},{2,1},{3,0},{4,7},{5,6},{6,5},{7,4},{8,11},{9,10},{10,... | collective-permute-start | bytes 196616 | tf_op jit(solution)/shard_map/ppermute | solution.py:373
  36.6 5.0 %collective-permute-start.10 = (bf16[576,128]{1,0:T(8,128)(2,1)S(1)}, bf16[576,128]{1,0:T(8,128)(2,1)S(1)}, u32[]{:S(2)}, u32[]{:S(2)}) collective-permute-start(bf16[576,128]{1,0:T(8,128)(2,1)S(1)} %get-tuple-element.149), channel_id=1, source_target_pairs={{0,3},{1,2},{2,1},{3,0},{4,7},{5,6},{6,5},{7,4},{8,11},{9,10},{10,... | collective-permute-start | bytes 442376 | tf_op jit(solution)/shard_map/ppermute | solution.py:373
  37.8 5.5 %collective-permute-start.8 = (bf16[576,128]{1,0:T(8,128)(2,1)S(1)}, bf16[576,128]{1,0:T(8,128)(2,1)S(1)}, u32[]{:S(2)}, u32[]{:S(2)}) collective-permute-start(bf16[576,128]{1,0:T(8,128)(2,1)S(1)} %get-tuple-element.147), channel_id=1, source_target_pairs={{0,1},{1,0},{2,3},{3,2},{4,5},{5,4},{6,7},{7,6},{8,9},{9,8},{10,11... | collective-permute-start | bytes 442376 | tf_op jit(solution)/shard_map/ppermute | solution.py:373
  38.6 5.1 %collective-permute-start.9 = (bf16[576,128]{1,0:T(8,128)(2,1)S(1)}, bf16[576,128]{1,0:T(8,128)(2,1)S(1)}, u32[]{:S(2)}, u32[]{:S(2)}) collective-permute-start(bf16[576,128]{1,0:T(8,128)(2,1)S(1)} %get-tuple-element.148), channel_id=1, source_target_pairs={{0,2},{1,3},{2,0},{3,1},{4,6},{5,7},{6,4},{7,5},{8,10},{9,11},{10,... | collective-permute-start | bytes 442376 | tf_op jit(solution)/shard_map/ppermute | solution.py:373
  39.3 9.5 %collective-permute-start.6 = (bf16[576,128]{1,0:T(8,128)(2,1)S(1)}, bf16[576,128]{1,0:T(8,128)(2,1)S(1)}, u32[]{:S(2)}, u32[]{:S(2)}) collective-permute-start(bf16[576,128]{1,0:T(8,128)(2,1)S(1)} %get-tuple-element.138.h_ref), channel_id=1, source_target_pairs={{0,4},{4,8},{8,12},{12,16},{16,20},{20,24},{24,28},{1,5},{5,9},{9,... | collective-permute-start | bytes 442376 | tf_op jit(solution)/shard_map/ppermute | solution.py:367
  43.7 7.9 %collective-permute-start.11 = (bf16[576,128]{1,0:T(8,128)(2,1)S(1)}, bf16[576,128]{1,0:T(8,128)(2,1)S(1)}, u32[]{:S(2)}, u32[]{:S(2)}) collective-permute-start(bf16[576,128]{1,0:T(8,128)(2,1)S(1)} %add_convert_fusion.1.refs_0_), channel_id=1, source_target_pairs={{8,0},{4,28},{9,1},{5,29},{10,2},{6,30},{11,3},{7,31}} | collective-permute-start | bytes 442376 | tf_op jit(solution)/shard_map/ppermute | solution.py:367
  45.1 8.0 %collective-permute-start.12 = (bf16[576,128]{1,0:T(8,128)(2,1)S(1)}, bf16[576,128]{1,0:T(8,128)(2,1)S(1)}, u32[]{:S(2)}, u32[]{:S(2)}) collective-permute-start(bf16[576,128]{1,0:T(8,128)(2,1)S(1)} %add_convert_fusion.1.refs_0_), channel_id=1, source_target_pairs={{16,0},{12,28},{17,1},{13,29},{18,2},{14,30},{19,3},{15,31}} | collective-permute-start | bytes 442376 | tf_op jit(solution)/shard_map/ppermute | solution.py:367
  46.4 8.2 %collective-permute-start.13 = (bf16[576,128]{1,0:T(8,128)(2,1)S(1)}, bf16[576,128]{1,0:T(8,128)(2,1)S(1)}, u32[]{:S(2)}, u32[]{:S(2)}) collective-permute-start(bf16[576,128]{1,0:T(8,128)(2,1)S(1)} %add_convert_fusion.1.refs_0_), channel_id=1, source_target_pairs={{24,0},{20,28},{25,1},{21,29},{26,2},{22,30},{27,3},{23,31}} | collective-permute-start | bytes 442376 | tf_op jit(solution)/shard_map/ppermute | solution.py:367
  47.7 9.0 %collective-permute-start.18 = (bf16[576,128]{1,0:T(8,128)(2,1)S(1)}, bf16[576,128]{1,0:T(8,128)(2,1)S(1)}, u32[]{:S(2)}, u32[]{:S(2)}) collective-permute-start(bf16[576,128]{1,0:T(8,128)(2,1)S(1)} %get-tuple-element.154.refs_0_.refs_6_.refs_7_), channel_id=1, source_target_pairs={{0,1},{1,0},{2,3},{3,2},{4,5},{5,4},{6,7},{7,6},{8,9},{9,8},{10,11... | collective-permute-start | bytes 442376 | tf_op jit(solution)/shard_map/ppermute | solution.py:373
  48.8 9.1 %collective-permute-start.19 = (bf16[576,128]{1,0:T(8,128)(2,1)S(1)}, bf16[576,128]{1,0:T(8,128)(2,1)S(1)}, u32[]{:S(2)}, u32[]{:S(2)}) collective-permute-start(bf16[576,128]{1,0:T(8,128)(2,1)S(1)} %get-tuple-element.154.refs_0_.refs_6_.refs_7_), channel_id=1, source_target_pairs={{0,2},{1,3},{2,0},{3,1},{4,6},{5,7},{6,4},{7,5},{8,10},{9,11},{10,... | collective-permute-start | bytes 442376 | tf_op jit(solution)/shard_map/ppermute | solution.py:373
  51.6 10.5 %collective-permute-start.20 = (bf16[576,128]{1,0:T(8,128)(2,1)S(1)}, bf16[576,128]{1,0:T(8,128)(2,1)S(1)}, u32[]{:S(2)}, u32[]{:S(2)}) collective-permute-start(bf16[576,128]{1,0:T(8,128)(2,1)S(1)} %get-tuple-element.154.refs_0_.refs_6_.refs_7_), channel_id=1, source_target_pairs={{0,3},{1,2},{2,1},{3,0},{4,7},{5,6},{6,5},{7,4},{8,11},{9,10},{10,... | collective-permute-start | bytes 442376 | tf_op jit(solution)/shard_map/ppermute | solution.py:373
  55.2 10.0 %collective-permute-start.15 = (bf16[576,128]{1,0:T(8,128)(2,1)S(1)}, bf16[576,128]{1,0:T(8,128)(2,1)S(1)}, u32[]{:S(2)}, u32[]{:S(2)}) collective-permute-start(bf16[576,128]{1,0:T(8,128)(2,1)S(1)} %enter.2.refs_0_.x_ref), channel_id=1, source_target_pairs={{0,1},{1,0},{2,3},{3,2},{4,5},{5,4},{6,7},{7,6},{8,9},{9,8},{10,11... | collective-permute-start | bytes 442376 | tf_op jit(solution)/shard_map/ppermute | solution.py:373
  56.7 8.5 %collective-permute-start.16 = (bf16[576,128]{1,0:T(8,128)(2,1)S(1)}, bf16[576,128]{1,0:T(8,128)(2,1)S(1)}, u32[]{:S(2)}, u32[]{:S(2)}) collective-permute-start(bf16[576,128]{1,0:T(8,128)(2,1)S(1)} %enter.2.refs_0_.x_ref), channel_id=1, source_target_pairs={{0,2},{1,3},{2,0},{3,1},{4,6},{5,7},{6,4},{7,5},{8,10},{9,11},{10,... | collective-permute-start | bytes 442376 | tf_op jit(solution)/shard_map/ppermute | solution.py:373
  56.7 8.5 %collective-permute-start.17 = (bf16[576,128]{1,0:T(8,128)(2,1)S(1)}, bf16[576,128]{1,0:T(8,128)(2,1)S(1)}, u32[]{:S(2)}, u32[]{:S(2)}) collective-permute-start(bf16[576,128]{1,0:T(8,128)(2,1)S(1)} %enter.2.refs_0_.x_ref), channel_id=1, source_target_pairs={{0,3},{1,2},{2,1},{3,0},{4,7},{5,6},{6,5},{7,4},{8,11},{9,10},{10,... | collective-permute-start | bytes 442376 | tf_op jit(solution)/shard_map/ppermute | solution.py:373
  58.0 12.3 %collective-permute-start.14 = (bf16[576,128]{1,0:T(8,128)(2,1)S(1)}, bf16[576,128]{1,0:T(8,128)(2,1)S(1)}, u32[]{:S(2)}, u32[]{:S(2)}) collective-permute-start(bf16[576,128]{1,0:T(8,128)(2,1)S(1)} %get-tuple-element.138.h_ref), channel_id=1, source_target_pairs={{28,24},{29,25},{30,26},{31,27}} | collective-permute-start | bytes 442376 | tf_op jit(solution)/shard_map/ppermute | solution.py:367
  67.1 9.7 %collective-permute-start.27 = (bf16[576,128]{1,0:T(8,128)(2,1)S(1)}, bf16[576,128]{1,0:T(8,128)(2,1)S(1)}, u32[]{:S(2)}, u32[]{:S(2)}) collective-permute-start(bf16[576,128]{1,0:T(8,128)(2,1)S(1)} %get-tuple-element.167.refs_0_.refs_6_), channel_id=1, source_target_pairs={{0,1},{1,0},{2,3},{3,2},{4,5},{5,4},{6,7},{7,6},{8,9},{9,8},{10,11... | collective-permute-start | bytes 442376 | tf_op jit(solution)/shard_map/ppermute | solution.py:373
  67.6 3.9 %collective-permute-start.21 = (bf16[128,128]{1,0:T(8,128)(2,1)S(1)}, bf16[128,128]{1,0:T(8,128)(2,1)S(1)}, u32[]{:S(2)}, u32[]{:S(2)}) collective-permute-start(bf16[128,128]{1,0:T(8,128)(2,1)S(1)} %forward.3.refs_0_), channel_id=1, source_target_pairs={{0,1},{1,0},{2,3},{3,2},{4,5},{5,4},{6,7},{7,6},{8,9},{9,8},{10,11... | collective-permute-start | bytes 98312 | tf_op jit(solution)/shard_map/ppermute | solution.py:373
  68.6 4.7 %collective-permute-start.22 = (bf16[128,128]{1,0:T(8,128)(2,1)S(1)}, bf16[128,128]{1,0:T(8,128)(2,1)S(1)}, u32[]{:S(2)}, u32[]{:S(2)}) collective-permute-start(bf16[128,128]{1,0:T(8,128)(2,1)S(1)} %forward.3.refs_0_), channel_id=1, source_target_pairs={{0,2},{1,3},{2,0},{3,1},{4,6},{5,7},{6,4},{7,5},{8,10},{9,11},{10,... | collective-permute-start | bytes 98312 | tf_op jit(solution)/shard_map/ppermute | solution.py:373
  68.9 4.4 %collective-permute-start.23 = (bf16[128,128]{1,0:T(8,128)(2,1)S(1)}, bf16[128,128]{1,0:T(8,128)(2,1)S(1)}, u32[]{:S(2)}, u32[]{:S(2)}) collective-permute-start(bf16[128,128]{1,0:T(8,128)(2,1)S(1)} %forward.3.refs_0_), channel_id=1, source_target_pairs={{0,3},{1,2},{2,1},{3,0},{4,7},{5,6},{6,5},{7,4},{8,11},{9,10},{10,... | collective-permute-start | bytes 98312 | tf_op jit(solution)/shard_map/ppermute | solution.py:373
  70.3 8.0 %collective-permute-start.28 = (bf16[576,128]{1,0:T(8,128)(2,1)S(1)}, bf16[576,128]{1,0:T(8,128)(2,1)S(1)}, u32[]{:S(2)}, u32[]{:S(2)}) collective-permute-start(bf16[576,128]{1,0:T(8,128)(2,1)S(1)} %get-tuple-element.167.refs_0_.refs_6_), channel_id=1, source_target_pairs={{0,2},{1,3},{2,0},{3,1},{4,6},{5,7},{6,4},{7,5},{8,10},{9,11},{10,... | collective-permute-start | bytes 442376 | tf_op jit(solution)/shard_map/ppermute | solution.py:373
  71.5 7.8 %collective-permute-start.29 = (bf16[576,128]{1,0:T(8,128)(2,1)S(1)}, bf16[576,128]{1,0:T(8,128)(2,1)S(1)}, u32[]{:S(2)}, u32[]{:S(2)}) collective-permute-start(bf16[576,128]{1,0:T(8,128)(2,1)S(1)} %get-tuple-element.167.refs_0_.refs_6_), channel_id=1, source_target_pairs={{0,3},{1,2},{2,1},{3,0},{4,7},{5,6},{6,5},{7,4},{8,11},{9,10},{10,... | collective-permute-start | bytes 442376 | tf_op jit(solution)/shard_map/ppermute | solution.py:373
  74.2 7.2 %collective-permute-start.24 = (bf16[576,128]{1,0:T(8,128)(2,1)S(1)}, bf16[576,128]{1,0:T(8,128)(2,1)S(1)}, u32[]{:S(2)}, u32[]{:S(2)}) collective-permute-start(bf16[576,128]{1,0:T(8,128)(2,1)S(1)} %get-tuple-element.166), channel_id=1, source_target_pairs={{28,4},{24,0},{29,5},{25,1},{30,6},{26,2},{31,7},{27,3}} | collective-permute-start | bytes 442376 | tf_op jit(solution)/shard_map/ppermute | solution.py:367
  75.5 7.4 %collective-permute-start.25 = (bf16[576,128]{1,0:T(8,128)(2,1)S(1)}, bf16[576,128]{1,0:T(8,128)(2,1)S(1)}, u32[]{:S(2)}, u32[]{:S(2)}) collective-permute-start(bf16[576,128]{1,0:T(8,128)(2,1)S(1)} %get-tuple-element.166), channel_id=1, source_target_pairs={{28,12},{24,8},{29,13},{25,9},{30,14},{26,10},{31,15},{27,11}} | collective-permute-start | bytes 442376 | tf_op jit(solution)/shard_map/ppermute | solution.py:367
  76.8 6.1 %collective-permute-start.26 = (bf16[576,128]{1,0:T(8,128)(2,1)S(1)}, bf16[576,128]{1,0:T(8,128)(2,1)S(1)}, u32[]{:S(2)}, u32[]{:S(2)}) collective-permute-start(bf16[576,128]{1,0:T(8,128)(2,1)S(1)} %get-tuple-element.166), channel_id=1, source_target_pairs={{28,20},{24,16},{29,21},{25,17},{30,22},{26,18},{31,23},{27,19}} | collective-permute-start | bytes 442376 | tf_op jit(solution)/shard_map/ppermute | solution.py:367
  78.3 5.9 %collective-permute-start.33 = (bf16[592,128]{1,0:T(8,128)(2,1)S(1)}, bf16[592,128]{1,0:T(8,128)(2,1)S(1)}, u32[]{:S(2)}, u32[]{:S(2)}) collective-permute-start(bf16[592,128]{1,0:T(8,128)(2,1)S(1)} %get-tuple-element.174), channel_id=1, source_target_pairs={{0,1},{1,0},{2,3},{3,2},{4,5},{5,4},{6,7},{7,6},{8,9},{9,8},{10,11... | collective-permute-start | bytes 454664 | tf_op jit(solution)/shard_map/ppermute | solution.py:373
  79.4 6.3 %collective-permute-start.34 = (bf16[592,128]{1,0:T(8,128)(2,1)S(1)}, bf16[592,128]{1,0:T(8,128)(2,1)S(1)}, u32[]{:S(2)}, u32[]{:S(2)}) collective-permute-start(bf16[592,128]{1,0:T(8,128)(2,1)S(1)} %get-tuple-element.175), channel_id=1, source_target_pairs={{0,2},{1,3},{2,0},{3,1},{4,6},{5,7},{6,4},{7,5},{8,10},{9,11},{10,... | collective-permute-start | bytes 454664 | tf_op jit(solution)/shard_map/ppermute | solution.py:373
  81.4 5.0 %collective-permute-start.35 = (bf16[592,128]{1,0:T(8,128)(2,1)S(1)}, bf16[592,128]{1,0:T(8,128)(2,1)S(1)}, u32[]{:S(2)}, u32[]{:S(2)}) collective-permute-start(bf16[592,128]{1,0:T(8,128)(2,1)S(1)} %get-tuple-element.176), channel_id=1, source_target_pairs={{0,3},{1,2},{2,1},{3,0},{4,7},{5,6},{6,5},{7,4},{8,11},{9,10},{10,... | collective-permute-start | bytes 454664 | tf_op jit(solution)/shard_map/ppermute | solution.py:373
  82.9 6.9 %collective-permute-start.30 = (bf16[576,128]{1,0:T(8,128)(2,1)S(1)}, bf16[576,128]{1,0:T(8,128)(2,1)S(1)}, u32[]{:S(2)}, u32[]{:S(2)}) collective-permute-start(bf16[576,128]{1,0:T(8,128)(2,1)S(1)} %add_add_fusion.1.refs_0_), channel_id=1, source_target_pairs={{0,1},{1,0},{2,3},{3,2},{4,5},{5,4},{6,7},{7,6},{8,9},{9,8},{10,11... | collective-permute-start | bytes 442376 | tf_op jit(solution)/shard_map/ppermute | solution.py:373
  84.0 5.8 %collective-permute-start.31 = (bf16[576,128]{1,0:T(8,128)(2,1)S(1)}, bf16[576,128]{1,0:T(8,128)(2,1)S(1)}, u32[]{:S(2)}, u32[]{:S(2)}) collective-permute-start(bf16[576,128]{1,0:T(8,128)(2,1)S(1)} %add_add_fusion.1.refs_0_), channel_id=1, source_target_pairs={{0,2},{1,3},{2,0},{3,1},{4,6},{5,7},{6,4},{7,5},{8,10},{9,11},{10,... | collective-permute-start | bytes 442376 | tf_op jit(solution)/shard_map/ppermute | solution.py:373
  84.2 7.0 %collective-permute-start.32 = (bf16[576,128]{1,0:T(8,128)(2,1)S(1)}, bf16[576,128]{1,0:T(8,128)(2,1)S(1)}, u32[]{:S(2)}, u32[]{:S(2)}) collective-permute-start(bf16[576,128]{1,0:T(8,128)(2,1)S(1)} %add_add_fusion.1.refs_0_), channel_id=1, source_target_pairs={{0,3},{1,2},{2,1},{3,0},{4,7},{5,6},{6,5},{7,4},{8,11},{9,10},{10,... | collective-permute-start | bytes 442376 | tf_op jit(solution)/shard_map/ppermute | solution.py:373
  91.8 7.7 %collective-permute-start.38 = (bf16[2304,128]{1,0:T(8,128)(2,1)S(1)}, bf16[2304,128]{1,0:T(8,128)(2,1)S(1)}, u32[]{:S(2)}, u32[]{:S(2)}) collective-permute-start(bf16[2304,128]{1,0:T(8,128)(2,1)S(1)} %assemble.2.h_ref), channel_id=1, source_target_pairs={{0,4},{4,0},{8,12},{12,8},{16,20},{20,16},{24,28},{28,24},{1,5},{5... | collective-permute-start | bytes 1769480 | tf_op jit(solution)/shard_map/ppermute | solution.py:367
  101.3 5.8 %collective-permute-start.39 = (bf16[2368,128]{1,0:T(8,128)(2,1)S(1)}, bf16[2368,128]{1,0:T(8,128)(2,1)S(1)}, u32[]{:S(2)}, u32[]{:S(2)}) collective-permute-start(bf16[2368,128]{1,0:T(8,128)(2,1)S(1)} %get-tuple-element.191), channel_id=1, source_target_pairs={{0,4},{4,0},{8,12},{12,8},{16,20},{20,16},{24,28},{28,24},{1,5},{5... | collective-permute-start | bytes 1818632 | tf_op jit(solution)/shard_map/ppermute | solution.py:367
  101.8 5.2 %collective-permute-start.37 = (bf16[576,128]{1,0:T(8,128)(2,1)S(1)}, bf16[576,128]{1,0:T(8,128)(2,1)S(1)}, u32[]{:S(2)}, u32[]{:S(2)}) collective-permute-start(bf16[576,128]{1,0:T(8,128)(2,1)S(1)} %back_out.2.even_ref), channel_id=1, source_target_pairs={{4,0},{8,4},{12,8},{16,12},{20,16},{24,20},{28,24},{5,1},{9,5},{13... | collective-permute-start | bytes 442376 | tf_op jit(solution)/shard_map/ppermute | solution.py:367
  107.8 4.1 %collective-permute-start.40 = (bf16[592,128]{1,0:T(8,128)(2,1)S(1)}, bf16[592,128]{1,0:T(8,128)(2,1)S(1)}, u32[]{:S(2)}, u32[]{:S(2)}) collective-permute-start(bf16[592,128]{1,0:T(8,128)(2,1)S(1)} %get-tuple-element.193), channel_id=1, source_target_pairs={{0,1},{1,0},{2,3},{3,2},{4,5},{5,4},{6,7},{7,6},{8,9},{9,8},{10,11... | collective-permute-start | bytes 454664 | tf_op jit(solution)/shard_map/ppermute | solution.py:373
  108.3 4.0 %collective-permute-start.41 = (bf16[592,128]{1,0:T(8,128)(2,1)S(1)}, bf16[592,128]{1,0:T(8,128)(2,1)S(1)}, u32[]{:S(2)}, u32[]{:S(2)}) collective-permute-start(bf16[592,128]{1,0:T(8,128)(2,1)S(1)} %get-tuple-element.194), channel_id=1, source_target_pairs={{0,2},{1,3},{2,0},{3,1},{4,6},{5,7},{6,4},{7,5},{8,10},{9,11},{10,... | collective-permute-start | bytes 454664 | tf_op jit(solution)/shard_map/ppermute | solution.py:373
  109.3 4.9 %collective-permute-start.42 = (bf16[592,128]{1,0:T(8,128)(2,1)S(1)}, bf16[592,128]{1,0:T(8,128)(2,1)S(1)}, u32[]{:S(2)}, u32[]{:S(2)}) collective-permute-start(bf16[592,128]{1,0:T(8,128)(2,1)S(1)} %get-tuple-element.195), channel_id=1, source_target_pairs={{0,3},{1,2},{2,1},{3,0},{4,7},{5,6},{6,5},{7,4},{8,11},{9,10},{10,... | collective-permute-start | bytes 454664 | tf_op jit(solution)/shard_map/ppermute | solution.py:373
  114.8 5.3 %collective-permute-start.43 = (bf16[576,128]{1,0:T(8,128)(2,1)S(1)}, bf16[576,128]{1,0:T(8,128)(2,1)S(1)}, u32[]{:S(2)}, u32[]{:S(2)}) collective-permute-start(bf16[576,128]{1,0:T(8,128)(2,1)S(1)} %get-tuple-element.197), channel_id=1, source_target_pairs={{0,1},{1,0},{2,3},{3,2},{4,5},{5,4},{6,7},{7,6},{8,9},{9,8},{10,11... | collective-permute-start | bytes 442376 | tf_op jit(solution)/shard_map/ppermute | solution.py:373
  115.7 5.8 %collective-permute-start.44 = (bf16[576,128]{1,0:T(8,128)(2,1)S(1)}, bf16[576,128]{1,0:T(8,128)(2,1)S(1)}, u32[]{:S(2)}, u32[]{:S(2)}) collective-permute-start(bf16[576,128]{1,0:T(8,128)(2,1)S(1)} %get-tuple-element.198), channel_id=1, source_target_pairs={{0,2},{1,3},{2,0},{3,1},{4,6},{5,7},{6,4},{7,5},{8,10},{9,11},{10,... | collective-permute-start | bytes 442376 | tf_op jit(solution)/shard_map/ppermute | solution.py:373
  116.5 5.1 %collective-permute-start.45 = (bf16[576,128]{1,0:T(8,128)(2,1)S(1)}, bf16[576,128]{1,0:T(8,128)(2,1)S(1)}, u32[]{:S(2)}, u32[]{:S(2)}) collective-permute-start(bf16[576,128]{1,0:T(8,128)(2,1)S(1)} %get-tuple-element.199), channel_id=1, source_target_pairs={{0,3},{1,2},{2,1},{3,0},{4,7},{5,6},{6,5},{7,4},{8,11},{9,10},{10,... | collective-permute-start | bytes 442376 | tf_op jit(solution)/shard_map/ppermute | solution.py:373
  117.6 8.8 %collective-permute-start.46 = (bf16[592,128]{1,0:T(8,128)(2,1)S(1)}, bf16[592,128]{1,0:T(8,128)(2,1)S(1)}, u32[]{:S(2)}, u32[]{:S(2)}) collective-permute-start(bf16[592,128]{1,0:T(8,128)(2,1)S(1)} %sum.2.refs_0_), channel_id=1, source_target_pairs={{0,24},{4,28},{1,25},{5,29},{2,26},{6,30},{3,27},{7,31}} | collective-permute-start | bytes 454664 | tf_op jit(solution)/shard_map/ppermute | solution.py:367
  118.8 8.8 %collective-permute-start.47 = (bf16[592,128]{1,0:T(8,128)(2,1)S(1)}, bf16[592,128]{1,0:T(8,128)(2,1)S(1)}, u32[]{:S(2)}, u32[]{:S(2)}) collective-permute-start(bf16[592,128]{1,0:T(8,128)(2,1)S(1)} %sum.2.refs_0_), channel_id=1, source_target_pairs={{8,24},{12,28},{9,25},{13,29},{10,26},{14,30},{11,27},{15,31}} | collective-permute-start | bytes 454664 | tf_op jit(solution)/shard_map/ppermute | solution.py:367
  120.2 8.8 %collective-permute-start.48 = (bf16[592,128]{1,0:T(8,128)(2,1)S(1)}, bf16[592,128]{1,0:T(8,128)(2,1)S(1)}, u32[]{:S(2)}, u32[]{:S(2)}) collective-permute-start(bf16[592,128]{1,0:T(8,128)(2,1)S(1)} %sum.2.refs_0_), channel_id=1, source_target_pairs={{16,24},{20,28},{17,25},{21,29},{18,26},{22,30},{19,27},{23,31}} | collective-permute-start | bytes 454664 | tf_op jit(solution)/shard_map/ppermute | solution.py:367
  129.6 9.0 %collective-permute-start.52 = (bf16[592,128]{1,0:T(8,128)(2,1)S(1)}, bf16[592,128]{1,0:T(8,128)(2,1)S(1)}, u32[]{:S(2)}, u32[]{:S(2)}) collective-permute-start(bf16[592,128]{1,0:T(8,128)(2,1)S(1)} %sum.3.total_ref), channel_id=1, source_target_pairs={{24,28},{25,29},{26,30},{27,31}} | collective-permute-start | bytes 454664 | tf_op jit(solution)/shard_map/ppermute | solution.py:367
  130.9 11.3 %collective-permute-start.49 = (bf16[576,128]{1,0:T(8,128)(2,1)S(1)}, bf16[576,128]{1,0:T(8,128)(2,1)S(1)}, u32[]{:S(2)}, u32[]{:S(2)}) collective-permute-start(bf16[576,128]{1,0:T(8,128)(2,1)S(1)} %add_convert_fusion.refs_0_), channel_id=1, source_target_pairs={{8,0},{4,28},{9,1},{5,29},{10,2},{6,30},{11,3},{7,31}} | collective-permute-start | bytes 442376 | tf_op jit(solution)/shard_map/ppermute | solution.py:367
  132.2 10.8 %collective-permute-start.50 = (bf16[576,128]{1,0:T(8,128)(2,1)S(1)}, bf16[576,128]{1,0:T(8,128)(2,1)S(1)}, u32[]{:S(2)}, u32[]{:S(2)}) collective-permute-start(bf16[576,128]{1,0:T(8,128)(2,1)S(1)} %add_convert_fusion.refs_0_), channel_id=1, source_target_pairs={{16,0},{12,28},{17,1},{13,29},{18,2},{14,30},{19,3},{15,31}} | collective-permute-start | bytes 442376 | tf_op jit(solution)/shard_map/ppermute | solution.py:367
  133.5 9.5 %collective-permute-start.51 = (bf16[576,128]{1,0:T(8,128)(2,1)S(1)}, bf16[576,128]{1,0:T(8,128)(2,1)S(1)}, u32[]{:S(2)}, u32[]{:S(2)}) collective-permute-start(bf16[576,128]{1,0:T(8,128)(2,1)S(1)} %add_convert_fusion.refs_0_), channel_id=1, source_target_pairs={{24,0},{20,28},{25,1},{21,29},{26,2},{22,30},{27,3},{23,31}} | collective-permute-start | bytes 442376 | tf_op jit(solution)/shard_map/ppermute | solution.py:367
  147.5 10.4 %collective-permute-start.56 = (bf16[592,128]{1,0:T(8,128)(2,1)S(1)}, bf16[592,128]{1,0:T(8,128)(2,1)S(1)}, u32[]{:S(2)}, u32[]{:S(2)}) collective-permute-start(bf16[592,128]{1,0:T(8,128)(2,1)S(1)} %get-tuple-element.223), channel_id=1, source_target_pairs={{0,1},{1,0},{2,3},{3,2},{4,5},{5,4},{6,7},{7,6},{8,9},{9,8},{10,11... | collective-permute-start | bytes 454664 | tf_op jit(solution)/shard_map/ppermute | solution.py:373
  147.5 10.3 %collective-permute-start.57 = (bf16[592,128]{1,0:T(8,128)(2,1)S(1)}, bf16[592,128]{1,0:T(8,128)(2,1)S(1)}, u32[]{:S(2)}, u32[]{:S(2)}) collective-permute-start(bf16[592,128]{1,0:T(8,128)(2,1)S(1)} %get-tuple-element.224), channel_id=1, source_target_pairs={{0,2},{1,3},{2,0},{3,1},{4,6},{5,7},{6,4},{7,5},{8,10},{9,11},{10,... | collective-permute-start | bytes 454664 | tf_op jit(solution)/shard_map/ppermute | solution.py:373
  148.4 9.4 %collective-permute-start.58 = (bf16[592,128]{1,0:T(8,128)(2,1)S(1)}, bf16[592,128]{1,0:T(8,128)(2,1)S(1)}, u32[]{:S(2)}, u32[]{:S(2)}) collective-permute-start(bf16[592,128]{1,0:T(8,128)(2,1)S(1)} %get-tuple-element.225), channel_id=1, source_target_pairs={{0,3},{1,2},{2,1},{3,0},{4,7},{5,6},{6,5},{7,4},{8,11},{9,10},{10,... | collective-permute-start | bytes 454664 | tf_op jit(solution)/shard_map/ppermute | solution.py:373
  150.9 6.9 %collective-permute-start.59 = (f32[16,128]{1,0:T(8,128)S(1)}, f32[16,128]{1,0:T(8,128)S(1)}, u32[]{:S(2)}, u32[]{:S(2)}) collective-permute-start(f32[16,128]{1,0:T(8,128)S(1)} %constant_dynamic-update-slice_fusion), channel_id=1, source_target_pairs={{28,24},{29,25},{30,26},{31,27}} | collective-permute-start | bytes 24584 | tf_op jit(solution)/shard_map/ppermute | solution.py:367
  159.9 9.8 %collective-permute-start.62 = (bf16[576,128]{1,0:T(8,128)(2,1)S(1)}, bf16[576,128]{1,0:T(8,128)(2,1)S(1)}, u32[]{:S(2)}, u32[]{:S(2)}) collective-permute-start(bf16[576,128]{1,0:T(8,128)(2,1)S(1)} %get-tuple-element.240), channel_id=1, source_target_pairs={{0,8},{4,12},{1,9},{5,13},{2,10},{6,14},{3,11},{7,15}} | collective-permute-start | bytes 442376 | tf_op jit(solution)/shard_map/ppermute | solution.py:367
  160.6 10.4 %collective-permute-start.63 = (bf16[576,128]{1,0:T(8,128)(2,1)S(1)}, bf16[576,128]{1,0:T(8,128)(2,1)S(1)}, u32[]{:S(2)}, u32[]{:S(2)}) collective-permute-start(bf16[576,128]{1,0:T(8,128)(2,1)S(1)} %get-tuple-element.240), channel_id=1, source_target_pairs={{0,16},{4,20},{1,17},{5,21},{2,18},{6,22},{3,19},{7,23}} | collective-permute-start | bytes 442376 | tf_op jit(solution)/shard_map/ppermute | solution.py:367
  161.2 12.9 %collective-permute-start.64 = (bf16[576,128]{1,0:T(8,128)(2,1)S(1)}, bf16[576,128]{1,0:T(8,128)(2,1)S(1)}, u32[]{:S(2)}, u32[]{:S(2)}) collective-permute-start(bf16[576,128]{1,0:T(8,128)(2,1)S(1)} %get-tuple-element.240), channel_id=1, source_target_pairs={{0,24},{4,28},{1,25},{5,29},{2,26},{6,30},{3,27},{7,31}} | collective-permute-start | bytes 442376 | tf_op jit(solution)/shard_map/ppermute | solution.py:367
  162.5 12.6 %collective-permute-start.68 = (f32[16,128]{1,0:T(8,128)S(1)}, f32[16,128]{1,0:T(8,128)S(1)}, u32[]{:S(2)}, u32[]{:S(2)}) collective-permute-start(f32[16,128]{1,0:T(8,128)S(1)} %add.61), channel_id=1, source_target_pairs={{28,4},{24,0},{29,5},{25,1},{30,6},{26,2},{31,7},{27,3}} | collective-permute-start | bytes 24584 | tf_op jit(solution)/shard_map/ppermute | solution.py:367
  168.3 7.8 %collective-permute-start.69 = (f32[16,128]{1,0:T(8,128)S(1)}, f32[16,128]{1,0:T(8,128)S(1)}, u32[]{:S(2)}, u32[]{:S(2)}) collective-permute-start(f32[16,128]{1,0:T(8,128)S(1)} %add.61), channel_id=1, source_target_pairs={{28,12},{24,8},{29,13},{25,9},{30,14},{26,10},{31,15},{27,11}} | collective-permute-start | bytes 24584 | tf_op jit(solution)/shard_map/ppermute | solution.py:367
  169.7 7.3 %collective-permute-start.70 = (f32[16,128]{1,0:T(8,128)S(1)}, f32[16,128]{1,0:T(8,128)S(1)}, u32[]{:S(2)}, u32[]{:S(2)}) collective-permute-start(f32[16,128]{1,0:T(8,128)S(1)} %add.61), channel_id=1, source_target_pairs={{28,20},{24,16},{29,21},{25,17},{30,22},{26,18},{31,23},{27,19}} | collective-permute-start | bytes 24584 | tf_op jit(solution)/shard_map/ppermute | solution.py:367
  171.0 7.3 %collective-permute-start.60 = (bf16[576,128]{1,0:T(8,128)(2,1)S(1)}, bf16[576,128]{1,0:T(8,128)(2,1)S(1)}, u32[]{:S(2)}, u32[]{:S(2)}) collective-permute-start(bf16[576,128]{1,0:T(8,128)(2,1)S(1)} %back_out.3), channel_id=1, source_target_pairs={{4,0},{8,4},{12,8},{16,12},{20,16},{24,20},{28,24},{5,1},{9,5},{13... | collective-permute-start | bytes 442376 | tf_op jit(solution)/shard_map/ppermute | solution.py:367
  174.2 5.5 %collective-permute-start.65 = (bf16[576,128]{1,0:T(8,128)(2,1)S(1)}, bf16[576,128]{1,0:T(8,128)(2,1)S(1)}, u32[]{:S(2)}, u32[]{:S(2)}) collective-permute-start(bf16[576,128]{1,0:T(8,128)(2,1)S(1)} %add_add_fusion.refs_0_), channel_id=1, source_target_pairs={{0,1},{1,0},{2,3},{3,2},{4,5},{5,4},{6,7},{7,6},{8,9},{9,8},{10,11... | collective-permute-start | bytes 442376 | tf_op jit(solution)/shard_map/ppermute | solution.py:373
  175.2 5.4 %collective-permute-start.66 = (bf16[576,128]{1,0:T(8,128)(2,1)S(1)}, bf16[576,128]{1,0:T(8,128)(2,1)S(1)}, u32[]{:S(2)}, u32[]{:S(2)}) collective-permute-start(bf16[576,128]{1,0:T(8,128)(2,1)S(1)} %add_add_fusion.refs_0_), channel_id=1, source_target_pairs={{0,2},{1,3},{2,0},{3,1},{4,6},{5,7},{6,4},{7,5},{8,10},{9,11},{10,... | collective-permute-start | bytes 442376 | tf_op jit(solution)/shard_map/ppermute | solution.py:373
  176.2 7.1 %collective-permute-start.67 = (bf16[576,128]{1,0:T(8,128)(2,1)S(1)}, bf16[576,128]{1,0:T(8,128)(2,1)S(1)}, u32[]{:S(2)}, u32[]{:S(2)}) collective-permute-start(bf16[576,128]{1,0:T(8,128)(2,1)S(1)} %add_add_fusion.refs_0_), channel_id=1, source_target_pairs={{0,3},{1,2},{2,1},{3,0},{4,7},{5,6},{6,5},{7,4},{8,11},{9,10},{10,... | collective-permute-start | bytes 442376 | tf_op jit(solution)/shard_map/ppermute | solution.py:373
  (21 other events, 121.1 us)

commit v4 on v3

--- a/solution.py
+++ b/solution.py
@@ -303,9 +303,19 @@
     add_terms(total_of(refs[:-1]), refs[-1])
 
 
+def sum_chips_kernel(here, *refs):
+    parts, (out, sums_ref) = refs[:-2], refs[-2:]
+    total = total_of(parts)
+    add_terms(total, out)
+    rest, _, raw_hit = join_rows(total[out.shape[0] - EXTRA :, :], 3)
+    place = lax.broadcasted_iota(jnp.int32, sums_ref.shape, 0)
+    sums = jnp.where(place == 0, rest, jnp.where(place == 1, raw_hit, 0.0))
+    sums_ref[...] = jnp.where(here[2] >= here[3] - 2, sums, 0.0)
+
+
 def cot_kernel(full, here, total_ref, scale_ref, h_ref, gain_ref, *refs):
-    found, (out, sums_ref) = refs[:-2], refs[-2:]
-    size, rows = h_ref.shape
+    found, out = refs[:-1], refs[-1]
+    size = h_ref.shape[0]
     gain = gain_ref[block_of(here, 0, size), :].astype(F32)
     rest, weighted, raw_hit = join_rows(total_ref[size:, :].astype(F32), 3)
     capped = jnp.tanh(raw_hit / LOGIT_CAP)
@@ -317,41 +327,36 @@
     out[...] = (
         scale * gain * dhid - h_ref[...].astype(F32) * (scale * scale * stat / full)
     ).astype(BF16)
-    place = lax.broadcasted_iota(jnp.int32, (8, rows), 0)
-    sums = jnp.where(place == 0, rest, jnp.where(place == 1, raw_hit, 0.0))
-    sums_ref[...] = jnp.where(here[2] == here[3] - 1, sums, 0.0)
-
-
-def grad_kernel(ticks, emb_scale, here, ids_ref, targets_ref, sums_ref, *refs):
+
+
+def grad_kernel(ticks, emb_scale, here, ids_ref, targets_ref, *refs):
     out, loss_ref = refs[-2:]
-    vocab, rows = refs[0].shape
+    vocab, rows = refs[1].shape
     column = here[1] + lax.broadcasted_iota(jnp.int32, (vocab, rows), 0)
     place = lax.broadcasted_iota(jnp.int32, loss_ref.shape, 0)
     losses = jnp.zeros(loss_ref.shape, F32)
-    for t in range(ticks):
-        rest, raw_hit = sums_ref[8 * t : 8 * t + 1, :], sums_ref[8 * t + 1 : 8 * t + 2, :]
-        logit = LOGIT_CAP * jnp.tanh(raw_hit / LOGIT_CAP)
-        loss = jnp.mean(jnp.log(rest + jnp.exp(logit)) - logit, axis=1, keepdims=True)
-        losses = jnp.where(place == t, jnp.broadcast_to(loss, losses.shape), losses)
-    loss_ref[...] = losses
     dlogs, hits = [], []
     for flip in range(2):
         first = here[2] % 2 == flip
-        sums = jnp.where(first, sums_ref[0:8, :], sums_ref[8:16, :])
-        rest, raw_hit = sums[0:1, :], sums[1:2, :]
-        whole = rest + jnp.exp(LOGIT_CAP * jnp.tanh(raw_hit / LOGIT_CAP))
-        capped = jnp.tanh(refs[3 * flip][...] / LOGIT_CAP)
+        rest, raw_hit = refs[4 * flip][0:1, :], refs[4 * flip][1:2, :]
+        logit = LOGIT_CAP * jnp.tanh(raw_hit / LOGIT_CAP)
+        whole = rest + jnp.exp(logit)
+        loss = jnp.mean(jnp.log(whole) - logit, axis=1, keepdims=True)
+        tick = jnp.where(first, 0, 1)
+        losses = jnp.where(place == tick, jnp.broadcast_to(loss, losses.shape), losses)
+        capped = jnp.tanh(refs[4 * flip + 1][...] / LOGIT_CAP)
         hit = column == jnp.where(first, targets_ref[0:1, :], targets_ref[1:2, :])
         top = jnp.where(hit, -rest, jnp.exp(LOGIT_CAP * capped))
         dlogs.append((top / whole * (1.0 - capped * capped)).astype(BF16))
         hit = column == jnp.where(first, ids_ref[0:1, :], ids_ref[1:2, :])
         hits.append(hit.astype(F32).astype(BF16))
+    loss_ref[...] = losses
     full = out.shape[1]
     step = 256 if full % 256 == 0 else full
     for at in range(0, full, step):
         cut = slice(at, at + step)
-        looked = sum(dot(hits[i], refs[3 * i + 2][cut, :], 1, 1) for i in range(2))
-        heads = sum(dot(dlogs[i], refs[3 * i + 1][cut, :], 1, 1) for i in range(2))
+        looked = sum(dot(hits[i], refs[4 * i + 3][cut, :], 1, 1) for i in range(2))
+        heads = sum(dot(dlogs[i], refs[4 * i + 2][cut, :], 1, 1) for i in range(2))
         out[:, cut] = (heads + looked * emb_scale).astype(BF16)
 
 
@@ -560,18 +565,20 @@
     total = call(sum_kernel, [message], [here, *swap(terms)], "sum")
     found1 = rows_of_tick(after(found[n:], total))
     total = after(to_chips(total, last - 1, last), found1)
-    total = call(sum_kernel, [message], [here, *total], "sum")
+    total, sums = call(
+        sum_chips_kernel, [message, ((8, rows), F32)], [here, *total], "sum_chips"
+    )
     looked1 = to_chips(after(found1, total), 0, last)
 
     def cot_of(total, scale, h, looked):
         return call(
             functools.partial(cot_kernel, full),
-            [act, ((8, rows), F32)],
+            [act],
             [here, total, scale, h, fgain, *looked],
             "cot",
         )
 
-    cot0, sums0 = cot_of(hop(total, [(last - 1, last)]), scale_b, y0, looked0)
+    cot0 = cot_of(hop(total, [(last - 1, last)]), scale_b, y0, looked0)
 
     cot_parts = call(
         functools.partial(parts_kernel, n, piece),
@@ -580,12 +587,12 @@
         "parts",
     )
     terms1 = back(after(swap(cot_parts), looked1), saved1)
-    cot1, sums1 = cot_of(after(total, terms1[0]), scale_a, y1, looked1)
-    sums = jnp.concatenate([sums0, sums1], axis=0)
-    sums = sums + hop(sums, [(last, last - 1)])
-    gin1 = back_out(after(swap(terms1), sums), saved1, held1, acts, cots1, cot0)
+    cot1 = cot_of(after(total, terms1[0]), scale_a, y1, looked1)
+    sums = after(sums, cot_parts)
+    sums_a = from_chip(sums, sums, last)
+    gin1 = back_out(after(swap(terms1), cot1, sums_a), saved1, held1, acts, cots1, cot0)
     g_send, g_own = call(pick_kernel, [act] * 2, [here, gin0, hop(gin1, [(0, 1)])], "pick")
-    sums = from_chip(sums, sums, last)
+    sums_b = other_core(after(sums_a, g_send))
     leaving_a = share(from_chip(g_own, g_send, 0))
     gin1_down = hop(gin1, down)
     acts2 = call(
@@ -594,16 +601,16 @@
         [here, y1_up, *after(looked1, gin1)],
         "enter",
     )
-    leaving_a = assemble(after(leaving_a, acts2, sums, gin1_down))
+    leaving_a = assemble(after(leaving_a, acts2, sums_b, gin1_down))
     leaving_b = other_core(leaving_a)
     cots2 = call(last_cots_kernel, [act], [here, after(gin1_down, leaving_a), cot1], "last_cots")
     grad, losses = call(
         functools.partial(grad_kernel, ticks, emb_scale),
         [((vocab, full), BF16), ((8, rows), F32)],
         [
-            *(here, back_ids, targets, sums),
-            *(raw_a, normed_a, leaving_a),
-            *(raw_b, normed_b, after(leaving_b, cots2)),
+            *(here, back_ids, targets),
+            *(sums_a, raw_a, normed_a, leaving_a),
+            *(sums_b, raw_b, normed_b, after(leaving_b, cots2)),
         ],
         "grad",
         8 * full * rows * vocab,

time: 192 us -> 192 us (level)
  starting transfers between devices: 94.1 us -> 87.4 us
  waiting for transfers between devices: 54.2 us -> 59.9 us
    ppermute x30, starting transfers between devices: 55.4 us -> 48.7 us  [hop(): return lax.ppermute(x, 'section', pairs)]
    ppermute x30, waiting for transfers between devices: 18.4 us -> 24.9 us  [hop(): return lax.ppermute(x, 'section', pairs)]
    unnamed x27 -> x26, local copies, waits for them, and re-layouts: 5.46 us -> 5.46 us
  transfers between devices with their start and end apart: 72 -> 72, of which waited for: 32 -> 30; matrix products, arithmetic and copies ran while one was open for 0% -> 0% of each run, Pallas kernels for 10% -> 11%
where the time goes in v4:
time: 192 us; the launch traced here: 190 us
  starting transfers between devices  87.4 us (46%)
  waiting for transfers between devices  59.9 us (31%)
  Pallas kernels  33.9 us (18%)
  local copies, waits for them, and re-layouts  6.81 us (4%)
    ppermute x30, starting transfers between devices, hop(): return lax.ppermute(x, 'section', pairs)  48.7 us
    ppermute x42, starting transfers between devices, swap(): lax.ppermute(blocks[d], 'tensor', [(i, i ^ d) for i in range(n)])  38.7 us
    ppermute x42, waiting for transfers between devices, swap(): lax.ppermute(blocks[d], 'tensor', [(i, i ^ d) for i in range(n)])  35 us
    pallas_call x28, Pallas kernels, call(): pl.pallas_call(body, out_shape=[jax.ShapeDtypeStruct(s, d) for s, d in ou...  33.9 us
    ppermute x30, waiting for transfers between devices, hop(): return lax.ppermute(x, 'section', pairs)  24.9 us
    unnamed x26, local copies, waits for them, and re-layouts  5.46 us
  transfers between devices with their start and end apart: 72, of which 30 were waited for; matrix products, arithmetic and copies ran while one was open for 0% of the time, Pallas kernels for 11%

profile of v4, /device:TPU:29, one launch (start us, length us, event | category | flops | bytes accessed | tf_op | source)
XLA Modules:
  0.0 189.6 jit_solution(7588899066692289415)
XLA Ops:
  5.2 1.4 copy-done.1
  8.0 2.0 %lookup.1 = (bf16[2304,256]{1,0:T(8,128)(2,1)S(1)}, bf16[2304,256]{1,0:T(8,128)(2,1)S(1)}, bf16[2304,256]{1,0:T(8,128)(2,1)S(1)}) custom-call(s32[4]{0:T(128)S(1)} %pad_add_fusion.here, s32[2,128]{1,0:T(2,128)S(1)} %copy-done.11, s32[2,128]{1,0:T(2,128)S(1)} %copy-done.7, bf16[256,2304]{1,0:T(8,128)(2,1)S(1)} %copy-done.1), custom_call_target="tpu_custom_call" | custom-call | flops 603979776 | bytes 4720656 | tf_op jit(solution)/shard_map/lookup/pallas_call | solution.py:27
  13.3 5.9 %collective-permute-done.refs_1_.refs_5_ = bf16[1152,128]{1,0:T(8,128)(2,1)S(1)} collective-permute-done((bf16[1152,128]{1,0:T(8,128)(2,1)S(1)}, bf16[1152,128]{1,0:T(8,128)(2,1)S(1)}, u32[]{:S(2)}, u32[]{:S(2)}) %collective-permute-start) | collective-permute-done | bytes 294944 | tf_op jit(solution)/shard_map/ppermute | solution.py:378
  19.3 7.2 %collective-permute-done.1.refs_2_.refs_6_ = bf16[1152,128]{1,0:T(8,128)(2,1)S(1)} collective-permute-done((bf16[1152,128]{1,0:T(8,128)(2,1)S(1)}, bf16[1152,128]{1,0:T(8,128)(2,1)S(1)}, u32[]{:S(2)}, u32[]{:S(2)}) %collective-permute-start.1) | collective-permute-done | bytes 294944 | tf_op jit(solution)/shard_map/ppermute | solution.py:378
  26.5 2.0 %forward.2 = (bf16[256,128]{1,0:T(8,128)(2,1)S(1)}, bf16[256,128]{1,0:T(8,128)(2,1)S(1)}, bf16[256,128]{1,0:T(8,128)(2,1)S(1)}, bf16[256,128]{1,0:T(8,128)(2,1)S(1)}) custom-call(s32[4]{0:T(128)S(1)} %pad_add_fusion.here, bf16[1152,128]{1,0:T(8,128)(2,1)S(1)} %get-tuple-element.129.refs_0_.refs_4_, ...), custom_call_target="tpu_custom_call" | custom-call | flops 234881024 | bytes 3948560 | tf_op jit(solution)/shard_map/forward/pallas_call | solution.py:27
  32.0 2.2 %collective-permute-done.5.refs_3_ = bf16[256,128]{1,0:T(8,128)(2,1)S(1)} collective-permute-done((bf16[256,128]{1,0:T(8,128)(2,1)S(1)}, bf16[256,128]{1,0:T(8,128)(2,1)S(1)}, u32[]{:S(2)}, u32[]{:S(2)}) %collective-permute-start.5) | collective-permute-done | bytes 65568 | tf_op jit(solution)/shard_map/ppermute | solution.py:378
  34.2 1.6 layer_out.2
  39.3 1.3 collective-permute-start.6
  41.6 1.7 collective-permute-done.8
  43.7 1.3 collective-permute-start.11
  45.1 1.3 collective-permute-start.12
  46.4 1.3 collective-permute-start.13
  49.1 2.5 %collective-permute-done.11.refs_1_ = bf16[576,128]{1,0:T(8,128)(2,1)S(1)} collective-permute-done((bf16[576,128]{1,0:T(8,128)(2,1)S(1)}, bf16[576,128]{1,0:T(8,128)(2,1)S(1)}, u32[]{:S(2)}, u32[]{:S(2)}) %collective-permute-start.11) | collective-permute-done | bytes 147488 | tf_op jit(solution)/shard_map/ppermute | solution.py:372
  53.1 1.5 collective-permute-done.13.refs_3_
  55.2 1.5 collective-permute-start.15
  56.7 1.3 collective-permute-start.17
  58.0 4.1 %collective-permute-start.14 = (bf16[576,128]{1,0:T(8,128)(2,1)S(1)}, bf16[576,128]{1,0:T(8,128)(2,1)S(1)}, u32[]{:S(2)}, u32[]{:S(2)}) collective-permute-start(bf16[576,128]{1,0:T(8,128)(2,1)S(1)} %get-tuple-element.138.h_ref), channel_id=1, source_target_pairs={{28,24},{29,25},{30,26},{31,27}} | collective-permute-start | bytes 442376 | tf_op jit(solution)/shard_map/ppermute | solution.py:372
  62.1 1.6 recompute.2
  63.7 1.5 back.2
  65.3 1.8 forward.3.refs_0_
  68.9 1.3 collective-permute-start.23
  71.5 1.8 collective-permute-start.29
  74.2 1.3 collective-permute-start.24
  75.5 1.3 collective-permute-start.25
  76.8 1.5 collective-permute-start.26
  79.6 1.8 recompute.3
  81.4 1.5 collective-permute-start.35
  84.2 1.4 collective-permute-start.32
  87.1 2.7 %collective-permute-done.30.refs_1_ = bf16[576,128]{1,0:T(8,128)(2,1)S(1)} collective-permute-done((bf16[576,128]{1,0:T(8,128)(2,1)S(1)}, bf16[576,128]{1,0:T(8,128)(2,1)S(1)}, u32[]{:S(2)}, u32[]{:S(2)}) %collective-permute-start.30) | collective-permute-done | bytes 147488 | tf_op jit(solution)/shard_map/ppermute | solution.py:378
  89.8 1.4 collective-permute-done.32.refs_3_
  91.8 6.1 %collective-permute-start.38 = (bf16[2304,128]{1,0:T(8,128)(2,1)S(1)}, bf16[2304,128]{1,0:T(8,128)(2,1)S(1)}, u32[]{:S(2)}, u32[]{:S(2)}) collective-permute-start(bf16[2304,128]{1,0:T(8,128)(2,1)S(1)} %assemble.2.h_ref), channel_id=1, source_target_pairs={{0,4},{4,0},{8,12},{12,8},{16,20},{20,16},{24,28},{28,24},{1,5},{5... | collective-permute-start | bytes 1769480 | tf_op jit(solution)/shard_map/ppermute | solution.py:372
  97.9 1.6 collective-permute-done.38.h_ref
  99.5 1.8 head.3
  101.8 2.0 %collective-permute-start.37 = (bf16[576,128]{1,0:T(8,128)(2,1)S(1)}, bf16[576,128]{1,0:T(8,128)(2,1)S(1)}, u32[]{:S(2)}, u32[]{:S(2)}) collective-permute-start(bf16[576,128]{1,0:T(8,128)(2,1)S(1)} %back_out.2.even_ref), channel_id=1, source_target_pairs={{4,0},{8,4},{12,8},{16,12},{20,16},{24,20},{28,24},{5,1},{9,5},{13... | collective-permute-start | bytes 442376 | tf_op jit(solution)/shard_map/ppermute | solution.py:372
  103.8 1.3 collective-permute-start.36
  105.1 1.8 head.2
  109.3 1.2 collective-permute-start.42
  110.5 1.4 collective-permute-done.40.refs_1_
  112.4 1.9 collective-permute-done.42.refs_3_
  117.6 1.3 collective-permute-start.46
  118.8 1.3 collective-permute-start.47
  120.2 1.3 collective-permute-start.48
  121.7 4.7 %collective-permute-done.46.refs_1_ = bf16[592,128]{1,0:T(8,128)(2,1)S(1)} collective-permute-done((bf16[592,128]{1,0:T(8,128)(2,1)S(1)}, bf16[592,128]{1,0:T(8,128)(2,1)S(1)}, u32[]{:S(2)}, u32[]{:S(2)}) %collective-permute-start.46) | collective-permute-done | bytes 151584 | tf_op jit(solution)/shard_map/ppermute | solution.py:372
  126.4 1.3 collective-permute-done.47.refs_2_
  127.6 1.3 collective-permute-done.48.refs_3_
  129.6 1.3 collective-permute-start.52
  130.9 1.3 collective-permute-start.49
  132.2 1.3 collective-permute-start.50
  133.5 1.3 collective-permute-start.51
  134.8 3.8 %collective-permute-done.52.total_ref = bf16[592,128]{1,0:T(8,128)(2,1)S(1)} collective-permute-done((bf16[592,128]{1,0:T(8,128)(2,1)S(1)}, bf16[592,128]{1,0:T(8,128)(2,1)S(1)}, u32[]{:S(2)}, u32[]{:S(2)}) %collective-permute-start.52) | collective-permute-done | bytes 151584 | tf_op jit(solution)/shard_map/ppermute | solution.py:372
  142.9 1.3 collective-permute-start.59
  144.2 1.3 collective-permute-start.60
  145.5 1.3 collective-permute-start.61
  146.9 1.5 back.3
  153.3 2.9 %collective-permute-done.58.refs_3_ = bf16[592,128]{1,0:T(8,128)(2,1)S(1)} collective-permute-done((bf16[592,128]{1,0:T(8,128)(2,1)S(1)}, bf16[592,128]{1,0:T(8,128)(2,1)S(1)}, u32[]{:S(2)}, u32[]{:S(2)}) %collective-permute-start.58) | collective-permute-done | bytes 151584 | tf_op jit(solution)/shard_map/ppermute | solution.py:378
  159.6 1.3 collective-permute-start.66
  160.9 5.3 %collective-permute-start.62 = (bf16[576,128]{1,0:T(8,128)(2,1)S(1)}, bf16[576,128]{1,0:T(8,128)(2,1)S(1)}, u32[]{:S(2)}, u32[]{:S(2)}) collective-permute-start(bf16[576,128]{1,0:T(8,128)(2,1)S(1)} %back_out.3), channel_id=1, source_target_pairs={{4,0},{8,4},{12,8},{16,12},{20,16},{24,20},{28,24},{5,1},{9,5},{13... | collective-permute-start | bytes 442376 | tf_op jit(solution)/shard_map/ppermute | solution.py:372
  166.2 7.4 %collective-permute-done.66 = bf16[576,128]{1,0:T(8,128)(2,1)S(1)} collective-permute-done((bf16[576,128]{1,0:T(8,128)(2,1)S(1)}, bf16[576,128]{1,0:T(8,128)(2,1)S(1)}, u32[]{:S(2)}, u32[]{:S(2)}) %collective-permute-start.66) | collective-permute-done | bytes 147488 | tf_op jit(solution)/shard_map/ppermute | solution.py:372
  176.3 1.6 collective-permute-start.70
  177.9 1.3 enter.3
  179.2 2.8 %collective-permute-done.69.refs_3_ = bf16[576,128]{1,0:T(8,128)(2,1)S(1)} collective-permute-done((bf16[576,128]{1,0:T(8,128)(2,1)S(1)}, bf16[576,128]{1,0:T(8,128)(2,1)S(1)}, u32[]{:S(2)}, u32[]{:S(2)}) %collective-permute-start.69) | collective-permute-done | bytes 147488 | tf_op jit(solution)/shard_map/ppermute | solution.py:378
  182.6 1.7 collective-permute-start.71
  184.3 1.2 last_cots.1
  185.9 3.0 %grad.1 = (bf16[256,2304]{1,0:T(8,128)(2,1)}, f32[8,128]{1,0:T(8,128)S(1)}) custom-call(s32[4]{0:T(128)S(1)} %pad_add_fusion.here, s32[2,128]{1,0:T(2,128)S(1)} %copy-done.10, s32[2,128]{1,0:T(2,128)S(1)} %copy-done.8, f32[8,128]{1,0:T(8,128)S(1)} %add_add_fusion.2.refs_0_, f32[256,128]{1,0:T(8,128)S(1)} %get-tuple-element.247.refs_1_, ...), custom_call_target="tpu_custom_call" | custom-call | flops 603979776 | bytes 3815440 | tf_op jit(solution)/shard_map/grad/pallas_call | solution.py:27
  (143 shorter events, 54.5 us)
Async XLA Ops:
  9.9 25.8 %collective-permute-start.7 = (bf16[2304,256]{1,0:T(8,128)(2,1)S(1)}, bf16[2304,256]{1,0:T(8,128)(2,1)S(1)}, u32[]{:S(2)}, u32[]{:S(2)}) collective-permute-start(bf16[2304,256]{1,0:T(8,128)(2,1)S(1)} %get-tuple-element.141), channel_id=1, source_target_pairs={{0,4},{4,0},{8,12},{12,8},{16,20},{20,16},{24,28},{28,24},{1,5},{5... | collective-permute-start | bytes 3538952 | tf_op jit(solution)/shard_map/ppermute | solution.py:372
  10.7 8.6 %collective-permute-start = (bf16[1152,128]{1,0:T(8,128)(2,1)S(1)}, bf16[1152,128]{1,0:T(8,128)(2,1)S(1)}, u32[]{:S(2)}, u32[]{:S(2)}) collective-permute-start(bf16[1152,128]{1,0:T(8,128)(2,1)S(1)} %get-tuple-element.130), channel_id=1, source_target_pairs={{0,1},{1,0},{2,3},{3,2},{4,5},{5,4},{6,7},{7,6},{8,9},{9,8},{10,11... | collective-permute-start | bytes 884744 | tf_op jit(solution)/shard_map/ppermute | solution.py:378
  11.9 14.6 %collective-permute-start.1 = (bf16[1152,128]{1,0:T(8,128)(2,1)S(1)}, bf16[1152,128]{1,0:T(8,128)(2,1)S(1)}, u32[]{:S(2)}, u32[]{:S(2)}) collective-permute-start(bf16[1152,128]{1,0:T(8,128)(2,1)S(1)} %get-tuple-element.131), channel_id=1, source_target_pairs={{0,2},{1,3},{2,0},{3,1},{4,6},{5,7},{6,4},{7,5},{8,10},{9,11},{10,... | collective-permute-start | bytes 884744 | tf_op jit(solution)/shard_map/ppermute | solution.py:378
  12.1 14.3 %collective-permute-start.2 = (bf16[1152,128]{1,0:T(8,128)(2,1)S(1)}, bf16[1152,128]{1,0:T(8,128)(2,1)S(1)}, u32[]{:S(2)}, u32[]{:S(2)}) collective-permute-start(bf16[1152,128]{1,0:T(8,128)(2,1)S(1)} %get-tuple-element.132), channel_id=1, source_target_pairs={{0,3},{1,2},{2,1},{3,0},{4,7},{5,6},{6,5},{7,4},{8,11},{9,10},{10,... | collective-permute-start | bytes 884744 | tf_op jit(solution)/shard_map/ppermute | solution.py:378
  30.1 4.1 %collective-permute-start.5 = (bf16[256,128]{1,0:T(8,128)(2,1)S(1)}, bf16[256,128]{1,0:T(8,128)(2,1)S(1)}, u32[]{:S(2)}, u32[]{:S(2)}) collective-permute-start(bf16[256,128]{1,0:T(8,128)(2,1)S(1)} %get-tuple-element.137), channel_id=1, source_target_pairs={{0,3},{1,2},{2,1},{3,0},{4,7},{5,6},{6,5},{7,4},{8,11},{9,10},{10,... | collective-permute-start | bytes 196616 | tf_op jit(solution)/shard_map/ppermute | solution.py:378
  36.6 5.0 %collective-permute-start.10 = (bf16[576,128]{1,0:T(8,128)(2,1)S(1)}, bf16[576,128]{1,0:T(8,128)(2,1)S(1)}, u32[]{:S(2)}, u32[]{:S(2)}) collective-permute-start(bf16[576,128]{1,0:T(8,128)(2,1)S(1)} %get-tuple-element.149), channel_id=1, source_target_pairs={{0,3},{1,2},{2,1},{3,0},{4,7},{5,6},{6,5},{7,4},{8,11},{9,10},{10,... | collective-permute-start | bytes 442376 | tf_op jit(solution)/shard_map/ppermute | solution.py:378
  37.8 5.5 %collective-permute-start.8 = (bf16[576,128]{1,0:T(8,128)(2,1)S(1)}, bf16[576,128]{1,0:T(8,128)(2,1)S(1)}, u32[]{:S(2)}, u32[]{:S(2)}) collective-permute-start(bf16[576,128]{1,0:T(8,128)(2,1)S(1)} %get-tuple-element.147), channel_id=1, source_target_pairs={{0,1},{1,0},{2,3},{3,2},{4,5},{5,4},{6,7},{7,6},{8,9},{9,8},{10,11... | collective-permute-start | bytes 442376 | tf_op jit(solution)/shard_map/ppermute | solution.py:378
  38.6 5.1 %collective-permute-start.9 = (bf16[576,128]{1,0:T(8,128)(2,1)S(1)}, bf16[576,128]{1,0:T(8,128)(2,1)S(1)}, u32[]{:S(2)}, u32[]{:S(2)}) collective-permute-start(bf16[576,128]{1,0:T(8,128)(2,1)S(1)} %get-tuple-element.148), channel_id=1, source_target_pairs={{0,2},{1,3},{2,0},{3,1},{4,6},{5,7},{6,4},{7,5},{8,10},{9,11},{10,... | collective-permute-start | bytes 442376 | tf_op jit(solution)/shard_map/ppermute | solution.py:378
  39.3 9.5 %collective-permute-start.6 = (bf16[576,128]{1,0:T(8,128)(2,1)S(1)}, bf16[576,128]{1,0:T(8,128)(2,1)S(1)}, u32[]{:S(2)}, u32[]{:S(2)}) collective-permute-start(bf16[576,128]{1,0:T(8,128)(2,1)S(1)} %get-tuple-element.138.h_ref), channel_id=1, source_target_pairs={{0,4},{4,8},{8,12},{12,16},{16,20},{20,24},{24,28},{1,5},{5,9},{9,... | collective-permute-start | bytes 442376 | tf_op jit(solution)/shard_map/ppermute | solution.py:372
  43.7 7.9 %collective-permute-start.11 = (bf16[576,128]{1,0:T(8,128)(2,1)S(1)}, bf16[576,128]{1,0:T(8,128)(2,1)S(1)}, u32[]{:S(2)}, u32[]{:S(2)}) collective-permute-start(bf16[576,128]{1,0:T(8,128)(2,1)S(1)} %add_convert_fusion.1.refs_0_), channel_id=1, source_target_pairs={{8,0},{4,28},{9,1},{5,29},{10,2},{6,30},{11,3},{7,31}} | collective-permute-start | bytes 442376 | tf_op jit(solution)/shard_map/ppermute | solution.py:372
  45.1 8.0 %collective-permute-start.12 = (bf16[576,128]{1,0:T(8,128)(2,1)S(1)}, bf16[576,128]{1,0:T(8,128)(2,1)S(1)}, u32[]{:S(2)}, u32[]{:S(2)}) collective-permute-start(bf16[576,128]{1,0:T(8,128)(2,1)S(1)} %add_convert_fusion.1.refs_0_), channel_id=1, source_target_pairs={{16,0},{12,28},{17,1},{13,29},{18,2},{14,30},{19,3},{15,31}} | collective-permute-start | bytes 442376 | tf_op jit(solution)/shard_map/ppermute | solution.py:372
  46.4 8.2 %collective-permute-start.13 = (bf16[576,128]{1,0:T(8,128)(2,1)S(1)}, bf16[576,128]{1,0:T(8,128)(2,1)S(1)}, u32[]{:S(2)}, u32[]{:S(2)}) collective-permute-start(bf16[576,128]{1,0:T(8,128)(2,1)S(1)} %add_convert_fusion.1.refs_0_), channel_id=1, source_target_pairs={{24,0},{20,28},{25,1},{21,29},{26,2},{22,30},{27,3},{23,31}} | collective-permute-start | bytes 442376 | tf_op jit(solution)/shard_map/ppermute | solution.py:372
  47.7 9.0 %collective-permute-start.18 = (bf16[576,128]{1,0:T(8,128)(2,1)S(1)}, bf16[576,128]{1,0:T(8,128)(2,1)S(1)}, u32[]{:S(2)}, u32[]{:S(2)}) collective-permute-start(bf16[576,128]{1,0:T(8,128)(2,1)S(1)} %get-tuple-element.154.refs_0_.refs_6_.refs_7_), channel_id=1, source_target_pairs={{0,1},{1,0},{2,3},{3,2},{4,5},{5,4},{6,7},{7,6},{8,9},{9,8},{10,11... | collective-permute-start | bytes 442376 | tf_op jit(solution)/shard_map/ppermute | solution.py:378
  48.8 9.1 %collective-permute-start.19 = (bf16[576,128]{1,0:T(8,128)(2,1)S(1)}, bf16[576,128]{1,0:T(8,128)(2,1)S(1)}, u32[]{:S(2)}, u32[]{:S(2)}) collective-permute-start(bf16[576,128]{1,0:T(8,128)(2,1)S(1)} %get-tuple-element.154.refs_0_.refs_6_.refs_7_), channel_id=1, source_target_pairs={{0,2},{1,3},{2,0},{3,1},{4,6},{5,7},{6,4},{7,5},{8,10},{9,11},{10,... | collective-permute-start | bytes 442376 | tf_op jit(solution)/shard_map/ppermute | solution.py:378
  51.6 10.5 %collective-permute-start.20 = (bf16[576,128]{1,0:T(8,128)(2,1)S(1)}, bf16[576,128]{1,0:T(8,128)(2,1)S(1)}, u32[]{:S(2)}, u32[]{:S(2)}) collective-permute-start(bf16[576,128]{1,0:T(8,128)(2,1)S(1)} %get-tuple-element.154.refs_0_.refs_6_.refs_7_), channel_id=1, source_target_pairs={{0,3},{1,2},{2,1},{3,0},{4,7},{5,6},{6,5},{7,4},{8,11},{9,10},{10,... | collective-permute-start | bytes 442376 | tf_op jit(solution)/shard_map/ppermute | solution.py:378
  55.2 10.0 %collective-permute-start.15 = (bf16[576,128]{1,0:T(8,128)(2,1)S(1)}, bf16[576,128]{1,0:T(8,128)(2,1)S(1)}, u32[]{:S(2)}, u32[]{:S(2)}) collective-permute-start(bf16[576,128]{1,0:T(8,128)(2,1)S(1)} %enter.2.refs_0_.x_ref), channel_id=1, source_target_pairs={{0,1},{1,0},{2,3},{3,2},{4,5},{5,4},{6,7},{7,6},{8,9},{9,8},{10,11... | collective-permute-start | bytes 442376 | tf_op jit(solution)/shard_map/ppermute | solution.py:378
  56.7 8.5 %collective-permute-start.16 = (bf16[576,128]{1,0:T(8,128)(2,1)S(1)}, bf16[576,128]{1,0:T(8,128)(2,1)S(1)}, u32[]{:S(2)}, u32[]{:S(2)}) collective-permute-start(bf16[576,128]{1,0:T(8,128)(2,1)S(1)} %enter.2.refs_0_.x_ref), channel_id=1, source_target_pairs={{0,2},{1,3},{2,0},{3,1},{4,6},{5,7},{6,4},{7,5},{8,10},{9,11},{10,... | collective-permute-start | bytes 442376 | tf_op jit(solution)/shard_map/ppermute | solution.py:378
  56.7 8.5 %collective-permute-start.17 = (bf16[576,128]{1,0:T(8,128)(2,1)S(1)}, bf16[576,128]{1,0:T(8,128)(2,1)S(1)}, u32[]{:S(2)}, u32[]{:S(2)}) collective-permute-start(bf16[576,128]{1,0:T(8,128)(2,1)S(1)} %enter.2.refs_0_.x_ref), channel_id=1, source_target_pairs={{0,3},{1,2},{2,1},{3,0},{4,7},{5,6},{6,5},{7,4},{8,11},{9,10},{10,... | collective-permute-start | bytes 442376 | tf_op jit(solution)/shard_map/ppermute | solution.py:378
  58.0 12.3 %collective-permute-start.14 = (bf16[576,128]{1,0:T(8,128)(2,1)S(1)}, bf16[576,128]{1,0:T(8,128)(2,1)S(1)}, u32[]{:S(2)}, u32[]{:S(2)}) collective-permute-start(bf16[576,128]{1,0:T(8,128)(2,1)S(1)} %get-tuple-element.138.h_ref), channel_id=1, source_target_pairs={{28,24},{29,25},{30,26},{31,27}} | collective-permute-start | bytes 442376 | tf_op jit(solution)/shard_map/ppermute | solution.py:372
  67.1 9.7 %collective-permute-start.27 = (bf16[576,128]{1,0:T(8,128)(2,1)S(1)}, bf16[576,128]{1,0:T(8,128)(2,1)S(1)}, u32[]{:S(2)}, u32[]{:S(2)}) collective-permute-start(bf16[576,128]{1,0:T(8,128)(2,1)S(1)} %get-tuple-element.167.refs_0_.refs_6_), channel_id=1, source_target_pairs={{0,1},{1,0},{2,3},{3,2},{4,5},{5,4},{6,7},{7,6},{8,9},{9,8},{10,11... | collective-permute-start | bytes 442376 | tf_op jit(solution)/shard_map/ppermute | solution.py:378
  68.6 4.7 %collective-permute-start.22 = (bf16[128,128]{1,0:T(8,128)(2,1)S(1)}, bf16[128,128]{1,0:T(8,128)(2,1)S(1)}, u32[]{:S(2)}, u32[]{:S(2)}) collective-permute-start(bf16[128,128]{1,0:T(8,128)(2,1)S(1)} %forward.3.refs_0_), channel_id=1, source_target_pairs={{0,2},{1,3},{2,0},{3,1},{4,6},{5,7},{6,4},{7,5},{8,10},{9,11},{10,... | collective-permute-start | bytes 98312 | tf_op jit(solution)/shard_map/ppermute | solution.py:378
  68.9 4.4 %collective-permute-start.23 = (bf16[128,128]{1,0:T(8,128)(2,1)S(1)}, bf16[128,128]{1,0:T(8,128)(2,1)S(1)}, u32[]{:S(2)}, u32[]{:S(2)}) collective-permute-start(bf16[128,128]{1,0:T(8,128)(2,1)S(1)} %forward.3.refs_0_), channel_id=1, source_target_pairs={{0,3},{1,2},{2,1},{3,0},{4,7},{5,6},{6,5},{7,4},{8,11},{9,10},{10,... | collective-permute-start | bytes 98312 | tf_op jit(solution)/shard_map/ppermute | solution.py:378
  70.3 8.0 %collective-permute-start.28 = (bf16[576,128]{1,0:T(8,128)(2,1)S(1)}, bf16[576,128]{1,0:T(8,128)(2,1)S(1)}, u32[]{:S(2)}, u32[]{:S(2)}) collective-permute-start(bf16[576,128]{1,0:T(8,128)(2,1)S(1)} %get-tuple-element.167.refs_0_.refs_6_), channel_id=1, source_target_pairs={{0,2},{1,3},{2,0},{3,1},{4,6},{5,7},{6,4},{7,5},{8,10},{9,11},{10,... | collective-permute-start | bytes 442376 | tf_op jit(solution)/shard_map/ppermute | solution.py:378
  71.5 7.8 %collective-permute-start.29 = (bf16[576,128]{1,0:T(8,128)(2,1)S(1)}, bf16[576,128]{1,0:T(8,128)(2,1)S(1)}, u32[]{:S(2)}, u32[]{:S(2)}) collective-permute-start(bf16[576,128]{1,0:T(8,128)(2,1)S(1)} %get-tuple-element.167.refs_0_.refs_6_), channel_id=1, source_target_pairs={{0,3},{1,2},{2,1},{3,0},{4,7},{5,6},{6,5},{7,4},{8,11},{9,10},{10,... | collective-permute-start | bytes 442376 | tf_op jit(solution)/shard_map/ppermute | solution.py:378
  74.2 7.2 %collective-permute-start.24 = (bf16[576,128]{1,0:T(8,128)(2,1)S(1)}, bf16[576,128]{1,0:T(8,128)(2,1)S(1)}, u32[]{:S(2)}, u32[]{:S(2)}) collective-permute-start(bf16[576,128]{1,0:T(8,128)(2,1)S(1)} %get-tuple-element.166), channel_id=1, source_target_pairs={{28,4},{24,0},{29,5},{25,1},{30,6},{26,2},{31,7},{27,3}} | collective-permute-start | bytes 442376 | tf_op jit(solution)/shard_map/ppermute | solution.py:372
  75.5 7.4 %collective-permute-start.25 = (bf16[576,128]{1,0:T(8,128)(2,1)S(1)}, bf16[576,128]{1,0:T(8,128)(2,1)S(1)}, u32[]{:S(2)}, u32[]{:S(2)}) collective-permute-start(bf16[576,128]{1,0:T(8,128)(2,1)S(1)} %get-tuple-element.166), channel_id=1, source_target_pairs={{28,12},{24,8},{29,13},{25,9},{30,14},{26,10},{31,15},{27,11}} | collective-permute-start | bytes 442376 | tf_op jit(solution)/shard_map/ppermute | solution.py:372
  76.8 6.1 %collective-permute-start.26 = (bf16[576,128]{1,0:T(8,128)(2,1)S(1)}, bf16[576,128]{1,0:T(8,128)(2,1)S(1)}, u32[]{:S(2)}, u32[]{:S(2)}) collective-permute-start(bf16[576,128]{1,0:T(8,128)(2,1)S(1)} %get-tuple-element.166), channel_id=1, source_target_pairs={{28,20},{24,16},{29,21},{25,17},{30,22},{26,18},{31,23},{27,19}} | collective-permute-start | bytes 442376 | tf_op jit(solution)/shard_map/ppermute | solution.py:372
  78.3 5.9 %collective-permute-start.33 = (bf16[592,128]{1,0:T(8,128)(2,1)S(1)}, bf16[592,128]{1,0:T(8,128)(2,1)S(1)}, u32[]{:S(2)}, u32[]{:S(2)}) collective-permute-start(bf16[592,128]{1,0:T(8,128)(2,1)S(1)} %get-tuple-element.174), channel_id=1, source_target_pairs={{0,1},{1,0},{2,3},{3,2},{4,5},{5,4},{6,7},{7,6},{8,9},{9,8},{10,11... | collective-permute-start | bytes 454664 | tf_op jit(solution)/shard_map/ppermute | solution.py:378
  79.4 6.3 %collective-permute-start.34 = (bf16[592,128]{1,0:T(8,128)(2,1)S(1)}, bf16[592,128]{1,0:T(8,128)(2,1)S(1)}, u32[]{:S(2)}, u32[]{:S(2)}) collective-permute-start(bf16[592,128]{1,0:T(8,128)(2,1)S(1)} %get-tuple-element.175), channel_id=1, source_target_pairs={{0,2},{1,3},{2,0},{3,1},{4,6},{5,7},{6,4},{7,5},{8,10},{9,11},{10,... | collective-permute-start | bytes 454664 | tf_op jit(solution)/shard_map/ppermute | solution.py:378
  81.4 5.0 %collective-permute-start.35 = (bf16[592,128]{1,0:T(8,128)(2,1)S(1)}, bf16[592,128]{1,0:T(8,128)(2,1)S(1)}, u32[]{:S(2)}, u32[]{:S(2)}) collective-permute-start(bf16[592,128]{1,0:T(8,128)(2,1)S(1)} %get-tuple-element.176), channel_id=1, source_target_pairs={{0,3},{1,2},{2,1},{3,0},{4,7},{5,6},{6,5},{7,4},{8,11},{9,10},{10,... | collective-permute-start | bytes 454664 | tf_op jit(solution)/shard_map/ppermute | solution.py:378
  82.9 6.9 %collective-permute-start.30 = (bf16[576,128]{1,0:T(8,128)(2,1)S(1)}, bf16[576,128]{1,0:T(8,128)(2,1)S(1)}, u32[]{:S(2)}, u32[]{:S(2)}) collective-permute-start(bf16[576,128]{1,0:T(8,128)(2,1)S(1)} %add_add_fusion.1.refs_0_), channel_id=1, source_target_pairs={{0,1},{1,0},{2,3},{3,2},{4,5},{5,4},{6,7},{7,6},{8,9},{9,8},{10,11... | collective-permute-start | bytes 442376 | tf_op jit(solution)/shard_map/ppermute | solution.py:378
  84.0 5.8 %collective-permute-start.31 = (bf16[576,128]{1,0:T(8,128)(2,1)S(1)}, bf16[576,128]{1,0:T(8,128)(2,1)S(1)}, u32[]{:S(2)}, u32[]{:S(2)}) collective-permute-start(bf16[576,128]{1,0:T(8,128)(2,1)S(1)} %add_add_fusion.1.refs_0_), channel_id=1, source_target_pairs={{0,2},{1,3},{2,0},{3,1},{4,6},{5,7},{6,4},{7,5},{8,10},{9,11},{10,... | collective-permute-start | bytes 442376 | tf_op jit(solution)/shard_map/ppermute | solution.py:378
  84.2 7.0 %collective-permute-start.32 = (bf16[576,128]{1,0:T(8,128)(2,1)S(1)}, bf16[576,128]{1,0:T(8,128)(2,1)S(1)}, u32[]{:S(2)}, u32[]{:S(2)}) collective-permute-start(bf16[576,128]{1,0:T(8,128)(2,1)S(1)} %add_add_fusion.1.refs_0_), channel_id=1, source_target_pairs={{0,3},{1,2},{2,1},{3,0},{4,7},{5,6},{6,5},{7,4},{8,11},{9,10},{10,... | collective-permute-start | bytes 442376 | tf_op jit(solution)/shard_map/ppermute | solution.py:378
  91.8 7.7 %collective-permute-start.38 = (bf16[2304,128]{1,0:T(8,128)(2,1)S(1)}, bf16[2304,128]{1,0:T(8,128)(2,1)S(1)}, u32[]{:S(2)}, u32[]{:S(2)}) collective-permute-start(bf16[2304,128]{1,0:T(8,128)(2,1)S(1)} %assemble.2.h_ref), channel_id=1, source_target_pairs={{0,4},{4,0},{8,12},{12,8},{16,20},{20,16},{24,28},{28,24},{1,5},{5... | collective-permute-start | bytes 1769480 | tf_op jit(solution)/shard_map/ppermute | solution.py:372
  101.3 5.8 %collective-permute-start.39 = (bf16[2368,128]{1,0:T(8,128)(2,1)S(1)}, bf16[2368,128]{1,0:T(8,128)(2,1)S(1)}, u32[]{:S(2)}, u32[]{:S(2)}) collective-permute-start(bf16[2368,128]{1,0:T(8,128)(2,1)S(1)} %get-tuple-element.191), channel_id=1, source_target_pairs={{0,4},{4,0},{8,12},{12,8},{16,20},{20,16},{24,28},{28,24},{1,5},{5... | collective-permute-start | bytes 1818632 | tf_op jit(solution)/shard_map/ppermute | solution.py:372
  101.8 5.2 %collective-permute-start.37 = (bf16[576,128]{1,0:T(8,128)(2,1)S(1)}, bf16[576,128]{1,0:T(8,128)(2,1)S(1)}, u32[]{:S(2)}, u32[]{:S(2)}) collective-permute-start(bf16[576,128]{1,0:T(8,128)(2,1)S(1)} %back_out.2.even_ref), channel_id=1, source_target_pairs={{4,0},{8,4},{12,8},{16,12},{20,16},{24,20},{28,24},{5,1},{9,5},{13... | collective-permute-start | bytes 442376 | tf_op jit(solution)/shard_map/ppermute | solution.py:372
  107.8 4.1 %collective-permute-start.40 = (bf16[592,128]{1,0:T(8,128)(2,1)S(1)}, bf16[592,128]{1,0:T(8,128)(2,1)S(1)}, u32[]{:S(2)}, u32[]{:S(2)}) collective-permute-start(bf16[592,128]{1,0:T(8,128)(2,1)S(1)} %get-tuple-element.193), channel_id=1, source_target_pairs={{0,1},{1,0},{2,3},{3,2},{4,5},{5,4},{6,7},{7,6},{8,9},{9,8},{10,11... | collective-permute-start | bytes 454664 | tf_op jit(solution)/shard_map/ppermute | solution.py:378
  108.3 4.0 %collective-permute-start.41 = (bf16[592,128]{1,0:T(8,128)(2,1)S(1)}, bf16[592,128]{1,0:T(8,128)(2,1)S(1)}, u32[]{:S(2)}, u32[]{:S(2)}) collective-permute-start(bf16[592,128]{1,0:T(8,128)(2,1)S(1)} %get-tuple-element.194), channel_id=1, source_target_pairs={{0,2},{1,3},{2,0},{3,1},{4,6},{5,7},{6,4},{7,5},{8,10},{9,11},{10,... | collective-permute-start | bytes 454664 | tf_op jit(solution)/shard_map/ppermute | solution.py:378
  109.3 4.9 %collective-permute-start.42 = (bf16[592,128]{1,0:T(8,128)(2,1)S(1)}, bf16[592,128]{1,0:T(8,128)(2,1)S(1)}, u32[]{:S(2)}, u32[]{:S(2)}) collective-permute-start(bf16[592,128]{1,0:T(8,128)(2,1)S(1)} %get-tuple-element.195), channel_id=1, source_target_pairs={{0,3},{1,2},{2,1},{3,0},{4,7},{5,6},{6,5},{7,4},{8,11},{9,10},{10,... | collective-permute-start | bytes 454664 | tf_op jit(solution)/shard_map/ppermute | solution.py:378
  114.8 5.3 %collective-permute-start.43 = (bf16[576,128]{1,0:T(8,128)(2,1)S(1)}, bf16[576,128]{1,0:T(8,128)(2,1)S(1)}, u32[]{:S(2)}, u32[]{:S(2)}) collective-permute-start(bf16[576,128]{1,0:T(8,128)(2,1)S(1)} %get-tuple-element.197), channel_id=1, source_target_pairs={{0,1},{1,0},{2,3},{3,2},{4,5},{5,4},{6,7},{7,6},{8,9},{9,8},{10,11... | collective-permute-start | bytes 442376 | tf_op jit(solution)/shard_map/ppermute | solution.py:378
  115.7 5.8 %collective-permute-start.44 = (bf16[576,128]{1,0:T(8,128)(2,1)S(1)}, bf16[576,128]{1,0:T(8,128)(2,1)S(1)}, u32[]{:S(2)}, u32[]{:S(2)}) collective-permute-start(bf16[576,128]{1,0:T(8,128)(2,1)S(1)} %get-tuple-element.198), channel_id=1, source_target_pairs={{0,2},{1,3},{2,0},{3,1},{4,6},{5,7},{6,4},{7,5},{8,10},{9,11},{10,... | collective-permute-start | bytes 442376 | tf_op jit(solution)/shard_map/ppermute | solution.py:378
  116.5 5.1 %collective-permute-start.45 = (bf16[576,128]{1,0:T(8,128)(2,1)S(1)}, bf16[576,128]{1,0:T(8,128)(2,1)S(1)}, u32[]{:S(2)}, u32[]{:S(2)}) collective-permute-start(bf16[576,128]{1,0:T(8,128)(2,1)S(1)} %get-tuple-element.199), channel_id=1, source_target_pairs={{0,3},{1,2},{2,1},{3,0},{4,7},{5,6},{6,5},{7,4},{8,11},{9,10},{10,... | collective-permute-start | bytes 442376 | tf_op jit(solution)/shard_map/ppermute | solution.py:378
  117.6 8.8 %collective-permute-start.46 = (bf16[592,128]{1,0:T(8,128)(2,1)S(1)}, bf16[592,128]{1,0:T(8,128)(2,1)S(1)}, u32[]{:S(2)}, u32[]{:S(2)}) collective-permute-start(bf16[592,128]{1,0:T(8,128)(2,1)S(1)} %sum.1.refs_0_), channel_id=1, source_target_pairs={{0,24},{4,28},{1,25},{5,29},{2,26},{6,30},{3,27},{7,31}} | collective-permute-start | bytes 454664 | tf_op jit(solution)/shard_map/ppermute | solution.py:372
  118.8 8.8 %collective-permute-start.47 = (bf16[592,128]{1,0:T(8,128)(2,1)S(1)}, bf16[592,128]{1,0:T(8,128)(2,1)S(1)}, u32[]{:S(2)}, u32[]{:S(2)}) collective-permute-start(bf16[592,128]{1,0:T(8,128)(2,1)S(1)} %sum.1.refs_0_), channel_id=1, source_target_pairs={{8,24},{12,28},{9,25},{13,29},{10,26},{14,30},{11,27},{15,31}} | collective-permute-start | bytes 454664 | tf_op jit(solution)/shard_map/ppermute | solution.py:372
  120.2 8.8 %collective-permute-start.48 = (bf16[592,128]{1,0:T(8,128)(2,1)S(1)}, bf16[592,128]{1,0:T(8,128)(2,1)S(1)}, u32[]{:S(2)}, u32[]{:S(2)}) collective-permute-start(bf16[592,128]{1,0:T(8,128)(2,1)S(1)} %sum.1.refs_0_), channel_id=1, source_target_pairs={{16,24},{20,28},{17,25},{21,29},{18,26},{22,30},{19,27},{23,31}} | collective-permute-start | bytes 454664 | tf_op jit(solution)/shard_map/ppermute | solution.py:372
  129.6 9.0 %collective-permute-start.52 = (bf16[592,128]{1,0:T(8,128)(2,1)S(1)}, bf16[592,128]{1,0:T(8,128)(2,1)S(1)}, u32[]{:S(2)}, u32[]{:S(2)}) collective-permute-start(bf16[592,128]{1,0:T(8,128)(2,1)S(1)} %get-tuple-element.226.total_ref), channel_id=1, source_target_pairs={{24,28},{25,29},{26,30},{27,31}} | collective-permute-start | bytes 454664 | tf_op jit(solution)/shard_map/ppermute | solution.py:372
  130.9 11.3 %collective-permute-start.49 = (bf16[576,128]{1,0:T(8,128)(2,1)S(1)}, bf16[576,128]{1,0:T(8,128)(2,1)S(1)}, u32[]{:S(2)}, u32[]{:S(2)}) collective-permute-start(bf16[576,128]{1,0:T(8,128)(2,1)S(1)} %add_convert_fusion.refs_0_), channel_id=1, source_target_pairs={{8,0},{4,28},{9,1},{5,29},{10,2},{6,30},{11,3},{7,31}} | collective-permute-start | bytes 442376 | tf_op jit(solution)/shard_map/ppermute | solution.py:372
  132.2 10.8 %collective-permute-start.50 = (bf16[576,128]{1,0:T(8,128)(2,1)S(1)}, bf16[576,128]{1,0:T(8,128)(2,1)S(1)}, u32[]{:S(2)}, u32[]{:S(2)}) collective-permute-start(bf16[576,128]{1,0:T(8,128)(2,1)S(1)} %add_convert_fusion.refs_0_), channel_id=1, source_target_pairs={{16,0},{12,28},{17,1},{13,29},{18,2},{14,30},{19,3},{15,31}} | collective-permute-start | bytes 442376 | tf_op jit(solution)/shard_map/ppermute | solution.py:372
  133.5 10.8 %collective-permute-start.51 = (bf16[576,128]{1,0:T(8,128)(2,1)S(1)}, bf16[576,128]{1,0:T(8,128)(2,1)S(1)}, u32[]{:S(2)}, u32[]{:S(2)}) collective-permute-start(bf16[576,128]{1,0:T(8,128)(2,1)S(1)} %add_convert_fusion.refs_0_), channel_id=1, source_target_pairs={{24,0},{20,28},{25,1},{21,29},{26,2},{22,30},{27,3},{23,31}} | collective-permute-start | bytes 442376 | tf_op jit(solution)/shard_map/ppermute | solution.py:372
  140.2 5.3 %collective-permute-start.53 = (bf16[128,128]{1,0:T(8,128)(2,1)S(1)}, bf16[128,128]{1,0:T(8,128)(2,1)S(1)}, u32[]{:S(2)}, u32[]{:S(2)}) collective-permute-start(bf16[128,128]{1,0:T(8,128)(2,1)S(1)} %get-tuple-element.212), channel_id=1, source_target_pairs={{0,1},{1,0},{2,3},{3,2},{4,5},{5,4},{6,7},{7,6},{8,9},{9,8},{10,11... | collective-permute-start | bytes 98312 | tf_op jit(solution)/shard_map/ppermute | solution.py:378
  141.1 5.7 %collective-permute-start.54 = (bf16[128,128]{1,0:T(8,128)(2,1)S(1)}, bf16[128,128]{1,0:T(8,128)(2,1)S(1)}, u32[]{:S(2)}, u32[]{:S(2)}) collective-permute-start(bf16[128,128]{1,0:T(8,128)(2,1)S(1)} %get-tuple-element.213), channel_id=1, source_target_pairs={{0,2},{1,3},{2,0},{3,1},{4,6},{5,7},{6,4},{7,5},{8,10},{9,11},{10,... | collective-permute-start | bytes 98312 | tf_op jit(solution)/shard_map/ppermute | solution.py:378
  142.1 4.7 %collective-permute-start.55 = (bf16[128,128]{1,0:T(8,128)(2,1)S(1)}, bf16[128,128]{1,0:T(8,128)(2,1)S(1)}, u32[]{:S(2)}, u32[]{:S(2)}) collective-permute-start(bf16[128,128]{1,0:T(8,128)(2,1)S(1)} %get-tuple-element.214), channel_id=1, source_target_pairs={{0,3},{1,2},{2,1},{3,0},{4,7},{5,6},{6,5},{7,4},{8,11},{9,10},{10,... | collective-permute-start | bytes 98312 | tf_op jit(solution)/shard_map/ppermute | solution.py:378
  142.9 7.3 %collective-permute-start.59 = (f32[8,128]{1,0:T(8,128)S(1)}, f32[8,128]{1,0:T(8,128)S(1)}, u32[]{:S(2)}, u32[]{:S(2)}) collective-permute-start(f32[8,128]{1,0:T(8,128)S(1)} %get-tuple-element.229), channel_id=1, source_target_pairs={{28,4},{24,0},{29,5},{25,1},{30,6},{26,2},{31,7},{27,3}} | collective-permute-start | bytes 12296 | tf_op jit(solution)/shard_map/ppermute | solution.py:372
  144.2 6.8 %collective-permute-start.60 = (f32[8,128]{1,0:T(8,128)S(1)}, f32[8,128]{1,0:T(8,128)S(1)}, u32[]{:S(2)}, u32[]{:S(2)}) collective-permute-start(f32[8,128]{1,0:T(8,128)S(1)} %get-tuple-element.229), channel_id=1, source_target_pairs={{28,12},{24,8},{29,13},{25,9},{30,14},{26,10},{31,15},{27,11}} | collective-permute-start | bytes 12296 | tf_op jit(solution)/shard_map/ppermute | solution.py:372
  145.5 5.5 %collective-permute-start.61 = (f32[8,128]{1,0:T(8,128)S(1)}, f32[8,128]{1,0:T(8,128)S(1)}, u32[]{:S(2)}, u32[]{:S(2)}) collective-permute-start(f32[8,128]{1,0:T(8,128)S(1)} %get-tuple-element.229), channel_id=1, source_target_pairs={{28,20},{24,16},{29,21},{25,17},{30,22},{26,18},{31,23},{27,19}} | collective-permute-start | bytes 12296 | tf_op jit(solution)/shard_map/ppermute | solution.py:372
  148.3 4.1 %collective-permute-start.56 = (bf16[592,128]{1,0:T(8,128)(2,1)S(1)}, bf16[592,128]{1,0:T(8,128)(2,1)S(1)}, u32[]{:S(2)}, u32[]{:S(2)}) collective-permute-start(bf16[592,128]{1,0:T(8,128)(2,1)S(1)} %get-tuple-element.223), channel_id=1, source_target_pairs={{0,1},{1,0},{2,3},{3,2},{4,5},{5,4},{6,7},{7,6},{8,9},{9,8},{10,11... | collective-permute-start | bytes 454664 | tf_op jit(solution)/shard_map/ppermute | solution.py:378
  150.3 6.0 %collective-permute-start.58 = (bf16[592,128]{1,0:T(8,128)(2,1)S(1)}, bf16[592,128]{1,0:T(8,128)(2,1)S(1)}, u32[]{:S(2)}, u32[]{:S(2)}) collective-permute-start(bf16[592,128]{1,0:T(8,128)(2,1)S(1)} %get-tuple-element.225), channel_id=1, source_target_pairs={{0,3},{1,2},{2,1},{3,0},{4,7},{5,6},{6,5},{7,4},{8,11},{9,10},{10,... | collective-permute-start | bytes 454664 | tf_op jit(solution)/shard_map/ppermute | solution.py:378
  158.2 7.9 %collective-permute-start.64 = (bf16[576,128]{1,0:T(8,128)(2,1)S(1)}, bf16[576,128]{1,0:T(8,128)(2,1)S(1)}, u32[]{:S(2)}, u32[]{:S(2)}) collective-permute-start(bf16[576,128]{1,0:T(8,128)(2,1)S(1)} %get-tuple-element.240), channel_id=1, source_target_pairs={{0,8},{4,12},{1,9},{5,13},{2,10},{6,14},{3,11},{7,15}} | collective-permute-start | bytes 442376 | tf_op jit(solution)/shard_map/ppermute | solution.py:372
  158.9 7.3 %collective-permute-start.65 = (bf16[576,128]{1,0:T(8,128)(2,1)S(1)}, bf16[576,128]{1,0:T(8,128)(2,1)S(1)}, u32[]{:S(2)}, u32[]{:S(2)}) collective-permute-start(bf16[576,128]{1,0:T(8,128)(2,1)S(1)} %get-tuple-element.240), channel_id=1, source_target_pairs={{0,16},{4,20},{1,17},{5,21},{2,18},{6,22},{3,19},{7,23}} | collective-permute-start | bytes 442376 | tf_op jit(solution)/shard_map/ppermute | solution.py:372
  159.6 14.0 %collective-permute-start.66 = (bf16[576,128]{1,0:T(8,128)(2,1)S(1)}, bf16[576,128]{1,0:T(8,128)(2,1)S(1)}, u32[]{:S(2)}, u32[]{:S(2)}) collective-permute-start(bf16[576,128]{1,0:T(8,128)(2,1)S(1)} %get-tuple-element.240), channel_id=1, source_target_pairs={{0,24},{4,28},{1,25},{5,29},{2,26},{6,30},{3,27},{7,31}} | collective-permute-start | bytes 442376 | tf_op jit(solution)/shard_map/ppermute | solution.py:372
  160.9 18.3 %collective-permute-start.62 = (bf16[576,128]{1,0:T(8,128)(2,1)S(1)}, bf16[576,128]{1,0:T(8,128)(2,1)S(1)}, u32[]{:S(2)}, u32[]{:S(2)}) collective-permute-start(bf16[576,128]{1,0:T(8,128)(2,1)S(1)} %back_out.3), channel_id=1, source_target_pairs={{4,0},{8,4},{12,8},{16,12},{20,16},{24,20},{28,24},{5,1},{9,5},{13... | collective-permute-start | bytes 442376 | tf_op jit(solution)/shard_map/ppermute | solution.py:372
  173.6 5.6 %collective-permute-start.67 = (bf16[576,128]{1,0:T(8,128)(2,1)S(1)}, bf16[576,128]{1,0:T(8,128)(2,1)S(1)}, u32[]{:S(2)}, u32[]{:S(2)}) collective-permute-start(bf16[576,128]{1,0:T(8,128)(2,1)S(1)} %add_add_fusion.refs_0_), channel_id=1, source_target_pairs={{0,1},{1,0},{2,3},{3,2},{4,5},{5,4},{6,7},{7,6},{8,9},{9,8},{10,11... | collective-permute-start | bytes 442376 | tf_op jit(solution)/shard_map/ppermute | solution.py:378
  174.2 5.0 %collective-permute-start.68 = (bf16[576,128]{1,0:T(8,128)(2,1)S(1)}, bf16[576,128]{1,0:T(8,128)(2,1)S(1)}, u32[]{:S(2)}, u32[]{:S(2)}) collective-permute-start(bf16[576,128]{1,0:T(8,128)(2,1)S(1)} %add_add_fusion.refs_0_), channel_id=1, source_target_pairs={{0,2},{1,3},{2,0},{3,1},{4,6},{5,7},{6,4},{7,5},{8,10},{9,11},{10,... | collective-permute-start | bytes 442376 | tf_op jit(solution)/shard_map/ppermute | solution.py:378
  175.2 6.8 %collective-permute-start.69 = (bf16[576,128]{1,0:T(8,128)(2,1)S(1)}, bf16[576,128]{1,0:T(8,128)(2,1)S(1)}, u32[]{:S(2)}, u32[]{:S(2)}) collective-permute-start(bf16[576,128]{1,0:T(8,128)(2,1)S(1)} %add_add_fusion.refs_0_), channel_id=1, source_target_pairs={{0,3},{1,2},{2,1},{3,0},{4,7},{5,6},{6,5},{7,4},{8,11},{9,10},{10,... | collective-permute-start | bytes 442376 | tf_op jit(solution)/shard_map/ppermute | solution.py:378
  (21 other events, 125.1 us)
